TPU v7x, 32 devices: a whole 2x2x4 slice. The times are simulated.
32 devices in a mesh: cuts: 4 (over y, core), sub: 8 (over z, x).
Axes of the slice: x: 2, y: 2, z: 4, core: 2. Of those that a mesh axis runs over, the one named last changes fastest.
Arguments:
- start_states: float32 [4, 16, 512, 128], P('cuts', 'sub'), may hold values from -8 to 8
- source: bfloat16 [16, 512, 128], P('sub'), may hold values from -3 to 3
- block_inverse: bfloat16 [16, 512, 512], P('sub'), may hold values from -1 to 1
- face_map: int32 [16, 2, 128], P('sub'), may hold values from 0 to 127, each once within a row
- transmissibility: float32 [16, 2, 128], P('sub'), may hold values from 7 to 11
- partner: int32 [16], replicated, may hold values from 0 to 15
- fracture_cond: float32 [16], replicated, may hold values from 0.3 to 3
Outputs:
- new_starts: float32 [4, 16, 512, 128], P('cuts', 'sub')
All inputs are finite; a program needn't handle non-finite values.
Results may differ from a plain program's by a relative error of at most 0.0024.
Values sent between devices are 32-bit elements; how exact they have to be, the bound alone decides.
No kernel may reach another device: no remote copies, remote signals or barrier semaphores. Data moves between devices by JAX's collectives and lax.ppermute only.
A program may use at most 64 MiB of HBM per device.

v0:
```python
import functools

import jax
import jax.numpy as jnp
from jax import lax
from jax.experimental import pallas as pl
from jax.experimental.pallas import tpu as pltpu
from jax.sharding import PartitionSpec as P

FINE_STEPS = 4
SWEEPS = 4
F32 = jnp.float32
BF16 = jnp.bfloat16
HIGH = lax.Precision.HIGHEST


def dot(a, b, dims=((1,), (0,)), precision=None):
    return lax.dot_general(a, b, (dims, ((), ())), precision=precision, preferred_element_type=F32)


def transpose(x):
    return jnp.transpose(x, (1, 0))


def iota(shape, axis):
    return lax.broadcasted_iota(jnp.int32, shape, axis)


def call(body, out_shape, args, flops=1 << 28):
    size = sum(a.size * a.dtype.itemsize for a in list(args) + list(out_shape))
    vmem = pl.BlockSpec(memory_space=pltpu.VMEM)
    return pl.pallas_call(
        body,
        out_shape=out_shape,
        in_specs=[vmem] * len(args),
        out_specs=[vmem] * len(out_shape),
        compiler_params=pltpu.CompilerParams(vmem_limit_bytes=24 << 20),
        cost_estimate=pl.CostEstimate(flops=flops, bytes_accessed=size, transcendentals=0),
    )(*args)


def face_vector(i, count, rhs_ref, link_ref, low, up, below, above):
    face = low[0].shape[0]
    under = below if i == 0 else up[i - 1]
    over = above if i == count - 1 else low[i + 1]
    v_low = rhs_ref[i, :face] + link_ref[2 * i] * under
    v_up = rhs_ref[i, face : 2 * face] + link_ref[2 * i + 1] * over
    return v_low.astype(BF16), v_up.astype(BF16)


def face_sweep(count, ff_ref, y_ref, rhs_ref, link_ref, low, up, below, above):
    face = low[0].shape[0]
    vectors, new_low, new_up = [], [], []
    for i in range(count):
        v = jnp.concatenate(face_vector(i, count, rhs_ref, link_ref, low, up, below, above), axis=0)
        x = y_ref[i] + dot(ff_ref[i], v)
        vectors.append(v)
        new_low.append(x[:face])
        new_up.append(x[face:])
    return vectors, new_low, new_up


def outgoing(count, ff_ref, y_ref, rhs_ref, link_ref, low, up):
    face = low[0].shape[0]
    last = count - 1
    zero = jnp.zeros_like(low[0])
    v = jnp.concatenate(face_vector(last, count, rhs_ref, link_ref, low, up, zero, zero), axis=0)
    next_up = y_ref[last, face:] + dot(ff_ref[last, face:], v)
    v = jnp.concatenate(face_vector(0, count, rhs_ref, link_ref, low, up, zero, zero), axis=0)
    next_low = y_ref[0, :face] + dot(ff_ref[0, :face], v)
    return (up[last], next_up), (low[0], next_low)


def store_messages(upward, downward, first_ref, second_ref):
    even = lax.rem(lax.axis_index("sub"), 2) == 0
    at = 0
    for one, other in zip(upward, downward):
        rows = pl.ds(at, one.shape[0])
        first_ref[rows] = jnp.where(even, one, other)
        second_ref[rows] = jnp.where(even, other, one)
        at += one.shape[0]


def received(first_ref, second_ref, rows):
    even = lax.rem(lax.axis_index("sub"), 2) == 0
    first, second = first_ref[rows], second_ref[rows]
    return jnp.where(even, second, first), jnp.where(even, first, second)


def prepare(count, start_ref, source_ref, inverse_ref, map_ref, trans_ref,
            ff_ref, fm_ref, rf_ref, rm_ref, rhs_ref, source_out, y_ref, link_ref, faces_ref,
            mean_ref, first_ref, second_ref):
    width = start_ref.shape[1]
    face = map_ref.shape[2]
    inner = slice(face, width - face)
    ends = (slice(0, face), slice(width - face, width))
    me, size = lax.axis_index("sub"), lax.axis_size("sub")
    low, up, middle, means = [], [], [], []
    for i in range(count):
        perms = []
        for side in range(2):
            linked = iota((face, face), 0) == map_ref[i, side : side + 1, :]
            perm = linked.astype(F32).astype(BF16)
            column = jnp.sum(
                jnp.where(linked, trans_ref[i, side : side + 1, :], 0.0), axis=1, keepdims=True
            )
            if i == 0 and side == 0:
                column = jnp.where(me == 0, 0.0, column)
            if i == count - 1 and side == 1:
                column = jnp.where(me == size - 1, 0.0, column)
            link_ref[2 * i + side] = jnp.broadcast_to(column, (face, start_ref.shape[2]))
            perms.append(perm)
            to = slice(side * face, (side + 1) * face)
            columns = dot(inverse_ref[i, :, ends[side]], perm, ((1,), (1,))).astype(BF16)
            ff_ref[i, :face, to] = columns[:face]
            ff_ref[i, face:, to] = columns[width - face :]
            rf_ref[i, 2 * face :, to] = columns[inner]
            value = start_ref[i, ends[side]]
            high = value.astype(BF16)
            rest = value - high.astype(F32)
            mid = rest.astype(BF16)
            tail = (rest - mid.astype(F32)).astype(BF16)
            permuted = dot(perm, high) + dot(perm, mid) + dot(perm, tail)
            wells = dot(perm, source_ref[i, ends[side]])
            rhs_ref[i, to] = permuted + wells
            source_out[i, to] = wells
        fm_ref[i, :face] = inverse_ref[i, :face, inner]
        fm_ref[i, face:] = inverse_ref[i, width - face :, inner]
        for side in range(2):
            to = slice(side * face, (side + 1) * face)
            rf_ref[i, to] = dot(perms[side], ff_ref[i, to]).astype(BF16)
            rm_ref[i, to] = dot(perms[side], fm_ref[i, to]).astype(BF16)
        rm_ref[i, 2 * face :] = inverse_ref[i, inner, inner]
        wells = source_ref[i, inner].astype(F32)
        rhs_ref[i, 2 * face :] = start_ref[i, inner] + wells
        source_out[i, 2 * face :] = wells
        low.append(start_ref[i, ends[0]])
        up.append(start_ref[i, ends[1]])
        faces_ref[i, :face] = low[i]
        faces_ref[i, face:] = up[i]
        mean_ref[i : i + 1] = jnp.sum(start_ref[i], axis=0, keepdims=True) / width
        y_ref[i] = dot(fm_ref[i], rhs_ref[i, 2 * face :].astype(BF16))
    upward, downward = outgoing(count, ff_ref, y_ref, rhs_ref, link_ref, low, up)
    last = count - 1
    upward += (ff_ref[last, face:, face:].astype(F32), transpose(link_ref[2 * last + 1])[:8])
    downward += (ff_ref[0, :face, :face].astype(F32), transpose(link_ref[0])[:8])
    store_messages(upward, downward, first_ref, second_ref)


def load_faces(count, faces_ref):
    face = faces_ref.shape[1] // 2
    return [faces_ref[i, :face] for i in range(count)], [faces_ref[i, face:] for i in range(count)]


def window(count, first_ref, second_ref, ff_ref, y_ref, rhs_ref, link_ref, faces_ref, near_ref, near_link_ref):
    low, up = load_faces(count, faces_ref)
    face = low[0].shape[0]
    below, above = received(first_ref, second_ref, slice(0, face))
    next_below, next_above = received(first_ref, second_ref, slice(face, 2 * face))
    next_below += dot(near_ref[0], (near_link_ref[0] * low[0]).astype(BF16))
    next_above += dot(near_ref[1], (near_link_ref[1] * up[count - 1]).astype(BF16))
    _, low, up = face_sweep(count, ff_ref, y_ref, rhs_ref, link_ref, low, up, below, above)
    return face_sweep(count, ff_ref, y_ref, rhs_ref, link_ref, low, up, next_below, next_above)


def middle_window(count, opening, *refs):
    if opening:
        (first_ref, second_ref, ff_ref, y_ref, rhs_ref, link_ref, faces_ref,
         new_faces, out_first, out_second, near_ref, near_link_ref) = refs
        face = faces_ref.shape[1] // 2
        for k, part in enumerate(received(first_ref, second_ref, slice(2 * face, 3 * face))):
            near_ref[k] = part.astype(BF16)
        for k, part in enumerate(received(first_ref, second_ref, slice(3 * face, 3 * face + 8))):
            near_link_ref[k] = transpose(jnp.broadcast_to(part[:1], (face, face)))
    else:
        (first_ref, second_ref, ff_ref, y_ref, rhs_ref, link_ref, faces_ref, near_ref, near_link_ref,
         new_faces, out_first, out_second) = refs
        face = faces_ref.shape[1] // 2
    _, low, up = window(
        count, first_ref, second_ref, ff_ref, y_ref, rhs_ref, link_ref, faces_ref, near_ref, near_link_ref
    )
    for i in range(count):
        new_faces[i, :face] = low[i]
        new_faces[i, face:] = up[i]
    store_messages(*outgoing(count, ff_ref, y_ref, rhs_ref, link_ref, low, up), out_first, out_second)


def step_window(count, first_ref, second_ref, ff_ref, y_ref, rhs_ref, link_ref, faces_ref, near_ref,
                near_link_ref, fm_ref, rf_ref, rm_ref, source_ref,
                new_faces, out_first, out_second, new_rhs, new_y):
    face = faces_ref.shape[1] // 2
    vectors, low, up = window(
        count, first_ref, second_ref, ff_ref, y_ref, rhs_ref, link_ref, faces_ref, near_ref, near_link_ref
    )
    for i in range(count):
        new_faces[i, :face] = low[i]
        new_faces[i, face:] = up[i]
        state = dot(rf_ref[i], vectors[i]) + dot(rm_ref[i], rhs_ref[i, 2 * face :].astype(BF16))
        rhs = state + source_ref[i]
        new_rhs[i] = rhs
        new_y[i] = dot(fm_ref[i], rhs[2 * face :].astype(BF16))
    store_messages(*outgoing(count, ff_ref, new_y, new_rhs, link_ref, low, up), out_first, out_second)


def last_window(count, first_ref, second_ref, ff_ref, y_ref, rhs_ref, link_ref, faces_ref, near_ref,
                near_link_ref, rf_ref, rm_ref, mean_ref, end_ref, means_ref):
    face = faces_ref.shape[1] // 2
    width = end_ref.shape[1]
    vectors, low, up = window(
        count, first_ref, second_ref, ff_ref, y_ref, rhs_ref, link_ref, faces_ref, near_ref, near_link_ref
    )
    rows = []
    for i in range(count):
        inner = dot(rf_ref[i, 2 * face :], vectors[i]) + dot(
            rm_ref[i, 2 * face :], rhs_ref[i, 2 * face :].astype(BF16)
        )
        end_ref[i, :face] = low[i]
        end_ref[i, face : width - face] = inner
        end_ref[i, width - face :] = up[i]
        total = jnp.sum(low[i], axis=0, keepdims=True) + jnp.sum(up[i], axis=0, keepdims=True)
        rows.append((total + jnp.sum(inner, axis=0, keepdims=True)) / width)
    rows += [mean_ref[i : i + 1] for i in range(count)]
    block = jnp.concatenate(rows, axis=0)
    for k in range(means_ref.shape[0] // (2 * count)):
        means_ref[2 * count * k : 2 * count * (k + 1)] = block


def coarse_operator(partner_row, partner_col, cond_row, cond_col, out_ref):
    n = out_ref.shape[0]
    row, col = iota((n, n), 0), iota((n, n), 1)
    chain = (jnp.abs(row - col) == 1).astype(F32)
    weights = (
        chain
        + jnp.where(partner_col[...] == col, cond_col[...], 0.0)
        + jnp.where(partner_row[...] == row, cond_row[...], 0.0)
    )
    eye = (row == col).astype(F32)
    m = eye + eye * jnp.sum(weights, axis=1, keepdims=True) - weights
    for i in range(n):
        pivot = 1.0 / m[i : i + 1, i : i + 1]
        line = m[i : i + 1, :] * pivot
        column = m[:, i : i + 1]
        inner = jnp.where(col == i, -column * pivot, m - column * line)
        m = jnp.where(row == i, jnp.where(col == i, pivot, line), inner)
    out_ref[...] = m


def correct(count, slices, means_ref, op_ref, previous_ref, start_ref, out_ref):
    here = lax.axis_index("cuts")
    me = lax.axis_index("sub")
    blocks = op_ref.shape[0]
    per = means_ref.shape[0] // slices
    shape = (blocks, per)
    block = iota(shape, 0)
    place = iota(shape, 1)
    unit, item = place // (2 * count), lax.rem(place, 2 * count)
    take_end = (unit * count + item == block) & (item < count)
    take_start = (unit * count + item - count == block) & (item >= count)
    take_end = take_end.astype(F32)
    take_start = take_start.astype(F32)
    op = op_ref[...]
    shift = jnp.zeros((blocks, means_ref.shape[1]), F32)
    for s in range(1, slices - 1):
        jump = dot(take_end, means_ref[(s - 1) * per : s * per], precision=HIGH) - dot(
            take_start, means_ref[s * per : (s + 1) * per], precision=HIGH
        )
        shift = jnp.where(s < here, dot(op, shift + jump, precision=HIGH), shift)
    chosen = (iota((8, blocks), 1) == me * count + iota((8, blocks), 0)).astype(F32)
    mine = dot(chosen, shift, precision=HIGH)
    later = here > 0
    for i in range(count):
        out_ref[i] = jnp.where(later, previous_ref[i] + mine[i : i + 1], start_ref[i])


def exchange(first, second):
    size = lax.axis_size("sub")
    pairs = [(i, i ^ 1) for i in range(size)]
    other = [(i, (i + (1 if i % 2 else -1)) % size) for i in range(size)]
    far = lax.ppermute(second, "sub", other)
    near = lax.ppermute(first, "sub", pairs)
    return near, far


def on_device(slices, start_states, source, block_inverse, face_map, transmissibility, partner, fracture_cond):
    start = start_states[0]
    count, width, scenarios = start.shape
    face = face_map.shape[-1]
    inner = width - 2 * face
    sub = lax.axis_size("sub")
    sds = jax.ShapeDtypeStruct
    message = sds((2 * face, scenarios), F32)
    opening = sds((3 * face + 8, scenarios), F32)
    faces_shape = sds((count, 2 * face, scenarios), F32)
    rhs_shape = sds((count, width, scenarios), F32)
    ff, fm, rf, rm, rhs, wells, y, link, faces, mean, first, second = call(
        functools.partial(prepare, count),
        [
            sds((count, 2 * face, 2 * face), BF16),
            sds((count, 2 * face, inner), BF16),
            sds((count, width, 2 * face), BF16),
            sds((count, width, inner), BF16),
            rhs_shape,
            rhs_shape,
            faces_shape,
            sds((2 * count, face, scenarios), F32),
            faces_shape,
            sds((count, scenarios), F32),
            opening,
            opening,
        ],
        (start, source, block_inverse, face_map, transmissibility),
    )
    blocks = partner.shape[0]
    (op,) = call(
        coarse_operator,
        [sds((blocks, blocks), F32)],
        (
            partner.reshape(1, blocks),
            partner.reshape(blocks, 1),
            fracture_cond.reshape(1, blocks),
            fracture_cond.reshape(blocks, 1),
        ),
    )
    near = near_link = None
    for step in range(FINE_STEPS):
        for turn in range(0, SWEEPS, 2):
            first, second = exchange(first, second)
            common = (first, second, ff, y, rhs, link, faces)
            if turn < SWEEPS - 2:
                outs = [faces_shape, message, message]
                if near is None:
                    outs += [sds((2, face, face), BF16), sds((2, face, scenarios), F32)]
                    faces, first, second, near, near_link = call(
                        functools.partial(middle_window, count, True), outs, common
                    )
                else:
                    faces, first, second = call(
                        functools.partial(middle_window, count, False), outs, common + (near, near_link)
                    )
            elif step < FINE_STEPS - 1:
                faces, first, second, rhs, y = call(
                    functools.partial(step_window, count),
                    [faces_shape, message, message, rhs_shape, faces_shape],
                    common + (near, near_link, fm, rf, rm, wells),
                )
            else:
                end, means = call(
                    functools.partial(last_window, count),
                    [rhs_shape, sds((slices * sub * 2 * count, scenarios), F32)],
                    common + (near, near_link, rf, rm, mean),
                )
    previous = lax.ppermute(end, "cuts", [(i, (i + 1) % slices) for i in range(slices)])
    means = lax.all_to_all(means, ("cuts", "sub"), 0, 0, tiled=True)
    (result,) = call(
        functools.partial(correct, count, slices), [rhs_shape], (means, op, previous, start)
    )
    return result[None]


def solution(mesh):
    slices = mesh.shape["cuts"]
    in_specs = (
        P("cuts", "sub", None, None),
        P("sub", None, None),
        P("sub", None, None),
        P("sub", None, None),
        P("sub", None, None),
        P(),
        P(),
    )
    return jax.shard_map(
        functools.partial(on_device, slices),
        mesh=mesh,
        in_specs=in_specs,
        out_specs=P("cuts", "sub", None, None),
        check_vma=False,
    )
```

profile of v0, /device:TPU:0, one launch (start us, length us, event | category | flops | bytes accessed | tf_op | source)
XLA Modules:
  0.0 97.3 jit_solution(14491362380892614429)
XLA Ops:
  1.0 1.2 %copy-done.2 = bf16[2,512,512]{2,1,0:T(8,128)(2,1)S(1)} copy-done((bf16[2,512,512]{2,1,0:T(8,128)(2,1)S(1)}, bf16[2,512,512]{2,1,0:T(8,128)(2,1)}, u32[]{:S(2)}) %copy-start.2) | copy-done | bytes 1048600
  5.5 3.0 %collective-permute-start = (f32[392,128]{1,0:T(8,128)S(1)}, f32[392,128]{1,0:T(8,128)S(1)}, u32[]{:S(2)}, u32[]{:S(2)}) collective-permute-start(f32[392,128]{1,0:T(8,128)S(1)} %get-tuple-element.48), channel_id=1, source_target_pairs={{0,1},{1,0},{2,3},{3,2},{4,5},{5,4},{6,7},{7,6},{8,9},{9,8},{10,11... | collective-permute-start | bytes 602120 | tf_op jit(solution)/shard_map/ppermute | solution.py:280
  8.5 3.6 %collective-permute-start.1 = (f32[392,128]{1,0:T(8,128)S(1)}, f32[392,128]{1,0:T(8,128)S(1)}, u32[]{:S(2)}, u32[]{:S(2)}) collective-permute-start(f32[392,128]{1,0:T(8,128)S(1)} %get-tuple-element.49), channel_id=1, source_target_pairs={{0,7},{1,2},{2,1},{3,4},{4,3},{5,6},{6,5},{7,0},{8,15},{9,10},{10,... | collective-permute-start | bytes 602120 | tf_op jit(solution)/shard_map/ppermute | solution.py:279
  12.1 5.7 %collective-permute-done.refs_0_ = f32[392,128]{1,0:T(8,128)S(1)} collective-permute-done((f32[392,128]{1,0:T(8,128)S(1)}, f32[392,128]{1,0:T(8,128)S(1)}, u32[]{:S(2)}, u32[]{:S(2)}) %collective-permute-start) | collective-permute-done | bytes 200736 | tf_op jit(solution)/shard_map/ppermute | solution.py:280
  18.5 1.8 %collective-permute-start.2 = (f32[256,128]{1,0:T(8,128)S(1)}, f32[256,128]{1,0:T(8,128)S(1)}, u32[]{:S(2)}, u32[]{:S(2)}) collective-permute-start(f32[256,128]{1,0:T(8,128)S(1)} %get-tuple-element.55), channel_id=1, source_target_pairs={{0,1},{1,0},{2,3},{3,2},{4,5},{5,4},{6,7},{7,6},{8,9},{9,8},{10,11... | collective-permute-start | bytes 393224 | tf_op jit(solution)/shard_map/ppermute | solution.py:280
  20.3 3.6 %collective-permute-start.3 = (f32[256,128]{1,0:T(8,128)S(1)}, f32[256,128]{1,0:T(8,128)S(1)}, u32[]{:S(2)}, u32[]{:S(2)}) collective-permute-start(f32[256,128]{1,0:T(8,128)S(1)} %get-tuple-element.56), channel_id=1, source_target_pairs={{0,7},{1,2},{2,1},{3,4},{4,3},{5,6},{6,5},{7,0},{8,15},{9,10},{10,... | collective-permute-start | bytes 393224 | tf_op jit(solution)/shard_map/ppermute | solution.py:279
  25.0 2.9 %collective-permute-done.3.second_ref = f32[256,128]{1,0:T(8,128)S(1)} collective-permute-done((f32[256,128]{1,0:T(8,128)S(1)}, f32[256,128]{1,0:T(8,128)S(1)}, u32[]{:S(2)}, u32[]{:S(2)}) %collective-permute-start.3) | collective-permute-done | bytes 131104 | tf_op jit(solution)/shard_map/ppermute | solution.py:279
  29.3 3.7 %collective-permute-start.5 = (f32[256,128]{1,0:T(8,128)S(1)}, f32[256,128]{1,0:T(8,128)S(1)}, u32[]{:S(2)}, u32[]{:S(2)}) collective-permute-start(f32[256,128]{1,0:T(8,128)S(1)} %get-tuple-element.65), channel_id=1, source_target_pairs={{0,7},{1,2},{2,1},{3,4},{4,3},{5,6},{6,5},{7,0},{8,15},{9,10},{10,... | collective-permute-start | bytes 393224 | tf_op jit(solution)/shard_map/ppermute | solution.py:279
  32.9 2.1 %collective-permute-done.4.refs_0_ = f32[256,128]{1,0:T(8,128)S(1)} collective-permute-done((f32[256,128]{1,0:T(8,128)S(1)}, f32[256,128]{1,0:T(8,128)S(1)}, u32[]{:S(2)}, u32[]{:S(2)}) %collective-permute-start.4) | collective-permute-done | bytes 131104 | tf_op jit(solution)/shard_map/ppermute | solution.py:280
  35.0 2.0 %collective-permute-done.5.refs_1_ = f32[256,128]{1,0:T(8,128)S(1)} collective-permute-done((f32[256,128]{1,0:T(8,128)S(1)}, f32[256,128]{1,0:T(8,128)S(1)}, u32[]{:S(2)}, u32[]{:S(2)}) %collective-permute-start.5) | collective-permute-done | bytes 131104 | tf_op jit(solution)/shard_map/ppermute | solution.py:279
  37.8 3.6 %collective-permute-start.7 = (f32[256,128]{1,0:T(8,128)S(1)}, f32[256,128]{1,0:T(8,128)S(1)}, u32[]{:S(2)}, u32[]{:S(2)}) collective-permute-start(f32[256,128]{1,0:T(8,128)S(1)} %get-tuple-element.70), channel_id=1, source_target_pairs={{0,7},{1,2},{2,1},{3,4},{4,3},{5,6},{6,5},{7,0},{8,15},{9,10},{10,... | collective-permute-start | bytes 393224 | tf_op jit(solution)/shard_map/ppermute | solution.py:279
  41.4 1.3 %collective-permute-done.6.first_ref = f32[256,128]{1,0:T(8,128)S(1)} collective-permute-done((f32[256,128]{1,0:T(8,128)S(1)}, f32[256,128]{1,0:T(8,128)S(1)}, u32[]{:S(2)}, u32[]{:S(2)}) %collective-permute-start.6) | collective-permute-done | bytes 131104 | tf_op jit(solution)/shard_map/ppermute | solution.py:280
  42.7 2.9 %collective-permute-done.7.second_ref = f32[256,128]{1,0:T(8,128)S(1)} collective-permute-done((f32[256,128]{1,0:T(8,128)S(1)}, f32[256,128]{1,0:T(8,128)S(1)}, u32[]{:S(2)}, u32[]{:S(2)}) %collective-permute-start.7) | collective-permute-done | bytes 131104 | tf_op jit(solution)/shard_map/ppermute | solution.py:279
  45.6 1.2 %shard_map.77 = (f32[2,256,128]{2,1,0:T(8,128)S(1)}, f32[256,128]{1,0:T(8,128)S(1)}, f32[256,128]{1,0:T(8,128)S(1)}, f32[2,512,128]{2,1,0:T(8,128)S(1)}, f32[2,256,128]{2,1,0:T(8,128)S(1)}) custom-call(f32[256,128]{1,0:T(8,128)S(1)} %collective-permute-done.6.first_ref, f32[256,128]{1,0:T(8,128)S(1)} %collective-permute-done.7.second_ref, ...), custom_call_target="tpu_custom_call" | custom-call | flops 268435456 | bytes 5177344 | tf_op jit(solution)/shard_map/pallas_call | solution.py:32
  46.9 3.6 %collective-permute-start.9 = (f32[256,128]{1,0:T(8,128)S(1)}, f32[256,128]{1,0:T(8,128)S(1)}, u32[]{:S(2)}, u32[]{:S(2)}) collective-permute-start(f32[256,128]{1,0:T(8,128)S(1)} %get-tuple-element.73), channel_id=1, source_target_pairs={{0,7},{1,2},{2,1},{3,4},{4,3},{5,6},{6,5},{7,0},{8,15},{9,10},{10,... | collective-permute-start | bytes 393224 | tf_op jit(solution)/shard_map/ppermute | solution.py:279
  50.5 1.3 %collective-permute-done.8.refs_0_ = f32[256,128]{1,0:T(8,128)S(1)} collective-permute-done((f32[256,128]{1,0:T(8,128)S(1)}, f32[256,128]{1,0:T(8,128)S(1)}, u32[]{:S(2)}, u32[]{:S(2)}) %collective-permute-start.8) | collective-permute-done | bytes 131104 | tf_op jit(solution)/shard_map/ppermute | solution.py:280
  51.8 2.9 %collective-permute-done.9.refs_1_ = f32[256,128]{1,0:T(8,128)S(1)} collective-permute-done((f32[256,128]{1,0:T(8,128)S(1)}, f32[256,128]{1,0:T(8,128)S(1)}, u32[]{:S(2)}, u32[]{:S(2)}) %collective-permute-start.9) | collective-permute-done | bytes 131104 | tf_op jit(solution)/shard_map/ppermute | solution.py:279
  55.7 3.5 %collective-permute-start.11 = (f32[256,128]{1,0:T(8,128)S(1)}, f32[256,128]{1,0:T(8,128)S(1)}, u32[]{:S(2)}, u32[]{:S(2)}) collective-permute-start(f32[256,128]{1,0:T(8,128)S(1)} %get-tuple-element.78), channel_id=1, source_target_pairs={{0,7},{1,2},{2,1},{3,4},{4,3},{5,6},{6,5},{7,0},{8,15},{9,10},{10,... | collective-permute-start | bytes 393224 | tf_op jit(solution)/shard_map/ppermute | solution.py:279
  59.2 1.7 %collective-permute-done.10.first_ref = f32[256,128]{1,0:T(8,128)S(1)} collective-permute-done((f32[256,128]{1,0:T(8,128)S(1)}, f32[256,128]{1,0:T(8,128)S(1)}, u32[]{:S(2)}, u32[]{:S(2)}) %collective-permute-start.10) | collective-permute-done | bytes 131104 | tf_op jit(solution)/shard_map/ppermute | solution.py:280
  60.9 3.4 %collective-permute-done.11.second_ref = f32[256,128]{1,0:T(8,128)S(1)} collective-permute-done((f32[256,128]{1,0:T(8,128)S(1)}, f32[256,128]{1,0:T(8,128)S(1)}, u32[]{:S(2)}, u32[]{:S(2)}) %collective-permute-start.11) | collective-permute-done | bytes 131104 | tf_op jit(solution)/shard_map/ppermute | solution.py:279
  64.3 1.2 %shard_map.79 = (f32[2,256,128]{2,1,0:T(8,128)S(1)}, f32[256,128]{1,0:T(8,128)S(1)}, f32[256,128]{1,0:T(8,128)S(1)}, f32[2,512,128]{2,1,0:T(8,128)S(1)}, f32[2,256,128]{2,1,0:T(8,128)S(1)}) custom-call(f32[256,128]{1,0:T(8,128)S(1)} %collective-permute-done.10.first_ref, f32[256,128]{1,0:T(8,128)S(1)} %collective-permute-done.11.second_ref, ...), custom_call_target="tpu_custom_call" | custom-call | flops 268435456 | bytes 5177344 | tf_op jit(solution)/shard_map/pallas_call | solution.py:32
  65.5 3.4 %collective-permute-start.13 = (f32[256,128]{1,0:T(8,128)S(1)}, f32[256,128]{1,0:T(8,128)S(1)}, u32[]{:S(2)}, u32[]{:S(2)}) collective-permute-start(f32[256,128]{1,0:T(8,128)S(1)} %get-tuple-element.81), channel_id=1, source_target_pairs={{0,7},{1,2},{2,1},{3,4},{4,3},{5,6},{6,5},{7,0},{8,15},{9,10},{10,... | collective-permute-start | bytes 393224 | tf_op jit(solution)/shard_map/ppermute | solution.py:279
  69.0 2.4 %collective-permute-done.12.refs_0_ = f32[256,128]{1,0:T(8,128)S(1)} collective-permute-done((f32[256,128]{1,0:T(8,128)S(1)}, f32[256,128]{1,0:T(8,128)S(1)}, u32[]{:S(2)}, u32[]{:S(2)}) %collective-permute-start.12) | collective-permute-done | bytes 131104 | tf_op jit(solution)/shard_map/ppermute | solution.py:280
  71.4 2.2 %collective-permute-done.13.refs_1_ = f32[256,128]{1,0:T(8,128)S(1)} collective-permute-done((f32[256,128]{1,0:T(8,128)S(1)}, f32[256,128]{1,0:T(8,128)S(1)}, u32[]{:S(2)}, u32[]{:S(2)}) %collective-permute-start.13) | collective-permute-done | bytes 131104 | tf_op jit(solution)/shard_map/ppermute | solution.py:279
  74.5 3.5 %collective-permute-start.15 = (f32[256,128]{1,0:T(8,128)S(1)}, f32[256,128]{1,0:T(8,128)S(1)}, u32[]{:S(2)}, u32[]{:S(2)}) collective-permute-start(f32[256,128]{1,0:T(8,128)S(1)} %get-tuple-element.86), channel_id=1, source_target_pairs={{0,7},{1,2},{2,1},{3,4},{4,3},{5,6},{6,5},{7,0},{8,15},{9,10},{10,... | collective-permute-start | bytes 393224 | tf_op jit(solution)/shard_map/ppermute | solution.py:279
  77.9 1.2 %collective-permute-done.14.first_ref = f32[256,128]{1,0:T(8,128)S(1)} collective-permute-done((f32[256,128]{1,0:T(8,128)S(1)}, f32[256,128]{1,0:T(8,128)S(1)}, u32[]{:S(2)}, u32[]{:S(2)}) %collective-permute-start.14) | collective-permute-done | bytes 131104 | tf_op jit(solution)/shard_map/ppermute | solution.py:280
  79.2 3.0 %collective-permute-done.15.second_ref = f32[256,128]{1,0:T(8,128)S(1)} collective-permute-done((f32[256,128]{1,0:T(8,128)S(1)}, f32[256,128]{1,0:T(8,128)S(1)}, u32[]{:S(2)}, u32[]{:S(2)}) %collective-permute-start.15) | collective-permute-done | bytes 131104 | tf_op jit(solution)/shard_map/ppermute | solution.py:279
  82.2 1.3 %shard_map.81 = (f32[2,512,128]{2,1,0:T(8,128)S(1)}, f32[128,128]{1,0:T(8,128)}) custom-call(f32[256,128]{1,0:T(8,128)S(1)} %collective-permute-done.14.first_ref, f32[256,128]{1,0:T(8,128)S(1)} %collective-permute-done.15.second_ref, bf16[2,256,256]{2,1,0:T(8,128)(2,1)S(1)} %get-tuple-element.50.refs_2_.ff_ref, ...), custom_call_target="tpu_custom_call" | custom-call | flops 268435456 | bytes 3671040 | tf_op jit(solution)/shard_map/pallas_call | solution.py:32
  83.4 5.1 %all-to-all-start = ((f32[32,4,128]{2,1,0:T(4,128)}), f32[32,4,128]{2,1,0:T(4,128)S(1)}, u32[]{:S(2)}, u32[]{:S(2)}) async-start(f32[32,4,128]{2,1,0:T(4,128)} %bitcast.1), calls=%async_computation | async-start | bytes 131072 | tf_op jit(solution)/shard_map/all_to_all | solution.py:353
  88.7 2.0 %shard_map.82.op_ref = f32[16,16]{1,0:T(8,128)S(1)} custom-call(s32[1,16]{1,0:T(1,128)S(1)} %bitcast.12, s32[16,1]{1,0:T(8,128)S(1)} %copy.8.partner_col, f32[1,16]{1,0:T(1,128)S(1)} %bitcast.14, f32[16,1]{1,0:T(8,128)S(1)} %copy.9.cond_col), custom_call_target="tpu_custom_call" | custom-call | flops 268435456 | bytes 1280 | tf_op jit(solution)/shard_map/pallas_call | solution.py:32
  90.7 5.0 %all-to-all-done = f32[32,4,128]{2,1,0:T(4,128)S(1)} async-done(((f32[32,4,128]{2,1,0:T(4,128)}), f32[32,4,128]{2,1,0:T(4,128)S(1)}, u32[]{:S(2)}, u32[]{:S(2)}) %all-to-all-start) | async-done | bytes 65568 | tf_op jit(solution)/shard_map/all_to_all | solution.py:353
  95.8 1.5 %shard_map.83 = f32[2,512,128]{2,1,0:T(8,128)} custom-call(f32[128,128]{1,0:T(8,128)S(1)} %bitcast.10, f32[16,16]{1,0:T(8,128)S(1)} %shard_map.82.op_ref, f32[2,512,128]{2,1,0:T(8,128)S(1)} %collective-permute-done.16.previous_ref, f32[2,512,128]{2,1,0:T(8,128)S(1)} %bitcast.9), custom_call_target="tpu_custom_call" | custom-call | flops 268435456 | bytes 1639424 | tf_op jit(solution)/shard_map/pallas_call | solution.py:32
  (33 shorter events, 10.6 us)
Async XLA Ops:
  0.0 1.0 %copy-start = (f32[1,2,512,128]{3,2,1,0:T(8,128)S(1)}, f32[1,2,512,128]{3,2,1,0:T(8,128)}, u32[]{:S(2)}) copy-start(f32[1,2,512,128]{3,2,1,0:T(8,128)} %param.7) | copy-start | bytes 1572868
  1.0 1.2 %copy-start.2 = (bf16[2,512,512]{2,1,0:T(8,128)(2,1)S(1)}, bf16[2,512,512]{2,1,0:T(8,128)(2,1)}, u32[]{:S(2)}) copy-start(bf16[2,512,512]{2,1,0:T(8,128)(2,1)} %inverse_ref.1) | copy-start | bytes 3145732
  2.3 0.9 copy-start.3
  3.2 0.7 copy-start.4
  3.9 0.7 copy-start.5
  5.5 12.3 %collective-permute-start = (f32[392,128]{1,0:T(8,128)S(1)}, f32[392,128]{1,0:T(8,128)S(1)}, u32[]{:S(2)}, u32[]{:S(2)}) collective-permute-start(f32[392,128]{1,0:T(8,128)S(1)} %get-tuple-element.48), channel_id=1, source_target_pairs={{0,1},{1,0},{2,3},{3,2},{4,5},{5,4},{6,7},{7,6},{8,9},{9,8},{10,11... | collective-permute-start | bytes 602120 | tf_op jit(solution)/shard_map/ppermute | solution.py:280
  8.5 9.3 %collective-permute-start.1 = (f32[392,128]{1,0:T(8,128)S(1)}, f32[392,128]{1,0:T(8,128)S(1)}, u32[]{:S(2)}, u32[]{:S(2)}) collective-permute-start(f32[392,128]{1,0:T(8,128)S(1)} %get-tuple-element.49), channel_id=1, source_target_pairs={{0,7},{1,2},{2,1},{3,4},{4,3},{5,6},{6,5},{7,0},{8,15},{9,10},{10,... | collective-permute-start | bytes 602120 | tf_op jit(solution)/shard_map/ppermute | solution.py:279
  18.5 6.5 %collective-permute-start.2 = (f32[256,128]{1,0:T(8,128)S(1)}, f32[256,128]{1,0:T(8,128)S(1)}, u32[]{:S(2)}, u32[]{:S(2)}) collective-permute-start(f32[256,128]{1,0:T(8,128)S(1)} %get-tuple-element.55), channel_id=1, source_target_pairs={{0,1},{1,0},{2,3},{3,2},{4,5},{5,4},{6,7},{7,6},{8,9},{9,8},{10,11... | collective-permute-start | bytes 393224 | tf_op jit(solution)/shard_map/ppermute | solution.py:280
  20.3 7.7 %collective-permute-start.3 = (f32[256,128]{1,0:T(8,128)S(1)}, f32[256,128]{1,0:T(8,128)S(1)}, u32[]{:S(2)}, u32[]{:S(2)}) collective-permute-start(f32[256,128]{1,0:T(8,128)S(1)} %get-tuple-element.56), channel_id=1, source_target_pairs={{0,7},{1,2},{2,1},{3,4},{4,3},{5,6},{6,5},{7,0},{8,15},{9,10},{10,... | collective-permute-start | bytes 393224 | tf_op jit(solution)/shard_map/ppermute | solution.py:279
  29.2 5.8 %collective-permute-start.4 = (f32[256,128]{1,0:T(8,128)S(1)}, f32[256,128]{1,0:T(8,128)S(1)}, u32[]{:S(2)}, u32[]{:S(2)}) collective-permute-start(f32[256,128]{1,0:T(8,128)S(1)} %get-tuple-element.64), channel_id=1, source_target_pairs={{0,1},{1,0},{2,3},{3,2},{4,5},{5,4},{6,7},{7,6},{8,9},{9,8},{10,11... | collective-permute-start | bytes 393224 | tf_op jit(solution)/shard_map/ppermute | solution.py:280
  29.3 7.8 %collective-permute-start.5 = (f32[256,128]{1,0:T(8,128)S(1)}, f32[256,128]{1,0:T(8,128)S(1)}, u32[]{:S(2)}, u32[]{:S(2)}) collective-permute-start(f32[256,128]{1,0:T(8,128)S(1)} %get-tuple-element.65), channel_id=1, source_target_pairs={{0,7},{1,2},{2,1},{3,4},{4,3},{5,6},{6,5},{7,0},{8,15},{9,10},{10,... | collective-permute-start | bytes 393224 | tf_op jit(solution)/shard_map/ppermute | solution.py:279
  37.6 5.0 %collective-permute-start.6 = (f32[256,128]{1,0:T(8,128)S(1)}, f32[256,128]{1,0:T(8,128)S(1)}, u32[]{:S(2)}, u32[]{:S(2)}) collective-permute-start(f32[256,128]{1,0:T(8,128)S(1)} %get-tuple-element.69), channel_id=1, source_target_pairs={{0,1},{1,0},{2,3},{3,2},{4,5},{5,4},{6,7},{7,6},{8,9},{9,8},{10,11... | collective-permute-start | bytes 393224 | tf_op jit(solution)/shard_map/ppermute | solution.py:280
  37.8 7.8 %collective-permute-start.7 = (f32[256,128]{1,0:T(8,128)S(1)}, f32[256,128]{1,0:T(8,128)S(1)}, u32[]{:S(2)}, u32[]{:S(2)}) collective-permute-start(f32[256,128]{1,0:T(8,128)S(1)} %get-tuple-element.70), channel_id=1, source_target_pairs={{0,7},{1,2},{2,1},{3,4},{4,3},{5,6},{6,5},{7,0},{8,15},{9,10},{10,... | collective-permute-start | bytes 393224 | tf_op jit(solution)/shard_map/ppermute | solution.py:279
  46.8 5.0 %collective-permute-start.8 = (f32[256,128]{1,0:T(8,128)S(1)}, f32[256,128]{1,0:T(8,128)S(1)}, u32[]{:S(2)}, u32[]{:S(2)}) collective-permute-start(f32[256,128]{1,0:T(8,128)S(1)} %get-tuple-element.72), channel_id=1, source_target_pairs={{0,1},{1,0},{2,3},{3,2},{4,5},{5,4},{6,7},{7,6},{8,9},{9,8},{10,11... | collective-permute-start | bytes 393224 | tf_op jit(solution)/shard_map/ppermute | solution.py:280
  46.9 7.8 %collective-permute-start.9 = (f32[256,128]{1,0:T(8,128)S(1)}, f32[256,128]{1,0:T(8,128)S(1)}, u32[]{:S(2)}, u32[]{:S(2)}) collective-permute-start(f32[256,128]{1,0:T(8,128)S(1)} %get-tuple-element.73), channel_id=1, source_target_pairs={{0,7},{1,2},{2,1},{3,4},{4,3},{5,6},{6,5},{7,0},{8,15},{9,10},{10,... | collective-permute-start | bytes 393224 | tf_op jit(solution)/shard_map/ppermute | solution.py:279
  55.3 5.6 %collective-permute-start.10 = (f32[256,128]{1,0:T(8,128)S(1)}, f32[256,128]{1,0:T(8,128)S(1)}, u32[]{:S(2)}, u32[]{:S(2)}) collective-permute-start(f32[256,128]{1,0:T(8,128)S(1)} %get-tuple-element.77), channel_id=1, source_target_pairs={{0,1},{1,0},{2,3},{3,2},{4,5},{5,4},{6,7},{7,6},{8,9},{9,8},{10,11... | collective-permute-start | bytes 393224 | tf_op jit(solution)/shard_map/ppermute | solution.py:280
  55.7 8.5 %collective-permute-start.11 = (f32[256,128]{1,0:T(8,128)S(1)}, f32[256,128]{1,0:T(8,128)S(1)}, u32[]{:S(2)}, u32[]{:S(2)}) collective-permute-start(f32[256,128]{1,0:T(8,128)S(1)} %get-tuple-element.78), channel_id=1, source_target_pairs={{0,7},{1,2},{2,1},{3,4},{4,3},{5,6},{6,5},{7,0},{8,15},{9,10},{10,... | collective-permute-start | bytes 393224 | tf_op jit(solution)/shard_map/ppermute | solution.py:279
  65.5 5.9 %collective-permute-start.12 = (f32[256,128]{1,0:T(8,128)S(1)}, f32[256,128]{1,0:T(8,128)S(1)}, u32[]{:S(2)}, u32[]{:S(2)}) collective-permute-start(f32[256,128]{1,0:T(8,128)S(1)} %get-tuple-element.80), channel_id=1, source_target_pairs={{0,1},{1,0},{2,3},{3,2},{4,5},{5,4},{6,7},{7,6},{8,9},{9,8},{10,11... | collective-permute-start | bytes 393224 | tf_op jit(solution)/shard_map/ppermute | solution.py:280
  65.5 8.0 %collective-permute-start.13 = (f32[256,128]{1,0:T(8,128)S(1)}, f32[256,128]{1,0:T(8,128)S(1)}, u32[]{:S(2)}, u32[]{:S(2)}) collective-permute-start(f32[256,128]{1,0:T(8,128)S(1)} %get-tuple-element.81), channel_id=1, source_target_pairs={{0,7},{1,2},{2,1},{3,4},{4,3},{5,6},{6,5},{7,0},{8,15},{9,10},{10,... | collective-permute-start | bytes 393224 | tf_op jit(solution)/shard_map/ppermute | solution.py:279
  74.1 5.0 %collective-permute-start.14 = (f32[256,128]{1,0:T(8,128)S(1)}, f32[256,128]{1,0:T(8,128)S(1)}, u32[]{:S(2)}, u32[]{:S(2)}) collective-permute-start(f32[256,128]{1,0:T(8,128)S(1)} %get-tuple-element.85), channel_id=1, source_target_pairs={{0,1},{1,0},{2,3},{3,2},{4,5},{5,4},{6,7},{7,6},{8,9},{9,8},{10,11... | collective-permute-start | bytes 393224 | tf_op jit(solution)/shard_map/ppermute | solution.py:280
  74.5 7.7 %collective-permute-start.15 = (f32[256,128]{1,0:T(8,128)S(1)}, f32[256,128]{1,0:T(8,128)S(1)}, u32[]{:S(2)}, u32[]{:S(2)}) collective-permute-start(f32[256,128]{1,0:T(8,128)S(1)} %get-tuple-element.86), channel_id=1, source_target_pairs={{0,7},{1,2},{2,1},{3,4},{4,3},{5,6},{6,5},{7,0},{8,15},{9,10},{10,... | collective-permute-start | bytes 393224 | tf_op jit(solution)/shard_map/ppermute | solution.py:279
  82.2 6.4 %copy-start.6 = (s32[16]{0:T(128)S(1)}, s32[16]{0:T(128)}, u32[]{:S(2)}) copy-start(s32[16]{0:T(128)} %param.12) | copy-start | bytes 196
  82.2 6.4 %copy-start.7 = (f32[16]{0:T(128)S(1)}, f32[16]{0:T(128)}, u32[]{:S(2)}) copy-start(f32[16]{0:T(128)} %param.13) | copy-start | bytes 196
  83.4 12.3 %collective-permute-start.16 = (f32[2,512,128]{2,1,0:T(8,128)S(1)}, f32[2,512,128]{2,1,0:T(8,128)S(1)}, u32[]{:S(2)}, u32[]{:S(2)}) collective-permute-start(f32[2,512,128]{2,1,0:T(8,128)S(1)} %get-tuple-element.90), channel_id=1, source_target_pairs={{0,8},{8,16},{16,24},{24,0},{1,9},{9,17},{17,25},{25,1},{2,10},{10... | collective-permute-start | bytes 1572872 | tf_op jit(solution)/shard_map/ppermute | solution.py:352
  83.4 12.3 %all-to-all-start = ((f32[32,4,128]{2,1,0:T(4,128)}), f32[32,4,128]{2,1,0:T(4,128)S(1)}, u32[]{:S(2)}, u32[]{:S(2)}) async-start(f32[32,4,128]{2,1,0:T(4,128)} %bitcast.1), calls=%async_computation | async-start | bytes 131072 | tf_op jit(solution)/shard_map/all_to_all | solution.py:353
  88.5 7.3 %copy-start.1 = (f32[1,2,512,128]{3,2,1,0:T(8,128)S(1)}, f32[1,2,512,128]{3,2,1,0:T(8,128)}, u32[]{:S(2)}) copy-start(f32[1,2,512,128]{3,2,1,0:T(8,128)} %param.7) | copy-start | bytes 1572868
where the time goes:
time: 97.6 us; the launch traced here: 97.3 us
  waiting for transfers between devices  41.1 us (42%)
  starting transfers between devices  39.5 us (40%)
  Pallas kernels  11.7 us (12%)
  local copies, waits for them, and re-layouts  4.76 us (5%)
    ppermute x8, starting transfers between devices, exchange(): far = lax.ppermute(second, 'sub', other)  28.3 us
    ppermute x8, waiting for transfers between devices, exchange(): far = lax.ppermute(second, 'sub', other)  19.3 us
    ppermute x8, waiting for transfers between devices, exchange(): near = lax.ppermute(first, 'sub', pairs)  16.8 us
    pallas_call x11, Pallas kernels, call(): pl.pallas_call(body, out_shape=out_shape, in_specs=[vmem] * len(args), ou...  11.7 us
    ppermute x8, starting transfers between devices, exchange(): near = lax.ppermute(first, 'sub', pairs)  6.13 us
    all_to_all x1, starting transfers between devices, on_device(): means = lax.all_to_all(means, ('cuts', 'sub'), 0, 0, tiled=True)  5.06 us
    all_to_all x1, waiting for transfers between devices, on_device(): means = lax.all_to_all(means, ('cuts', 'sub'), 0, 0, tiled=True)  5.04 us
    unnamed x16, local copies, waits for them, and re-layouts  4.59 us
  transfers between devices with their start and end apart: 18, of which 16 were waited for; matrix products, arithmetic and copies ran while one was open for 0% of the time, Pallas kernels for 2%

commit v1 on v0

--- a/solution.py
+++ b/solution.py
@@ -26,14 +26,16 @@
     return lax.broadcasted_iota(jnp.int32, shape, axis)
 
 
-def call(body, out_shape, args, flops=1 << 28):
+def call(body, out_shape, args, flops=1 << 28, stay=(), stay_out=(), scratch=()):
     size = sum(a.size * a.dtype.itemsize for a in list(args) + list(out_shape))
     vmem = pl.BlockSpec(memory_space=pltpu.VMEM)
+    hbm = pl.BlockSpec(memory_space=pltpu.HBM)
     return pl.pallas_call(
         body,
         out_shape=out_shape,
-        in_specs=[vmem] * len(args),
-        out_specs=[vmem] * len(out_shape),
+        in_specs=[hbm if k in stay else vmem for k in range(len(args))],
+        out_specs=[hbm if k in stay_out else vmem for k in range(len(out_shape))],
+        scratch_shapes=list(scratch),
         compiler_params=pltpu.CompilerParams(vmem_limit_bytes=24 << 20),
         cost_estimate=pl.CostEstimate(flops=flops, bytes_accessed=size, transcendentals=0),
     )(*args)
@@ -87,9 +89,25 @@
     return jnp.where(even, second, first), jnp.where(even, first, second)
 
 
-def prepare(count, start_ref, source_ref, inverse_ref, map_ref, trans_ref,
+def prepare(count, start_hbm, source_hbm, inverse_hbm, map_hbm, trans_hbm,
             ff_ref, fm_ref, rf_ref, rm_ref, rhs_ref, source_out, y_ref, link_ref, faces_ref,
-            mean_ref, first_ref, second_ref):
+            mean_ref, first_ref, second_ref,
+            start_ref, source_ref, inverse_ref, map_ref, trans_ref, sems):
+    copies = [
+        pltpu.make_async_copy(map_hbm, map_ref, sems.at[0]),
+        pltpu.make_async_copy(trans_hbm, trans_ref, sems.at[1]),
+    ]
+    for i in range(count):
+        copies += [
+            pltpu.make_async_copy(src.at[i], dst.at[i], sems.at[2 + 3 * i + k])
+            for k, (src, dst) in enumerate(
+                ((inverse_hbm, inverse_ref), (start_hbm, start_ref), (source_hbm, source_ref))
+            )
+        ]
+    for copy in copies:
+        copy.start()
+    copies[0].wait()
+    copies[1].wait()
     width = start_ref.shape[1]
     face = map_ref.shape[2]
     inner = slice(face, width - face)
@@ -98,6 +116,8 @@
     low, up, middle, means = [], [], [], []
     for i in range(count):
         perms = []
+        for copy in copies[2 + 3 * i : 5 + 3 * i]:
+            copy.wait()
         for side in range(2):
             linked = iota((face, face), 0) == map_ref[i, side : side + 1, :]
             perm = linked.astype(F32).astype(BF16)
@@ -186,7 +206,7 @@
 
 
 def step_window(count, first_ref, second_ref, ff_ref, y_ref, rhs_ref, link_ref, faces_ref, near_ref,
-                near_link_ref, fm_ref, rf_ref, rm_ref, source_ref,
+                near_link_ref, fm_ref, rf_ref, base_ref, source_ref,
                 new_faces, out_first, out_second, new_rhs, new_y):
     face = faces_ref.shape[1] // 2
     vectors, low, up = window(
@@ -195,28 +215,36 @@
     for i in range(count):
         new_faces[i, :face] = low[i]
         new_faces[i, face:] = up[i]
-        state = dot(rf_ref[i], vectors[i]) + dot(rm_ref[i], rhs_ref[i, 2 * face :].astype(BF16))
-        rhs = state + source_ref[i]
+        rhs = base_ref[i] + dot(rf_ref[i], vectors[i]) + source_ref[i]
         new_rhs[i] = rhs
         new_y[i] = dot(fm_ref[i], rhs[2 * face :].astype(BF16))
     store_messages(*outgoing(count, ff_ref, new_y, new_rhs, link_ref, low, up), out_first, out_second)
 
 
+def inner_base(count, rhs_ref, rm_ref, base_ref):
+    for i in range(count):
+        face = (rhs_ref.shape[1] - rm_ref.shape[2]) // 2
+        base_ref[i] = dot(rm_ref[i], rhs_ref[i, 2 * face :].astype(BF16))
+
+
+def end_base(count, rhs_ref, rm_ref, y_ref, base_ref):
+    face = y_ref.shape[1] // 2
+    for i in range(count):
+        base_ref[i, : 2 * face] = y_ref[i]
+        base_ref[i, 2 * face :] = dot(rm_ref[i, 2 * face :], rhs_ref[i, 2 * face :].astype(BF16))
+
+
 def last_window(count, first_ref, second_ref, ff_ref, y_ref, rhs_ref, link_ref, faces_ref, near_ref,
-                near_link_ref, rf_ref, rm_ref, mean_ref, end_ref, means_ref):
+                near_link_ref, rf_ref, base_ref, mean_ref, vector_ref, means_ref):
     face = faces_ref.shape[1] // 2
-    width = end_ref.shape[1]
+    width = base_ref.shape[1]
     vectors, low, up = window(
         count, first_ref, second_ref, ff_ref, y_ref, rhs_ref, link_ref, faces_ref, near_ref, near_link_ref
     )
     rows = []
     for i in range(count):
-        inner = dot(rf_ref[i, 2 * face :], vectors[i]) + dot(
-            rm_ref[i, 2 * face :], rhs_ref[i, 2 * face :].astype(BF16)
-        )
-        end_ref[i, :face] = low[i]
-        end_ref[i, face : width - face] = inner
-        end_ref[i, width - face :] = up[i]
+        vector_ref[i] = vectors[i].astype(F32)
+        inner = base_ref[i, 2 * face :] + dot(rf_ref[i, 2 * face :], vectors[i])
         total = jnp.sum(low[i], axis=0, keepdims=True) + jnp.sum(up[i], axis=0, keepdims=True)
         rows.append((total + jnp.sum(inner, axis=0, keepdims=True)) / width)
     rows += [mean_ref[i : i + 1] for i in range(count)]
@@ -225,8 +253,19 @@
         means_ref[2 * count * k : 2 * count * (k + 1)] = block
 
 
-def coarse_operator(partner_row, partner_col, cond_row, cond_col, out_ref):
-    n = out_ref.shape[0]
+def previous_end(count, base_ref, vector_ref, ff_ref, rf_ref, end_ref):
+    face = vector_ref.shape[1] // 2
+    width = base_ref.shape[1]
+    for i in range(count):
+        v = vector_ref[i].astype(BF16)
+        faces = base_ref[i, : 2 * face] + dot(ff_ref[i], v)
+        end_ref[i, :face] = faces[:face]
+        end_ref[i, face : width - face] = base_ref[i, 2 * face :] + dot(rf_ref[i, 2 * face :], v)
+        end_ref[i, width - face :] = faces[face:]
+
+
+def coarse_operator(count, slices, partner_row, partner_col, cond_row, cond_col, out_ref):
+    n = partner_row.shape[1]
     row, col = iota((n, n), 0), iota((n, n), 1)
     chain = (jnp.abs(row - col) == 1).astype(F32)
     weights = (
@@ -242,41 +281,50 @@
         column = m[:, i : i + 1]
         inner = jnp.where(col == i, -column * pivot, m - column * line)
         m = jnp.where(row == i, jnp.where(col == i, pivot, line), inner)
-    out_ref[...] = m
-
-
-def correct(count, slices, means_ref, op_ref, previous_ref, start_ref, out_ref):
-    here = lax.axis_index("cuts")
-    me = lax.axis_index("sub")
-    blocks = op_ref.shape[0]
-    per = means_ref.shape[0] // slices
-    shape = (blocks, per)
-    block = iota(shape, 0)
-    place = iota(shape, 1)
+    here, me = lax.axis_index("cuts"), lax.axis_index("sub")
+    per = out_ref.shape[1] // slices
+    shape = (n, per)
+    block, place = iota(shape, 0), iota(shape, 1)
     unit, item = place // (2 * count), lax.rem(place, 2 * count)
-    take_end = (unit * count + item == block) & (item < count)
-    take_start = (unit * count + item - count == block) & (item >= count)
-    take_end = take_end.astype(F32)
-    take_start = take_start.astype(F32)
-    op = op_ref[...]
-    shift = jnp.zeros((blocks, means_ref.shape[1]), F32)
-    for s in range(1, slices - 1):
-        jump = dot(take_end, means_ref[(s - 1) * per : s * per], precision=HIGH) - dot(
-            take_start, means_ref[s * per : (s + 1) * per], precision=HIGH
+    take_end = ((unit * count + item == block) & (item < count)).astype(F32)
+    take_start = ((unit * count + item - count == block) & (item >= count)).astype(F32)
+    power = (iota((8, n), 1) == me * count + iota((8, n), 0)).astype(F32)
+    none = jnp.zeros_like(power)
+    weight = [none] * slices
+    for s in reversed(range(1, slices - 1)):
+        power = jnp.where(s < here, dot(power, m, precision=HIGH), power)
+        weight[s] = jnp.where(s < here, power, none)
+    for s in range(slices):
+        after = weight[s + 1] if s + 1 < slices else none
+        out_ref[:, s * per : (s + 1) * per] = dot(after, take_end, precision=HIGH) - dot(
+            weight[s], take_start, precision=HIGH
         )
-        shift = jnp.where(s < here, dot(op, shift + jump, precision=HIGH), shift)
-    chosen = (iota((8, blocks), 1) == me * count + iota((8, blocks), 0)).astype(F32)
-    mine = dot(chosen, shift, precision=HIGH)
-    later = here > 0
+
+
+def correct(count, means_ref, op_ref, previous_ref, start_ref, out_hbm, out_ref, sems):
+    later = lax.axis_index("cuts") > 0
+    mine = dot(op_ref[...], means_ref[...], precision=HIGH)
+    copies = []
     for i in range(count):
         out_ref[i] = jnp.where(later, previous_ref[i] + mine[i : i + 1], start_ref[i])
+        copies.append(pltpu.make_async_copy(out_ref.at[i], out_hbm.at[i], sems.at[i]))
+        copies[i].start()
+    for copy in copies:
+        copy.wait()
 
 
 def exchange(first, second):
-    size = lax.axis_size("sub")
+    size, slices = lax.axis_size("sub"), lax.axis_size("cuts")
     pairs = [(i, i ^ 1) for i in range(size)]
-    other = [(i, (i + (1 if i % 2 else -1)) % size) for i in range(size)]
-    far = lax.ppermute(second, "sub", other)
+    other = []
+    for c in range(slices):
+        for i in range(size):
+            j = i + (1 if i % 2 else -1)
+            d = c
+            if not 0 <= j < size:
+                d, j = (c ^ 1 if c ^ 1 < slices else c), i
+            other.append((c * size + i, d * size + j))
+    far = lax.ppermute(second, ("cuts", "sub"), other)
     near = lax.ppermute(first, "sub", pairs)
     return near, far
 
@@ -308,12 +356,15 @@
             opening,
             opening,
         ],
-        (start, source, block_inverse, face_map, transmissibility),
+        [pltpu.with_memory_space_constraint(a, pltpu.HBM) for a in (start, source, block_inverse, face_map, transmissibility)],
+        stay=range(5),
+        scratch=[pltpu.VMEM(a.shape, a.dtype) for a in (start, source, block_inverse, face_map, transmissibility)]
+        + [pltpu.SemaphoreType.DMA((2 + 3 * count,))],
     )
     blocks = partner.shape[0]
     (op,) = call(
-        coarse_operator,
-        [sds((blocks, blocks), F32)],
+        functools.partial(coarse_operator, count, slices),
+        [sds((8, slices * sub * 2 * count), F32)],
         (
             partner.reshape(1, blocks),
             partner.reshape(blocks, 1),
@@ -322,7 +373,13 @@
         ),
     )
     near = near_link = None
+    ring = [(i, (i + 1) % slices) for i in range(slices)]
     for step in range(FINE_STEPS):
+        if step < FINE_STEPS - 1:
+            (base,) = call(functools.partial(inner_base, count), [rhs_shape], (rhs, rm))
+        else:
+            (base,) = call(functools.partial(end_base, count), [rhs_shape], (rhs, rm, y))
+            previous_base = lax.ppermute(base, "cuts", ring)
         for turn in range(0, SWEEPS, 2):
             first, second = exchange(first, second)
             common = (first, second, ff, y, rhs, link, faces)
@@ -341,18 +398,25 @@
                 faces, first, second, rhs, y = call(
                     functools.partial(step_window, count),
                     [faces_shape, message, message, rhs_shape, faces_shape],
-                    common + (near, near_link, fm, rf, rm, wells),
+                    common + (near, near_link, fm, rf, base, wells),
                 )
             else:
-                end, means = call(
+                vector, means = call(
                     functools.partial(last_window, count),
-                    [rhs_shape, sds((slices * sub * 2 * count, scenarios), F32)],
-                    common + (near, near_link, rf, rm, mean),
+                    [faces_shape, sds((slices * sub * 2 * count, scenarios), F32)],
+                    common + (near, near_link, rf, base, mean),
                 )
-    previous = lax.ppermute(end, "cuts", [(i, (i + 1) % slices) for i in range(slices)])
+    previous_vector = lax.ppermute(vector, "cuts", ring)
     means = lax.all_to_all(means, ("cuts", "sub"), 0, 0, tiled=True)
+    (previous,) = call(
+        functools.partial(previous_end, count), [rhs_shape], (previous_base, previous_vector, ff, rf)
+    )
     (result,) = call(
-        functools.partial(correct, count, slices), [rhs_shape], (means, op, previous, start)
+        functools.partial(correct, count),
+        [rhs_shape],
+        (means, op, previous, start),
+        stay_out=(0,),
+        scratch=[pltpu.VMEM(rhs_shape.shape, F32), pltpu.SemaphoreType.DMA((count,))],
     )
     return result[None]
 

time: 97.6 us -> 86.8 us (0.89)
  waiting for transfers between devices: 41.1 us -> 33.6 us
  local copies, waits for them, and re-layouts: 4.76 us -> 1.47 us
  Pallas kernels: 11.7 us -> 14.2 us
  starting transfers between devices: 39.5 us -> 37.1 us
    ppermute x9 -> x10, starting transfers between devices: 28.3 us -> 0.58 us  [the longest x1 0.56 us: on_device(): previous_base = lax.ppermute(base, 'cuts', ring)]
    ppermute x8, starting transfers between devices: 6.13 us -> 27.4 us  [exchange(): near = lax.ppermute(first, 'sub', pairs)]
    ppermute x9 -> x10, waiting for transfers between devices: 19.3 us -> 0.04 us  [the longest x8 0.02 us: exchange(): far = lax.ppermute(second, ('cuts', 'sub'), other)]
    ppermute x8, waiting for transfers between devices: 16.8 us -> 30.7 us  [exchange(): near = lax.ppermute(first, 'sub', pairs)]
    all_to_all x1, starting transfers between devices: 5.06 us -> 9.19 us  [on_device(): means = lax.all_to_all(means, ('cuts', 'sub'), 0, 0, tiled=True)]
    unnamed x16 -> x6, local copies, waits for them, and re-layouts: 4.59 us -> 1.31 us
    pallas_call x11 -> x16, Pallas kernels: 11.7 us -> 14.2 us  [call(): pl.pallas_call(body, out_shape=out_shape, in_specs=[hbm if k in stay else...]
    all_to_all x1, waiting for transfers between devices: 5.04 us -> 2.92 us  [on_device(): means = lax.all_to_all(means, ('cuts', 'sub'), 0, 0, tiled=True)]
  transfers between devices with their start and end apart: 18 -> 19, of which waited for: 16 -> 9; matrix products, arithmetic and copies ran while one was open for 0% -> 0% of each run, Pallas kernels for 2% -> 7%
where the time goes in v1:
time: 86.8 us; the launch traced here: 86.6 us
  starting transfers between devices  37.1 us (43%)
  waiting for transfers between devices  33.6 us (39%)
  Pallas kernels  14.2 us (16%)
  local copies, waits for them, and re-layouts  1.47 us (2%)
    ppermute x8, waiting for transfers between devices, exchange(): near = lax.ppermute(first, 'sub', pairs)  30.7 us
    ppermute x8, starting transfers between devices, exchange(): near = lax.ppermute(first, 'sub', pairs)  27.4 us
    pallas_call x16, Pallas kernels, call(): pl.pallas_call(body, out_shape=out_shape, in_specs=[hbm if k in stay else...  14.2 us
    all_to_all x1, starting transfers between devices, on_device(): means = lax.all_to_all(means, ('cuts', 'sub'), 0, 0, tiled=True)  9.19 us
    all_to_all x1, waiting for transfers between devices, on_device(): means = lax.all_to_all(means, ('cuts', 'sub'), 0, 0, tiled=True)  2.92 us
  transfers between devices with their start and end apart: 19, of which 9 were waited for; matrix products, arithmetic and copies ran while one was open for 0% of the time, Pallas kernels for 7%

profile of v1, /device:TPU:0, one launch (start us, length us, event | category | flops | bytes accessed | tf_op | source)
XLA Modules:
  0.0 86.6 jit_solution(16820282006520663974)
XLA Ops:
  0.0 2.4 %shard_map.73 = (bf16[2,256,256]{2,1,0:T(8,128)(2,1)S(1)}, bf16[2,256,256]{2,1,0:T(8,128)(2,1)S(1)}, bf16[2,512,256]{2,1,0:T(8,128)(2,1)S(1)}, bf16[2,512,256]{2...) custom-call(f32[2,512,128]{2,1,0:T(8,128)} %bitcast.8, ...), custom_call_target="tpu_custom_call" | custom-call | flops 268435456 | bytes 5649408 | tf_op jit(solution)/shard_map/pallas_call | solution.py:33
  2.4 3.0 %collective-permute-start = (f32[392,128]{1,0:T(8,128)S(1)}, f32[392,128]{1,0:T(8,128)S(1)}, u32[]{:S(2)}, u32[]{:S(2)}) collective-permute-start(f32[392,128]{1,0:T(8,128)S(1)} %get-tuple-element.48), channel_id=1, source_target_pairs={{0,1},{1,0},{2,3},{3,2},{4,5},{5,4},{6,7},{7,6},{8,9},{9,8},{10,11... | collective-permute-start | bytes 602120 | tf_op jit(solution)/shard_map/ppermute | solution.py:328
  5.5 8.5 %collective-permute-done.refs_0_ = f32[392,128]{1,0:T(8,128)S(1)} collective-permute-done((f32[392,128]{1,0:T(8,128)S(1)}, f32[392,128]{1,0:T(8,128)S(1)}, u32[]{:S(2)}, u32[]{:S(2)}) %collective-permute-start) | collective-permute-done | bytes 200736 | tf_op jit(solution)/shard_map/ppermute | solution.py:328
  14.0 0.7 shard_map.74
  14.7 2.5 %collective-permute-start.2 = (f32[256,128]{1,0:T(8,128)S(1)}, f32[256,128]{1,0:T(8,128)S(1)}, u32[]{:S(2)}, u32[]{:S(2)}) collective-permute-start(f32[256,128]{1,0:T(8,128)S(1)} %get-tuple-element.55), channel_id=1, source_target_pairs={{0,1},{1,0},{2,3},{3,2},{4,5},{5,4},{6,7},{7,6},{8,9},{9,8},{10,11... | collective-permute-start | bytes 393224 | tf_op jit(solution)/shard_map/ppermute | solution.py:328
  17.5 4.4 %collective-permute-done.2.first_ref = f32[256,128]{1,0:T(8,128)S(1)} collective-permute-done((f32[256,128]{1,0:T(8,128)S(1)}, f32[256,128]{1,0:T(8,128)S(1)}, u32[]{:S(2)}, u32[]{:S(2)}) %collective-permute-start.2) | collective-permute-done | bytes 131104 | tf_op jit(solution)/shard_map/ppermute | solution.py:328
  21.9 1.1 %shard_map.76 = (f32[2,256,128]{2,1,0:T(8,128)S(1)}, f32[256,128]{1,0:T(8,128)S(1)}, f32[256,128]{1,0:T(8,128)S(1)}, f32[2,512,128]{2,1,0:T(8,128)S(1)}, f32[2,256,128]{2,1,0:T(8,128)S(1)}) custom-call(f32[256,128]{1,0:T(8,128)S(1)} %collective-permute-done.2.first_ref, f32[256,128]{1,0:T(8,128)S(1)} %collective-permute-done.3.second_ref, ...), custom_call_target="tpu_custom_call" | custom-call | flops 268435456 | bytes 5177344 | tf_op jit(solution)/shard_map/pallas_call | solution.py:33
  23.1 2.5 %collective-permute-start.4 = (f32[256,128]{1,0:T(8,128)S(1)}, f32[256,128]{1,0:T(8,128)S(1)}, u32[]{:S(2)}, u32[]{:S(2)}) collective-permute-start(f32[256,128]{1,0:T(8,128)S(1)} %get-tuple-element.64), channel_id=1, source_target_pairs={{0,1},{1,0},{2,3},{3,2},{4,5},{5,4},{6,7},{7,6},{8,9},{9,8},{10,11... | collective-permute-start | bytes 393224 | tf_op jit(solution)/shard_map/ppermute | solution.py:328
  25.6 4.0 %collective-permute-done.4.refs_0_ = f32[256,128]{1,0:T(8,128)S(1)} collective-permute-done((f32[256,128]{1,0:T(8,128)S(1)}, f32[256,128]{1,0:T(8,128)S(1)}, u32[]{:S(2)}, u32[]{:S(2)}) %collective-permute-start.4) | collective-permute-done | bytes 131104 | tf_op jit(solution)/shard_map/ppermute | solution.py:328
  29.7 0.6 shard_map.77
  30.2 2.7 %collective-permute-start.6 = (f32[256,128]{1,0:T(8,128)S(1)}, f32[256,128]{1,0:T(8,128)S(1)}, u32[]{:S(2)}, u32[]{:S(2)}) collective-permute-start(f32[256,128]{1,0:T(8,128)S(1)} %get-tuple-element.69), channel_id=1, source_target_pairs={{0,1},{1,0},{2,3},{3,2},{4,5},{5,4},{6,7},{7,6},{8,9},{9,8},{10,11... | collective-permute-start | bytes 393224 | tf_op jit(solution)/shard_map/ppermute | solution.py:328
  33.2 2.6 %collective-permute-done.6.first_ref = f32[256,128]{1,0:T(8,128)S(1)} collective-permute-done((f32[256,128]{1,0:T(8,128)S(1)}, f32[256,128]{1,0:T(8,128)S(1)}, u32[]{:S(2)}, u32[]{:S(2)}) %collective-permute-start.6) | collective-permute-done | bytes 131104 | tf_op jit(solution)/shard_map/ppermute | solution.py:328
  35.9 1.1 %shard_map.79 = (f32[2,256,128]{2,1,0:T(8,128)S(1)}, f32[256,128]{1,0:T(8,128)S(1)}, f32[256,128]{1,0:T(8,128)S(1)}, f32[2,512,128]{2,1,0:T(8,128)S(1)}, f32[2,256,128]{2,1,0:T(8,128)S(1)}) custom-call(f32[256,128]{1,0:T(8,128)S(1)} %collective-permute-done.6.first_ref, f32[256,128]{1,0:T(8,128)S(1)} %collective-permute-done.7.second_ref, ...), custom_call_target="tpu_custom_call" | custom-call | flops 268435456 | bytes 5177344 | tf_op jit(solution)/shard_map/pallas_call | solution.py:33
  37.0 3.6 %collective-permute-start.8 = (f32[256,128]{1,0:T(8,128)S(1)}, f32[256,128]{1,0:T(8,128)S(1)}, u32[]{:S(2)}, u32[]{:S(2)}) collective-permute-start(f32[256,128]{1,0:T(8,128)S(1)} %get-tuple-element.72), channel_id=1, source_target_pairs={{0,1},{1,0},{2,3},{3,2},{4,5},{5,4},{6,7},{7,6},{8,9},{9,8},{10,11... | collective-permute-start | bytes 393224 | tf_op jit(solution)/shard_map/ppermute | solution.py:328
  40.6 2.9 %collective-permute-done.8.refs_0_ = f32[256,128]{1,0:T(8,128)S(1)} collective-permute-done((f32[256,128]{1,0:T(8,128)S(1)}, f32[256,128]{1,0:T(8,128)S(1)}, u32[]{:S(2)}, u32[]{:S(2)}) %collective-permute-start.8) | collective-permute-done | bytes 131104 | tf_op jit(solution)/shard_map/ppermute | solution.py:328
  43.6 0.6 shard_map.80
  44.1 4.1 %collective-permute-start.10 = (f32[256,128]{1,0:T(8,128)S(1)}, f32[256,128]{1,0:T(8,128)S(1)}, u32[]{:S(2)}, u32[]{:S(2)}) collective-permute-start(f32[256,128]{1,0:T(8,128)S(1)} %get-tuple-element.77), channel_id=1, source_target_pairs={{0,1},{1,0},{2,3},{3,2},{4,5},{5,4},{6,7},{7,6},{8,9},{9,8},{10,11... | collective-permute-start | bytes 393224 | tf_op jit(solution)/shard_map/ppermute | solution.py:328
  48.6 2.6 %collective-permute-done.10.first_ref = f32[256,128]{1,0:T(8,128)S(1)} collective-permute-done((f32[256,128]{1,0:T(8,128)S(1)}, f32[256,128]{1,0:T(8,128)S(1)}, u32[]{:S(2)}, u32[]{:S(2)}) %collective-permute-start.10) | collective-permute-done | bytes 131104 | tf_op jit(solution)/shard_map/ppermute | solution.py:328
  51.2 1.1 %shard_map.82 = (f32[2,256,128]{2,1,0:T(8,128)S(1)}, f32[256,128]{1,0:T(8,128)S(1)}, f32[256,128]{1,0:T(8,128)S(1)}, f32[2,512,128]{2,1,0:T(8,128)S(1)}, f32[2,256,128]{2,1,0:T(8,128)S(1)}) custom-call(f32[256,128]{1,0:T(8,128)S(1)} %collective-permute-done.10.first_ref, f32[256,128]{1,0:T(8,128)S(1)} %collective-permute-done.11.second_ref, ...), custom_call_target="tpu_custom_call" | custom-call | flops 268435456 | bytes 5177344 | tf_op jit(solution)/shard_map/pallas_call | solution.py:33
  52.3 4.1 %collective-permute-start.12 = (f32[256,128]{1,0:T(8,128)S(1)}, f32[256,128]{1,0:T(8,128)S(1)}, u32[]{:S(2)}, u32[]{:S(2)}) collective-permute-start(f32[256,128]{1,0:T(8,128)S(1)} %get-tuple-element.80), channel_id=1, source_target_pairs={{0,1},{1,0},{2,3},{3,2},{4,5},{5,4},{6,7},{7,6},{8,9},{9,8},{10,11... | collective-permute-start | bytes 393224 | tf_op jit(solution)/shard_map/ppermute | solution.py:328
  56.6 0.6 collective-permute-start.16
  57.2 2.2 %collective-permute-done.12.refs_0_ = f32[256,128]{1,0:T(8,128)S(1)} collective-permute-done((f32[256,128]{1,0:T(8,128)S(1)}, f32[256,128]{1,0:T(8,128)S(1)}, u32[]{:S(2)}, u32[]{:S(2)}) %collective-permute-start.12) | collective-permute-done | bytes 131104 | tf_op jit(solution)/shard_map/ppermute | solution.py:328
  59.4 0.6 shard_map.83
  59.9 4.8 %collective-permute-start.14 = (f32[256,128]{1,0:T(8,128)S(1)}, f32[256,128]{1,0:T(8,128)S(1)}, u32[]{:S(2)}, u32[]{:S(2)}) collective-permute-start(f32[256,128]{1,0:T(8,128)S(1)} %get-tuple-element.85), channel_id=1, source_target_pairs={{0,1},{1,0},{2,3},{3,2},{4,5},{5,4},{6,7},{7,6},{8,9},{9,8},{10,11... | collective-permute-start | bytes 393224 | tf_op jit(solution)/shard_map/ppermute | solution.py:328
  64.7 3.2 %collective-permute-done.14.first_ref = f32[256,128]{1,0:T(8,128)S(1)} collective-permute-done((f32[256,128]{1,0:T(8,128)S(1)}, f32[256,128]{1,0:T(8,128)S(1)}, u32[]{:S(2)}, u32[]{:S(2)}) %collective-permute-start.14) | collective-permute-done | bytes 131104 | tf_op jit(solution)/shard_map/ppermute | solution.py:328
  67.9 1.2 %shard_map.85 = (f32[2,256,128]{2,1,0:T(8,128)S(1)}, f32[128,128]{1,0:T(8,128)}) custom-call(f32[256,128]{1,0:T(8,128)S(1)} %collective-permute-done.14.first_ref, f32[256,128]{1,0:T(8,128)S(1)} %collective-permute-done.15.second_ref, bf16[2,256,256]{2,1,0:T(8,128)(2,1)S(1)} %get-tuple-element.50.refs_2_.ff_ref, ...), custom_call_target="tpu_custom_call" | custom-call | flops 268435456 | bytes 3408896 | tf_op jit(solution)/shard_map/pallas_call | solution.py:33
  69.1 9.2 %all-to-all-start = ((f32[32,4,128]{2,1,0:T(4,128)}), f32[32,4,128]{2,1,0:T(4,128)S(1)}, u32[]{:S(2)}, u32[]{:S(2)}) async-start(f32[32,4,128]{2,1,0:T(4,128)} %bitcast.1), calls=%async_computation | async-start | bytes 131072 | tf_op jit(solution)/shard_map/all_to_all | solution.py:410
  78.3 0.6 copy-done.1
  79.1 0.7 copy-done.2
  79.8 2.6 %shard_map.86.op_ref = f32[8,128]{1,0:T(8,128)S(1)} custom-call(s32[1,16]{1,0:T(1,128)S(1)} %bitcast.12, s32[16,1]{1,0:T(8,128)S(1)} %copy.8.partner_col, f32[1,16]{1,0:T(1,128)S(1)} %bitcast.14, f32[16,1]{1,0:T(8,128)S(1)} %copy.9.cond_col), custom_call_target="tpu_custom_call" | custom-call | flops 268435456 | bytes 4352 | tf_op jit(solution)/shard_map/pallas_call | solution.py:33
  82.7 2.9 %all-to-all-done = f32[32,4,128]{2,1,0:T(4,128)S(1)} async-done(((f32[32,4,128]{2,1,0:T(4,128)}), f32[32,4,128]{2,1,0:T(4,128)S(1)}, u32[]{:S(2)}, u32[]{:S(2)}) %all-to-all-start) | async-done | bytes 65568 | tf_op jit(solution)/shard_map/all_to_all | solution.py:410
  85.6 1.0 %shard_map.88 = f32[2,512,128]{2,1,0:T(8,128)} custom-call(f32[128,128]{1,0:T(8,128)S(1)} %bitcast.10, f32[8,128]{1,0:T(8,128)S(1)} %shard_map.86.op_ref, f32[2,512,128]{2,1,0:T(8,128)S(1)} %shard_map.87.previous_ref, f32[2,512,128]{2,1,0:T(8,128)S(1)} %bitcast.9), custom_call_target="tpu_custom_call" | custom-call | flops 268435456 | bytes 1642496 | tf_op jit(solution)/shard_map/pallas_call | solution.py:33
  (30 shorter events, 1.6 us)
Async XLA Ops:
  2.4 11.6 %collective-permute-start = (f32[392,128]{1,0:T(8,128)S(1)}, f32[392,128]{1,0:T(8,128)S(1)}, u32[]{:S(2)}, u32[]{:S(2)}) collective-permute-start(f32[392,128]{1,0:T(8,128)S(1)} %get-tuple-element.48), channel_id=1, source_target_pairs={{0,1},{1,0},{2,3},{3,2},{4,5},{5,4},{6,7},{7,6},{8,9},{9,8},{10,11... | collective-permute-start | bytes 602120 | tf_op jit(solution)/shard_map/ppermute | solution.py:328
  5.5 8.6 %collective-permute-start.1 = (f32[392,128]{1,0:T(8,128)S(1)}, f32[392,128]{1,0:T(8,128)S(1)}, u32[]{:S(2)}, u32[]{:S(2)}) collective-permute-start(f32[392,128]{1,0:T(8,128)S(1)} %get-tuple-element.49), channel_id=1, source_target_pairs={{0,8},{1,2},{2,1},{3,4},{4,3},{5,6},{6,5},{7,15},{8,0},{9,10},{10,... | collective-permute-start | bytes 602120 | tf_op jit(solution)/shard_map/ppermute | solution.py:327
  14.7 7.3 %collective-permute-start.2 = (f32[256,128]{1,0:T(8,128)S(1)}, f32[256,128]{1,0:T(8,128)S(1)}, u32[]{:S(2)}, u32[]{:S(2)}) collective-permute-start(f32[256,128]{1,0:T(8,128)S(1)} %get-tuple-element.55), channel_id=1, source_target_pairs={{0,1},{1,0},{2,3},{3,2},{4,5},{5,4},{6,7},{7,6},{8,9},{9,8},{10,11... | collective-permute-start | bytes 393224 | tf_op jit(solution)/shard_map/ppermute | solution.py:328
  17.2 4.7 %collective-permute-start.3 = (f32[256,128]{1,0:T(8,128)S(1)}, f32[256,128]{1,0:T(8,128)S(1)}, u32[]{:S(2)}, u32[]{:S(2)}) collective-permute-start(f32[256,128]{1,0:T(8,128)S(1)} %get-tuple-element.56), channel_id=1, source_target_pairs={{0,8},{1,2},{2,1},{3,4},{4,3},{5,6},{6,5},{7,15},{8,0},{9,10},{10,... | collective-permute-start | bytes 393224 | tf_op jit(solution)/shard_map/ppermute | solution.py:327
  23.1 6.6 %collective-permute-start.4 = (f32[256,128]{1,0:T(8,128)S(1)}, f32[256,128]{1,0:T(8,128)S(1)}, u32[]{:S(2)}, u32[]{:S(2)}) collective-permute-start(f32[256,128]{1,0:T(8,128)S(1)} %get-tuple-element.64), channel_id=1, source_target_pairs={{0,1},{1,0},{2,3},{3,2},{4,5},{5,4},{6,7},{7,6},{8,9},{9,8},{10,11... | collective-permute-start | bytes 393224 | tf_op jit(solution)/shard_map/ppermute | solution.py:328
  25.6 4.0 %collective-permute-start.5 = (f32[256,128]{1,0:T(8,128)S(1)}, f32[256,128]{1,0:T(8,128)S(1)}, u32[]{:S(2)}, u32[]{:S(2)}) collective-permute-start(f32[256,128]{1,0:T(8,128)S(1)} %get-tuple-element.65), channel_id=1, source_target_pairs={{0,8},{1,2},{2,1},{3,4},{4,3},{5,6},{6,5},{7,15},{8,0},{9,10},{10,... | collective-permute-start | bytes 393224 | tf_op jit(solution)/shard_map/ppermute | solution.py:327
  30.2 5.6 %collective-permute-start.6 = (f32[256,128]{1,0:T(8,128)S(1)}, f32[256,128]{1,0:T(8,128)S(1)}, u32[]{:S(2)}, u32[]{:S(2)}) collective-permute-start(f32[256,128]{1,0:T(8,128)S(1)} %get-tuple-element.69), channel_id=1, source_target_pairs={{0,1},{1,0},{2,3},{3,2},{4,5},{5,4},{6,7},{7,6},{8,9},{9,8},{10,11... | collective-permute-start | bytes 393224 | tf_op jit(solution)/shard_map/ppermute | solution.py:328
  32.9 3.0 %collective-permute-start.7 = (f32[256,128]{1,0:T(8,128)S(1)}, f32[256,128]{1,0:T(8,128)S(1)}, u32[]{:S(2)}, u32[]{:S(2)}) collective-permute-start(f32[256,128]{1,0:T(8,128)S(1)} %get-tuple-element.70), channel_id=1, source_target_pairs={{0,8},{1,2},{2,1},{3,4},{4,3},{5,6},{6,5},{7,15},{8,0},{9,10},{10,... | collective-permute-start | bytes 393224 | tf_op jit(solution)/shard_map/ppermute | solution.py:327
  37.0 6.6 %collective-permute-start.8 = (f32[256,128]{1,0:T(8,128)S(1)}, f32[256,128]{1,0:T(8,128)S(1)}, u32[]{:S(2)}, u32[]{:S(2)}) collective-permute-start(f32[256,128]{1,0:T(8,128)S(1)} %get-tuple-element.72), channel_id=1, source_target_pairs={{0,1},{1,0},{2,3},{3,2},{4,5},{5,4},{6,7},{7,6},{8,9},{9,8},{10,11... | collective-permute-start | bytes 393224 | tf_op jit(solution)/shard_map/ppermute | solution.py:328
  40.6 3.0 %collective-permute-start.9 = (f32[256,128]{1,0:T(8,128)S(1)}, f32[256,128]{1,0:T(8,128)S(1)}, u32[]{:S(2)}, u32[]{:S(2)}) collective-permute-start(f32[256,128]{1,0:T(8,128)S(1)} %get-tuple-element.73), channel_id=1, source_target_pairs={{0,8},{1,2},{2,1},{3,4},{4,3},{5,6},{6,5},{7,15},{8,0},{9,10},{10,... | collective-permute-start | bytes 393224 | tf_op jit(solution)/shard_map/ppermute | solution.py:327
  44.1 7.1 %collective-permute-start.10 = (f32[256,128]{1,0:T(8,128)S(1)}, f32[256,128]{1,0:T(8,128)S(1)}, u32[]{:S(2)}, u32[]{:S(2)}) collective-permute-start(f32[256,128]{1,0:T(8,128)S(1)} %get-tuple-element.77), channel_id=1, source_target_pairs={{0,1},{1,0},{2,3},{3,2},{4,5},{5,4},{6,7},{7,6},{8,9},{9,8},{10,11... | collective-permute-start | bytes 393224 | tf_op jit(solution)/shard_map/ppermute | solution.py:328
  48.3 3.0 %collective-permute-start.11 = (f32[256,128]{1,0:T(8,128)S(1)}, f32[256,128]{1,0:T(8,128)S(1)}, u32[]{:S(2)}, u32[]{:S(2)}) collective-permute-start(f32[256,128]{1,0:T(8,128)S(1)} %get-tuple-element.78), channel_id=1, source_target_pairs={{0,8},{1,2},{2,1},{3,4},{4,3},{5,6},{6,5},{7,15},{8,0},{9,10},{10,... | collective-permute-start | bytes 393224 | tf_op jit(solution)/shard_map/ppermute | solution.py:327
  52.3 7.0 %collective-permute-start.12 = (f32[256,128]{1,0:T(8,128)S(1)}, f32[256,128]{1,0:T(8,128)S(1)}, u32[]{:S(2)}, u32[]{:S(2)}) collective-permute-start(f32[256,128]{1,0:T(8,128)S(1)} %get-tuple-element.80), channel_id=1, source_target_pairs={{0,1},{1,0},{2,3},{3,2},{4,5},{5,4},{6,7},{7,6},{8,9},{9,8},{10,11... | collective-permute-start | bytes 393224 | tf_op jit(solution)/shard_map/ppermute | solution.py:328
  56.4 3.0 %collective-permute-start.13 = (f32[256,128]{1,0:T(8,128)S(1)}, f32[256,128]{1,0:T(8,128)S(1)}, u32[]{:S(2)}, u32[]{:S(2)}) collective-permute-start(f32[256,128]{1,0:T(8,128)S(1)} %get-tuple-element.81), channel_id=1, source_target_pairs={{0,8},{1,2},{2,1},{3,4},{4,3},{5,6},{6,5},{7,15},{8,0},{9,10},{10,... | collective-permute-start | bytes 393224 | tf_op jit(solution)/shard_map/ppermute | solution.py:327
  56.6 25.7 %collective-permute-start.16 = (f32[2,512,128]{2,1,0:T(8,128)S(1)}, f32[2,512,128]{2,1,0:T(8,128)S(1)}, u32[]{:S(2)}, u32[]{:S(2)}) collective-permute-start(f32[2,512,128]{2,1,0:T(8,128)S(1)} %shard_map.84.base_ref), channel_id=1, source_target_pairs={{0,8},{8,16},{16,24},{24,0},{1,9},{9,17},{17,25},{25,1},{2,10},{10... | collective-permute-start | bytes 1572872 | tf_op jit(solution)/shard_map/ppermute | solution.py:382
  59.9 8.0 %collective-permute-start.14 = (f32[256,128]{1,0:T(8,128)S(1)}, f32[256,128]{1,0:T(8,128)S(1)}, u32[]{:S(2)}, u32[]{:S(2)}) collective-permute-start(f32[256,128]{1,0:T(8,128)S(1)} %get-tuple-element.85), channel_id=1, source_target_pairs={{0,1},{1,0},{2,3},{3,2},{4,5},{5,4},{6,7},{7,6},{8,9},{9,8},{10,11... | collective-permute-start | bytes 393224 | tf_op jit(solution)/shard_map/ppermute | solution.py:328
  64.7 3.3 %collective-permute-start.15 = (f32[256,128]{1,0:T(8,128)S(1)}, f32[256,128]{1,0:T(8,128)S(1)}, u32[]{:S(2)}, u32[]{:S(2)}) collective-permute-start(f32[256,128]{1,0:T(8,128)S(1)} %get-tuple-element.86), channel_id=1, source_target_pairs={{0,8},{1,2},{2,1},{3,4},{4,3},{5,6},{6,5},{7,15},{8,0},{9,10},{10,... | collective-permute-start | bytes 393224 | tf_op jit(solution)/shard_map/ppermute | solution.py:327
  69.1 13.2 %collective-permute-start.17 = (f32[2,256,128]{2,1,0:T(8,128)S(1)}, f32[2,256,128]{2,1,0:T(8,128)S(1)}, u32[]{:S(2)}, u32[]{:S(2)}) collective-permute-start(f32[2,256,128]{2,1,0:T(8,128)S(1)} %get-tuple-element.90), channel_id=1, source_target_pairs={{0,8},{8,16},{16,24},{24,0},{1,9},{9,17},{17,25},{25,1},{2,10},{10... | collective-permute-start | bytes 786440 | tf_op jit(solution)/shard_map/ppermute | solution.py:409
  69.1 16.5 %all-to-all-start = ((f32[32,4,128]{2,1,0:T(4,128)}), f32[32,4,128]{2,1,0:T(4,128)S(1)}, u32[]{:S(2)}, u32[]{:S(2)}) async-start(f32[32,4,128]{2,1,0:T(4,128)} %bitcast.1), calls=%async_computation | async-start | bytes 131072 | tf_op jit(solution)/shard_map/all_to_all | solution.py:410
  78.3 0.7 copy-start.1
  79.1 0.7 copy-start.2
  82.3 3.2 %copy-start = (f32[1,2,512,128]{3,2,1,0:T(8,128)S(1)}, f32[1,2,512,128]{3,2,1,0:T(8,128)}, u32[]{:S(2)}) copy-start(f32[1,2,512,128]{3,2,1,0:T(8,128)} %param.7) | copy-start | bytes 1572868

commit v2 on v1

v2 whole, which is shorter than its diff:
```python
import functools

import jax
import jax.numpy as jnp
from jax import lax
from jax.experimental import pallas as pl
from jax.experimental.pallas import tpu as pltpu
from jax.sharding import PartitionSpec as P


FINE_STEPS = 4
SWEEPS = 4
F32 = jnp.float32
BF16 = jnp.bfloat16
HIGH = lax.Precision.HIGHEST


def dot(a, b, dims=((1,), (0,)), precision=None):
    return lax.dot_general(a, b, (dims, ((), ())), precision=precision, preferred_element_type=F32)


def transpose(x):
    return jnp.transpose(x, (1, 0))


def iota(shape, axis):
    return lax.broadcasted_iota(jnp.int32, shape, axis)


def call(body, out_shape, args, flops=1 << 28, stay=(), stay_out=(), scratch=()):
    size = sum(a.size * a.dtype.itemsize for a in list(args) + list(out_shape))
    vmem = pl.BlockSpec(memory_space=pltpu.VMEM)
    hbm = pl.BlockSpec(memory_space=pltpu.HBM)
    return pl.pallas_call(
        body,
        out_shape=out_shape,
        in_specs=[hbm if k in stay else vmem for k in range(len(args))],
        out_specs=[hbm if k in stay_out else vmem for k in range(len(out_shape))],
        scratch_shapes=list(scratch),
        compiler_params=pltpu.CompilerParams(vmem_limit_bytes=24 << 20),
        cost_estimate=pl.CostEstimate(flops=flops, bytes_accessed=size, transcendentals=0),
    )(*args)


def face_vector(i, count, rhs_ref, link_ref, low, up, below, above):
    face = low[0].shape[0]
    under = below if i == 0 else up[i - 1]
    over = above if i == count - 1 else low[i + 1]
    v_low = rhs_ref[i, :face] + link_ref[2 * i] * under
    v_up = rhs_ref[i, face : 2 * face] + link_ref[2 * i + 1] * over
    return v_low.astype(BF16), v_up.astype(BF16)


def face_sweep(count, ff_ref, y_ref, rhs_ref, link_ref, low, up, below, above):
    face = low[0].shape[0]
    vectors, new_low, new_up = [], [], []
    for i in range(count):
        v = jnp.concatenate(face_vector(i, count, rhs_ref, link_ref, low, up, below, above), axis=0)
        x = y_ref[i] + dot(ff_ref[i], v)
        vectors.append(v)
        new_low.append(x[:face])
        new_up.append(x[face:])
    return vectors, new_low, new_up


def outgoing(count, ff_ref, y_ref, rhs_ref, link_ref, low, up):
    face = low[0].shape[0]
    last = count - 1
    zero = jnp.zeros_like(low[0])
    v = jnp.concatenate(face_vector(last, count, rhs_ref, link_ref, low, up, zero, zero), axis=0)
    next_up = y_ref[last, face:] + dot(ff_ref[last, face:], v)
    v = jnp.concatenate(face_vector(0, count, rhs_ref, link_ref, low, up, zero, zero), axis=0)
    next_low = y_ref[0, :face] + dot(ff_ref[0, :face], v)
    return (up[last], next_up), (low[0], next_low)


def store_messages(upward, downward, first_ref, second_ref):
    even = lax.rem(lax.axis_index("sub"), 2) == 0
    at = 0
    for one, other in zip(upward, downward):
        rows = pl.ds(at, one.shape[0])
        first_ref[rows] = jnp.where(even, one, other)
        second_ref[rows] = jnp.where(even, other, one)
        at += one.shape[0]


def received(first_ref, second_ref, rows):
    even = lax.rem(lax.axis_index("sub"), 2) == 0
    first, second = first_ref[rows], second_ref[rows]
    return jnp.where(even, second, first), jnp.where(even, first, second)


def read_all(sources, targets, sems):
    copies = [pltpu.make_async_copy(a, b, sems.at[k]) for k, (a, b) in enumerate(zip(sources, targets))]
    for copy in copies:
        copy.start()
    return copies


def face_rows(side, face, width):
    return slice(0, face) if side == 0 else slice(width - face, width)


def permutation(i, side, map_ref):
    face = map_ref.shape[2]
    return iota((face, face), 0) == map_ref[i, side : side + 1, :]


def as_bf16(mask):
    return mask.astype(F32).astype(BF16)


def prepare(count, start_hbm, source_hbm, inverse_hbm, map_hbm, trans_hbm,
            rhs_ref, link_ref, faces_ref, first_ref, second_ref,
            start_ref, source_ref, low_ref, up_ref, map_ref, trans_ref, sems):
    width = start_ref.shape[1]
    face = map_ref.shape[2]
    last = count - 1
    copies = read_all(
        (map_hbm, trans_hbm, start_hbm, source_hbm,
         inverse_hbm.at[0, pl.ds(0, face)], inverse_hbm.at[last, pl.ds(width - face, face)]),
        (map_ref, trans_ref, start_ref, source_ref, low_ref, up_ref),
        sems,
    )
    me, size = lax.axis_index("sub"), lax.axis_size("sub")
    copies[0].wait()
    copies[1].wait()
    perms = []
    for i in range(count):
        for side in range(2):
            linked = permutation(i, side, map_ref)
            column = jnp.sum(
                jnp.where(linked, trans_ref[i, side : side + 1, :], 0.0), axis=1, keepdims=True
            )
            if i == 0 and side == 0:
                column = jnp.where(me == 0, 0.0, column)
            if i == last and side == 1:
                column = jnp.where(me == size - 1, 0.0, column)
            link_ref[2 * i + side] = jnp.broadcast_to(column, (face, start_ref.shape[2]))
            perms.append(as_bf16(linked))
    for copy in copies[2:]:
        copy.wait()
    low, up = [], []
    for i in range(count):
        for side in range(2):
            rows = face_rows(side, face, width)
            to = slice(side * face, (side + 1) * face)
            value = start_ref[i, rows]
            high = value.astype(BF16)
            rest = value - high.astype(F32)
            mid = rest.astype(BF16)
            tail = (rest - mid.astype(F32)).astype(BF16)
            perm = perms[2 * i + side]
            parts = dot(perm, jnp.concatenate([high, mid, tail, source_ref[i, rows]], axis=1))
            cut = value.shape[1]
            parts = [parts[:, k * cut : (k + 1) * cut] for k in range(4)]
            rhs_ref[i, to] = parts[0] + parts[1] + parts[2] + parts[3]
            faces_ref[i, to] = value
            (up if side else low).append(value)
    zero = jnp.zeros_like(low[0])
    inner = slice(face, width - face)
    ahead, operators = [], []
    for i, matrix, at in ((last, up_ref, 1), (0, low_ref, 0)):
        columns = [
            dot(matrix[:, face_rows(side, face, width)], perms[2 * i + side], ((1,), (1,))).astype(BF16)
            for side in range(2)
        ]
        middle = (start_ref[i, inner] + source_ref[i, inner].astype(F32)).astype(BF16)
        v = jnp.concatenate(face_vector(i, count, rhs_ref, link_ref, low, up, zero, zero), axis=0)
        ahead.append(dot(matrix[:, inner], middle) + dot(jnp.concatenate(columns, axis=1), v))
        operators.append(columns[at].astype(F32))
    upward = (up[last], ahead[0], operators[0], transpose(link_ref[2 * last + 1])[:8])
    downward = (low[0], ahead[1], operators[1], transpose(link_ref[0])[:8])
    store_messages(upward, downward, first_ref, second_ref)


def prepare_rest(count, start_hbm, source_hbm, inverse_hbm, map_hbm,
                 ff_ref, fm_ref, rf_ref, rm_ref, mid_ref, wells_ref, y_ref, mean_ref,
                 start_ref, source_ref, inverse_ref, map_ref, sems):
    for copy in read_all(
        (start_hbm, source_hbm, inverse_hbm, map_hbm), (start_ref, source_ref, inverse_ref, map_ref), sems
    ):
        copy.wait()
    width = start_ref.shape[1]
    face = map_ref.shape[2]
    inner = slice(face, width - face)
    for i in range(count):
        perms = [as_bf16(permutation(i, side, map_ref)) for side in range(2)]
        for side in range(2):
            to = slice(side * face, (side + 1) * face)
            rows = face_rows(side, face, width)
            columns = dot(inverse_ref[i, :, rows], perms[side], ((1,), (1,))).astype(BF16)
            ff_ref[i, :face, to] = columns[:face]
            ff_ref[i, face:, to] = columns[width - face :]
            rf_ref[i, 2 * face :, to] = columns[inner]
            wells_ref[i, to] = dot(perms[side], source_ref[i, rows])
            fm_ref[i, to] = inverse_ref[i, rows, inner]
        for side in range(2):
            to = slice(side * face, (side + 1) * face)
            rf_ref[i, to] = dot(perms[side], ff_ref[i, to]).astype(BF16)
            rm_ref[i, to] = dot(perms[side], fm_ref[i, to]).astype(BF16)
        rm_ref[i, 2 * face :] = inverse_ref[i, inner, inner]
        wells = source_ref[i, inner].astype(F32)
        mid_ref[i] = start_ref[i, inner] + wells
        wells_ref[i, 2 * face :] = wells
        mean_ref[i : i + 1] = jnp.sum(start_ref[i], axis=0, keepdims=True) / width
        y_ref[i] = dot(fm_ref[i], mid_ref[i].astype(BF16))


def load_faces(count, faces_ref):
    face = faces_ref.shape[1] // 2
    return [faces_ref[i, :face] for i in range(count)], [faces_ref[i, face:] for i in range(count)]


def window(count, first_ref, second_ref, ff_ref, y_ref, rhs_ref, link_ref, faces_ref, near_ref, near_link_ref):
    low, up = load_faces(count, faces_ref)
    face = low[0].shape[0]
    below, above = received(first_ref, second_ref, slice(0, face))
    next_below, next_above = received(first_ref, second_ref, slice(face, 2 * face))
    next_below += dot(near_ref[0], (near_link_ref[0] * low[0]).astype(BF16))
    next_above += dot(near_ref[1], (near_link_ref[1] * up[count - 1]).astype(BF16))
    _, low, up = face_sweep(count, ff_ref, y_ref, rhs_ref, link_ref, low, up, below, above)
    return face_sweep(count, ff_ref, y_ref, rhs_ref, link_ref, low, up, next_below, next_above)


def middle_window(count, opening, *refs):
    if opening:
        (first_ref, second_ref, ff_ref, y_ref, rhs_ref, link_ref, faces_ref, share_ref,
         new_faces, out_first, out_second, near_ref, near_link_ref) = refs
        face = faces_ref.shape[1] // 2
        for k, part in enumerate(received(first_ref, second_ref, slice(2 * face, 3 * face))):
            near_ref[k] = part.astype(BF16)
        for k, part in enumerate(received(first_ref, second_ref, slice(3 * face, 3 * face + 8))):
            near_link_ref[k] = transpose(jnp.broadcast_to(part[:1], (face, face)))
    else:
        (first_ref, second_ref, ff_ref, y_ref, rhs_ref, link_ref, faces_ref, near_ref, near_link_ref,
         new_faces, out_first, out_second) = refs
        face = faces_ref.shape[1] // 2
    _, low, up = window(
        count, first_ref, second_ref, ff_ref, y_ref, rhs_ref, link_ref, faces_ref, near_ref, near_link_ref
    )
    for i in range(count):
        new_faces[i, :face] = low[i]
        new_faces[i, face:] = up[i]
    upward, downward = outgoing(count, ff_ref, y_ref, rhs_ref, link_ref, low, up)
    if opening:
        upward += (share_ref[1],)
        downward += (share_ref[0],)
    store_messages(upward, downward, out_first, out_second)


def step_window(count, opening, first_ref, second_ref, ff_ref, y_ref, rhs_ref, link_ref, faces_ref, near_ref,
                near_link_ref, fm_ref, rf_ref, base_ref, source_ref,
                new_faces, out_first, out_second, new_rhs, new_mid, new_y, *near_share):
    face = faces_ref.shape[1] // 2
    if opening:
        for k, part in enumerate(received(first_ref, second_ref, slice(2 * face, 2 * face + 8))):
            near_share[0][k] = part
    vectors, low, up = window(
        count, first_ref, second_ref, ff_ref, y_ref, rhs_ref, link_ref, faces_ref, near_ref, near_link_ref
    )
    for i in range(count):
        new_faces[i, :face] = low[i]
        new_faces[i, face:] = up[i]
        rhs = base_ref[i] + dot(rf_ref[i], vectors[i]) + source_ref[i]
        new_rhs[i] = rhs[: 2 * face]
        new_mid[i] = rhs[2 * face :]
        new_y[i] = dot(fm_ref[i], rhs[2 * face :].astype(BF16))
    store_messages(*outgoing(count, ff_ref, new_y, new_rhs, link_ref, low, up), out_first, out_second)


def inner_base(count, mid_ref, rm_ref, base_ref):
    for i in range(count):
        base_ref[i] = dot(rm_ref[i], mid_ref[i].astype(BF16))


def shares(count, ff_ref, rf_ref, link_ref, mass_ref, share_ref):
    face = ff_ref.shape[1] // 2
    mass = []
    for i in range(count):
        total = jnp.sum(ff_ref[i].astype(F32), axis=0, keepdims=True)
        total += jnp.sum(rf_ref[i, 2 * face :].astype(F32), axis=0, keepdims=True)
        mass.append(jnp.broadcast_to(total / rf_ref.shape[1], (8, 2 * face)))
        for k in range(2):
            line = mass[i][:1, k * face : (k + 1) * face]
            mass_ref[i, k * face : (k + 1) * face] = transpose(jnp.broadcast_to(line, (face, face)))
    for k, (outer, other) in enumerate(((0, 1), (count - 1, count - 2))):
        here, there = slice(k * face, (k + 1) * face), pl.ds((1 - k) * face, face)
        line = transpose(link_ref[2 * outer + k])[:8]
        inner_line = transpose(link_ref[2 * other + k])[:8]
        one = mass[outer][:, here] * line
        operator = ff_ref[outer, there, here].astype(F32)
        two = dot(mass[other][:, here] * inner_line, operator, precision=HIGH) * line
        share_ref[k] = jnp.where(iota(one.shape, 0) == 0, one, two)


def end_mean(count, mid_ref, rm_ref, y_ref, near_share_ref, out_ref, column_ref):
    face = y_ref.shape[1] // 2
    for k in range(2):
        for j in range(2):
            line = jnp.broadcast_to(near_share_ref[k, j : j + 1], (face, face))
            column_ref[2 * k + j] = transpose(line)
    for i in range(count):
        inner = dot(rm_ref[i, 2 * face :], mid_ref[i].astype(BF16))
        total = jnp.sum(y_ref[i], axis=0, keepdims=True) + jnp.sum(inner, axis=0, keepdims=True)
        out_ref[i : i + 1] = total / rm_ref.shape[1]


def means_payload(count, ff_ref, y_ref, rhs_ref, link_ref, faces_ref, near_ref, near_link_ref,
                  column_ref, mass_ref, base_mean_ref, mean_ref, op_ref, parts_ref):
    low, up = load_faces(count, faces_ref)
    zero = jnp.zeros_like(low[0])
    last = count - 1
    next_below = dot(near_ref[0], (near_link_ref[0] * low[0]).astype(BF16))
    next_above = dot(near_ref[1], (near_link_ref[1] * up[last]).astype(BF16))
    _, next_low, next_up = face_sweep(count, ff_ref, y_ref, rhs_ref, link_ref, low, up, zero, zero)
    rows = []
    for i in range(count):
        v = jnp.concatenate(
            face_vector(i, count, rhs_ref, link_ref, next_low, next_up, next_below, next_above), axis=0
        )
        rows.append(base_mean_ref[i : i + 1] + weighted(mass_ref[i], v.astype(F32)))
    rows += [mean_ref[i : i + 1] for i in range(count)]
    for k, (two, one) in ((1, (up[last], next_up[last])), (0, (low[0], next_low[0]))):
        rows.append(weighted(column_ref[2 * k], one))
        rows.append(weighted(column_ref[2 * k + 1], two))
    rows += [zero[:1]] * (payload_rows(count) - len(rows))
    parts_ref[...] = dot(op_ref[...], jnp.concatenate(rows, axis=0), precision=HIGH)


def weighted(column, x):
    return jnp.sum(column * x, axis=0, keepdims=True)


def payload_rows(count):
    return -(-(2 * count + 4) // 8) * 8


def taken_base(count, mid_ref, fm_ref, rm_ref, y_ref, inner_ref):
    face = y_ref.shape[1] // 2
    for i in range(count):
        v = mid_ref[i].astype(BF16)
        y_ref[i] = dot(fm_ref[i], v)
        inner_ref[i] = dot(rm_ref[i, 2 * face :], v)


def last_window(count, first_ref, second_ref, ff_ref, y_ref, rhs_ref, link_ref, faces_ref, near_ref,
                near_link_ref, rf_ref, inner_ref, end_ref):
    face = faces_ref.shape[1] // 2
    width = end_ref.shape[1]
    vectors, low, up = window(
        count, first_ref, second_ref, ff_ref, y_ref, rhs_ref, link_ref, faces_ref, near_ref, near_link_ref
    )
    for i in range(count):
        end_ref[i, :face] = low[i]
        end_ref[i, face : width - face] = inner_ref[i] + dot(rf_ref[i, 2 * face :], vectors[i])
        end_ref[i, width - face :] = up[i]


def coarse_operator(count, slices, partner_hbm, cond_hbm, out_ref, partner_ref, cond_ref, sems):
    copies = [
        pltpu.make_async_copy(partner_hbm, partner_ref, sems.at[0]),
        pltpu.make_async_copy(cond_hbm, cond_ref, sems.at[1]),
    ]
    for copy in copies:
        copy.start()
    for copy in copies:
        copy.wait()
    n = partner_ref.shape[0]
    row, col = iota((n, n), 0), iota((n, n), 1)
    weights = (jnp.abs(row - col) == 1).astype(F32)
    for b in range(n):
        to, cond = partner_ref[b], cond_ref[b]
        weights += jnp.where((row == b) & (col == to), cond, 0.0)
        weights += jnp.where((col == b) & (row == to), cond, 0.0)
    eye = (row == col).astype(F32)
    m = eye + eye * jnp.sum(weights, axis=1, keepdims=True) - weights
    for i in range(n):
        pivot = 1.0 / m[i : i + 1, i : i + 1]
        line = m[i : i + 1, :] * pivot
        column = m[:, i : i + 1]
        inner = jnp.where(col == i, -column * pivot, m - column * line)
        m = jnp.where(row == i, jnp.where(col == i, pivot, line), inner)
    here, me = lax.axis_index("cuts"), lax.axis_index("sub")
    shape = (n, out_ref.shape[1])
    block, item = iota(shape, 0) - me * count, iota(shape, 1)
    own = (item < count) & (block == item)
    above = (item >= 2 * count) & (item < 2 * count + 2) & (block == item - count)
    below = (item >= 2 * count + 2) & (item < 2 * count + 4) & (block == 2 * count + 1 - item)
    end = (own | above | below).astype(F32)
    start = ((item >= count) & (item < 2 * count) & (block == item - count)).astype(F32)
    ends, starts = [], []
    for _ in range(1, slices - 1):
        end, start = dot(m, end, precision=HIGH), dot(m, start, precision=HIGH)
        ends.append(end)
        starts.append(start)
    for s in range(slices):
        total = jnp.zeros(shape, F32)
        for k in range(1, slices - 1):
            if s - 1 - k >= 0:
                total += jnp.where(here == s - 1 - k, ends[k - 1], 0.0)
            if s - k >= 1:
                total -= jnp.where(here == s - k, starts[k - 1], 0.0)
        out_ref[s * n : (s + 1) * n] = total


def correct(count, parts_ref, previous_ref, start_ref, out_hbm, out_ref, sems):
    later = lax.axis_index("cuts") > 0
    mine = jnp.sum(parts_ref[...], axis=0)
    copies = []
    for i in range(count):
        out_ref[i] = jnp.where(later, previous_ref[i] + mine[i : i + 1], start_ref[i])
        copies.append(pltpu.make_async_copy(out_ref.at[i], out_hbm.at[i], sems.at[i]))
        copies[i].start()
    for copy in copies:
        copy.wait()


def exchange(first, second, ahead=0):
    size, slices = lax.axis_size("sub"), lax.axis_size("cuts")
    pairs, other = [], []
    for c in range(slices):
        d = (c + ahead) % slices
        for i in range(size):
            pairs.append((c * size + i, d * size + (i ^ 1)))
            j = i + (1 if i % 2 else -1)
            if 0 <= j < size:
                other.append((c * size + i, d * size + j))
            elif ahead:
                other.append((c * size + i, d * size + i))
            else:
                other.append((c * size + i, (c ^ 1 if c ^ 1 < slices else c) * size + i))
    far = lax.ppermute(second, ("cuts", "sub"), other)
    near = lax.ppermute(first, ("cuts", "sub"), pairs)
    return near, far


def on_device(slices, start_states, source, block_inverse, face_map, transmissibility, partner, fracture_cond):
    start = start_states[0]
    count, width, scenarios = start.shape
    face = face_map.shape[-1]
    inner = width - 2 * face
    sub = lax.axis_size("sub")
    sds = jax.ShapeDtypeStruct
    message = sds((2 * face, scenarios), F32)
    opening = sds((3 * face + 8, scenarios), F32)
    sharing = sds((2 * face + 8, scenarios), F32)
    share_shape = sds((2, 8, face), F32)
    per = payload_rows(count)
    faces_shape = sds((count, 2 * face, scenarios), F32)
    rhs_shape = sds((count, width, scenarios), F32)
    held = [
        pltpu.with_memory_space_constraint(a, pltpu.HBM)
        for a in (start, source, block_inverse, face_map, transmissibility)
    ]
    buffers = [pltpu.VMEM(a.shape, a.dtype) for a in (start, source)]
    row = pltpu.VMEM((face, width), BF16)
    tables = [pltpu.VMEM(a.shape, a.dtype) for a in (face_map, transmissibility)]
    mid_shape = sds((count, inner, scenarios), F32)
    rhs, link, faces, first, second = call(
        functools.partial(prepare, count),
        [faces_shape, sds((2 * count, face, scenarios), F32), faces_shape, opening, opening],
        held,
        stay=range(5),
        scratch=buffers + [row, row] + tables + [pltpu.SemaphoreType.DMA((6,))],
    )
    ff, fm, rf, rm, mid, wells, y, mean = call(
        functools.partial(prepare_rest, count),
        [
            sds((count, 2 * face, 2 * face), BF16),
            sds((count, 2 * face, inner), BF16),
            sds((count, width, 2 * face), BF16),
            sds((count, width, inner), BF16),
            mid_shape,
            rhs_shape,
            faces_shape,
            sds((count, scenarios), F32),
        ],
        held[:4],
        stay=range(4),
        scratch=buffers
        + [pltpu.VMEM(block_inverse.shape, BF16), tables[0], pltpu.SemaphoreType.DMA((4,))],
    )
    blocks = partner.shape[0]
    (op,) = call(
        functools.partial(coarse_operator, count, slices),
        [sds((slices * blocks, per), F32)],
        [pltpu.with_memory_space_constraint(v, pltpu.HBM) for v in (partner, fracture_cond)],
        stay=range(2),
        scratch=[
            pltpu.SMEM((blocks,), jnp.int32),
            pltpu.SMEM((blocks,), F32),
            pltpu.SemaphoreType.DMA((2,)),
        ],
    )
    mass, share = call(
        functools.partial(shares, count),
        [faces_shape, share_shape],
        (ff, rf, link),
    )
    near = near_link = None
    ring = [(i, (i + 1) % slices) for i in range(slices)]
    for step in range(FINE_STEPS):
        final = step == FINE_STEPS - 1
        if final:
            taken_mid = lax.ppermute(mid, "cuts", ring)
            taken_rhs = lax.ppermute(rhs, "cuts", ring)
            base_mean, near_column = call(
                functools.partial(end_mean, count),
                [sds((count, scenarios), F32), sds((4, face, scenarios), F32)],
                (mid, rm, y, near_share),
            )
        else:
            (base,) = call(functools.partial(inner_base, count), [rhs_shape], (mid, rm))
        for turn in range(0, SWEEPS, 2):
            ending = final and turn == SWEEPS - 2
            first, second = exchange(first, second, 1 if ending else 0)
            common = (first, second, ff, y, rhs, link, faces)
            if turn < SWEEPS - 2:
                if near is None:
                    faces, first, second, near, near_link = call(
                        functools.partial(middle_window, count, True),
                        [faces_shape, sharing, sharing, sds((2, face, face), BF16), sds((2, face, scenarios), F32)],
                        common + (share,),
                    )
                else:
                    faces, first, second = call(
                        functools.partial(middle_window, count, False),
                        [faces_shape, message, message],
                        common + (near, near_link),
                    )
            elif not ending:
                outs = [faces_shape, message, message, faces_shape, mid_shape, faces_shape]
                outs = call(
                    functools.partial(step_window, count, step == 0),
                    outs + [share_shape] if step == 0 else outs,
                    common + (near, near_link, fm, rf, base, wells),
                )
                faces, first, second, rhs, mid, y = outs[:6]
                if step == 0:
                    near_share = outs[6]
    taken_faces = lax.ppermute(faces, "cuts", ring)
    taken_y, taken_inner = call(
        functools.partial(taken_base, count),
        [faces_shape, mid_shape],
        (taken_mid, fm, rm),
    )
    taken_y, parts_rhs = lax.optimization_barrier((taken_y, rhs))
    (parts,) = call(
        functools.partial(means_payload, count),
        [sds((slices * blocks, scenarios), F32)],
        (ff, y, parts_rhs, link, faces, near, near_link, near_column, mass, base_mean, mean, op),
    )
    parts = parts.reshape(slices * sub, count, scenarios)
    parts = lax.all_to_all(parts, ("cuts", "sub"), 0, 0, tiled=True)
    (previous,) = call(
        functools.partial(last_window, count),
        [rhs_shape],
        (first, second, ff, taken_y, taken_rhs, link, taken_faces, near, near_link, rf, taken_inner),
    )
    (result,) = call(
        functools.partial(correct, count),
        [rhs_shape],
        (parts, previous, start),
        stay_out=(0,),
        scratch=[pltpu.VMEM(rhs_shape.shape, F32), pltpu.SemaphoreType.DMA((count,))],
    )
    return result[None]


def solution(mesh):
    slices = mesh.shape["cuts"]

    def body(*args):
        return on_device(slices, *args)

    in_specs = (
        P("cuts", "sub", None, None),
        P("sub", None, None),
        P("sub", None, None),
        P("sub", None, None),
        P("sub", None, None),
        P(),
        P(),
    )
    return jax.shard_map(
        body,
        mesh=mesh,
        in_specs=in_specs,
        out_specs=P("cuts", "sub", None, None),
        check_vma=False,
    )
```

time: 86.8 us -> 85.6 us (0.986)
  starting transfers between devices: 37.1 us -> 28.8 us
  Pallas kernels: 14.2 us -> 18.6 us
  waiting for transfers between devices: 33.6 us -> 37.9 us
  local copies, waits for them, and re-layouts: 1.47 us -> 0.01 us
    pallas_call x16 -> x19, Pallas kernels: 14.2 us -> 18.6 us  [call(): pl.pallas_call(body, out_shape=out_shape, in_specs=[hbm if k in stay else...]
    ppermute x10 -> x11, starting transfers between devices: 27.9 us -> 23.6 us  [the longest x8 22 us: exchange(): near = lax.ppermute(first, ('cuts', 'sub'), pairs)]
    all_to_all x1, starting transfers between devices: 9.19 us -> 5.13 us  [on_device(): parts = lax.all_to_all(parts, ('cuts', 'sub'), 0, 0, tiled=True)]
    all_to_all x1, waiting for transfers between devices: 2.92 us -> 5.65 us  [on_device(): parts = lax.all_to_all(parts, ('cuts', 'sub'), 0, 0, tiled=True)]
    ppermute x10 -> x11, waiting for transfers between devices: 30.7 us -> 32.2 us  [the longest x8 32.2 us: exchange(): near = lax.ppermute(first, ('cuts', 'sub'), pairs)]
    unnamed x6 -> x2, local copies, waits for them, and re-layouts: 1.31 us -> 0.01 us
  transfers between devices with their start and end apart: 19 -> 20, of which waited for: 9 -> 8; matrix products, arithmetic and copies ran while one was open for 0% -> 0% of each run, Pallas kernels for 7% -> 12%
where the time goes in v2:
time: 85.6 us; the launch traced here: 85.4 us
  waiting for transfers between devices  37.9 us (44%)
  starting transfers between devices  28.8 us (34%)
  Pallas kernels  18.6 us (22%)
    ppermute x8, waiting for transfers between devices, exchange(): near = lax.ppermute(first, ('cuts', 'sub'), pairs)  32.2 us
    ppermute x8, starting transfers between devices, exchange(): near = lax.ppermute(first, ('cuts', 'sub'), pairs)  22 us
    pallas_call x19, Pallas kernels, call(): pl.pallas_call(body, out_shape=out_shape, in_specs=[hbm if k in stay else...  18.6 us
    all_to_all x1, waiting for transfers between devices, on_device(): parts = lax.all_to_all(parts, ('cuts', 'sub'), 0, 0, tiled=True)  5.65 us
    all_to_all x1, starting transfers between devices, on_device(): parts = lax.all_to_all(parts, ('cuts', 'sub'), 0, 0, tiled=True)  5.13 us
  transfers between devices with their start and end apart: 20, of which 8 were waited for; matrix products, arithmetic and copies ran while one was open for 0% of the time, Pallas kernels for 12%

profile of v2, /device:TPU:0, one launch (start us, length us, event | category | flops | bytes accessed | tf_op | source)
XLA Modules:
  0.0 85.4 jit_solution(1999898913768333676)
XLA Ops:
  0.0 1.9 %shard_map.74 = (f32[2,256,128]{2,1,0:T(8,128)S(1)}, f32[4,128,128]{2,1,0:T(8,128)S(1)}, f32[2,256,128]{2,1,0:T(8,128)S(1)}, f32[392,128]{1,0:T(8,128)S(1)}, f32[392,128]{1,0:T(8,128)S(1)}) custom-call(f32[2,512,128]{2,1,0:T(8,128)} %bitcast.3, bf16[2,512,128]{2,1,0:T(8,128)(2,1)} %source_hbm.3, bf16[2,512,512]{2,1,0:T(8,128)(2,1)} %inverse_hbm.3, ...), custom_call_target="tpu_custom_call" | custom-call | flops 268435456 | bytes 3026944 | tf_op jit(solution)/shard_map/pallas_call | solution.py:34
  1.9 3.0 %collective-permute-start = (f32[392,128]{1,0:T(8,128)S(1)}, f32[392,128]{1,0:T(8,128)S(1)}, u32[]{:S(2)}, u32[]{:S(2)}) collective-permute-start(f32[392,128]{1,0:T(8,128)S(1)} %get-tuple-element.60), channel_id=1, source_target_pairs={{0,1},{1,0},{2,3},{3,2},{4,5},{5,4},{6,7},{7,6},{8,9},{9,8},{10,11... | collective-permute-start | bytes 602120 | tf_op jit(solution)/shard_map/ppermute | solution.py:434
  4.9 2.2 %shard_map.73 = (bf16[2,256,256]{2,1,0:T(8,128)(2,1)S(1)}, bf16[2,256,256]{2,1,0:T(8,128)(2,1)S(1)}, bf16[2,512,256]{2,1,0:T(8,128)(2,1)S(1)}, bf16[2,512,256]{2...) custom-call(f32[2,512,128]{2,1,0:T(8,128)} %bitcast.4, ...), custom_call_target="tpu_custom_call" | custom-call | flops 268435456 | bytes 4459520 | tf_op jit(solution)/shard_map/pallas_call | solution.py:34
  7.5 6.0 %collective-permute-done.refs_0_ = f32[392,128]{1,0:T(8,128)S(1)} collective-permute-done((f32[392,128]{1,0:T(8,128)S(1)}, f32[392,128]{1,0:T(8,128)S(1)}, u32[]{:S(2)}, u32[]{:S(2)}) %collective-permute-start) | collective-permute-done | bytes 200736 | tf_op jit(solution)/shard_map/ppermute | solution.py:434
  13.5 0.7 shard_map.76
  14.2 2.5 %collective-permute-start.2 = (f32[264,128]{1,0:T(8,128)S(1)}, f32[264,128]{1,0:T(8,128)S(1)}, u32[]{:S(2)}, u32[]{:S(2)}) collective-permute-start(f32[264,128]{1,0:T(8,128)S(1)} %get-tuple-element.68), channel_id=1, source_target_pairs={{0,1},{1,0},{2,3},{3,2},{4,5},{5,4},{6,7},{7,6},{8,9},{9,8},{10,11... | collective-permute-start | bytes 405512 | tf_op jit(solution)/shard_map/ppermute | solution.py:434
  17.0 4.6 %collective-permute-done.2.first_ref = f32[264,128]{1,0:T(8,128)S(1)} collective-permute-done((f32[264,128]{1,0:T(8,128)S(1)}, f32[264,128]{1,0:T(8,128)S(1)}, u32[]{:S(2)}, u32[]{:S(2)}) %collective-permute-start.2) | collective-permute-done | bytes 135200 | tf_op jit(solution)/shard_map/ppermute | solution.py:434
  21.6 1.1 %shard_map.78 = (f32[2,256,128]{2,1,0:T(8,128)S(1)}, f32[256,128]{1,0:T(8,128)S(1)}, f32[256,128]{1,0:T(8,128)S(1)}, f32[2,256,128]{2,1,0:T(8,128)S(1)}, f32[2,2...) custom-call(f32[264,128]{1,0:T(8,128)S(1)} %collective-permute-done.2.first_ref, ...), custom_call_target="tpu_custom_call" | custom-call | flops 268435456 | bytes 4931584 | tf_op jit(solution)/shard_map/pallas_call | solution.py:34
  22.7 2.5 %collective-permute-start.4 = (f32[256,128]{1,0:T(8,128)S(1)}, f32[256,128]{1,0:T(8,128)S(1)}, u32[]{:S(2)}, u32[]{:S(2)}) collective-permute-start(f32[256,128]{1,0:T(8,128)S(1)} %get-tuple-element.77), channel_id=1, source_target_pairs={{0,1},{1,0},{2,3},{3,2},{4,5},{5,4},{6,7},{7,6},{8,9},{9,8},{10,11... | collective-permute-start | bytes 393224 | tf_op jit(solution)/shard_map/ppermute | solution.py:434
  25.3 4.7 %collective-permute-done.4.refs_0_ = f32[256,128]{1,0:T(8,128)S(1)} collective-permute-done((f32[256,128]{1,0:T(8,128)S(1)}, f32[256,128]{1,0:T(8,128)S(1)}, u32[]{:S(2)}, u32[]{:S(2)}) %collective-permute-start.4) | collective-permute-done | bytes 131104 | tf_op jit(solution)/shard_map/ppermute | solution.py:434
  30.0 0.6 shard_map.79
  30.6 2.5 %collective-permute-start.6 = (f32[256,128]{1,0:T(8,128)S(1)}, f32[256,128]{1,0:T(8,128)S(1)}, u32[]{:S(2)}, u32[]{:S(2)}) collective-permute-start(f32[256,128]{1,0:T(8,128)S(1)} %get-tuple-element.82), channel_id=1, source_target_pairs={{0,1},{1,0},{2,3},{3,2},{4,5},{5,4},{6,7},{7,6},{8,9},{9,8},{10,11... | collective-permute-start | bytes 393224 | tf_op jit(solution)/shard_map/ppermute | solution.py:434
  33.5 4.5 %collective-permute-done.6.first_ref = f32[256,128]{1,0:T(8,128)S(1)} collective-permute-done((f32[256,128]{1,0:T(8,128)S(1)}, f32[256,128]{1,0:T(8,128)S(1)}, u32[]{:S(2)}, u32[]{:S(2)}) %collective-permute-start.6) | collective-permute-done | bytes 131104 | tf_op jit(solution)/shard_map/ppermute | solution.py:434
  38.0 1.1 %shard_map.81 = (f32[2,256,128]{2,1,0:T(8,128)S(1)}, f32[256,128]{1,0:T(8,128)S(1)}, f32[256,128]{1,0:T(8,128)S(1)}, f32[2,256,128]{2,1,0:T(8,128)S(1)}, f32[2,2...) custom-call(f32[256,128]{1,0:T(8,128)S(1)} %collective-permute-done.6.first_ref, ...), custom_call_target="tpu_custom_call" | custom-call | flops 268435456 | bytes 4915200 | tf_op jit(solution)/shard_map/pallas_call | solution.py:34
  39.1 2.5 %collective-permute-start.8 = (f32[256,128]{1,0:T(8,128)S(1)}, f32[256,128]{1,0:T(8,128)S(1)}, u32[]{:S(2)}, u32[]{:S(2)}) collective-permute-start(f32[256,128]{1,0:T(8,128)S(1)} %get-tuple-element.86), channel_id=1, source_target_pairs={{0,1},{1,0},{2,3},{3,2},{4,5},{5,4},{6,7},{7,6},{8,9},{9,8},{10,11... | collective-permute-start | bytes 393224 | tf_op jit(solution)/shard_map/ppermute | solution.py:434
  41.6 4.8 %collective-permute-done.8.refs_0_ = f32[256,128]{1,0:T(8,128)S(1)} collective-permute-done((f32[256,128]{1,0:T(8,128)S(1)}, f32[256,128]{1,0:T(8,128)S(1)}, u32[]{:S(2)}, u32[]{:S(2)}) %collective-permute-start.8) | collective-permute-done | bytes 131104 | tf_op jit(solution)/shard_map/ppermute | solution.py:434
  46.4 0.6 shard_map.82
  47.0 2.5 %collective-permute-start.10 = (f32[256,128]{1,0:T(8,128)S(1)}, f32[256,128]{1,0:T(8,128)S(1)}, u32[]{:S(2)}, u32[]{:S(2)}) collective-permute-start(f32[256,128]{1,0:T(8,128)S(1)} %get-tuple-element.91), channel_id=1, source_target_pairs={{0,1},{1,0},{2,3},{3,2},{4,5},{5,4},{6,7},{7,6},{8,9},{9,8},{10,11... | collective-permute-start | bytes 393224 | tf_op jit(solution)/shard_map/ppermute | solution.py:434
  49.8 4.5 %collective-permute-done.10.first_ref = f32[256,128]{1,0:T(8,128)S(1)} collective-permute-done((f32[256,128]{1,0:T(8,128)S(1)}, f32[256,128]{1,0:T(8,128)S(1)}, u32[]{:S(2)}, u32[]{:S(2)}) %collective-permute-start.10) | collective-permute-done | bytes 131104 | tf_op jit(solution)/shard_map/ppermute | solution.py:434
  54.3 1.1 %shard_map.84 = (f32[2,256,128]{2,1,0:T(8,128)S(1)}, f32[256,128]{1,0:T(8,128)S(1)}, f32[256,128]{1,0:T(8,128)S(1)}, f32[2,256,128]{2,1,0:T(8,128)S(1)}, f32[2,2...) custom-call(f32[256,128]{1,0:T(8,128)S(1)} %collective-permute-done.10.first_ref, ...), custom_call_target="tpu_custom_call" | custom-call | flops 268435456 | bytes 4915200 | tf_op jit(solution)/shard_map/pallas_call | solution.py:34
  55.4 2.5 %collective-permute-start.13 = (f32[256,128]{1,0:T(8,128)S(1)}, f32[256,128]{1,0:T(8,128)S(1)}, u32[]{:S(2)}, u32[]{:S(2)}) collective-permute-start(f32[256,128]{1,0:T(8,128)S(1)} %get-tuple-element.100), channel_id=1, source_target_pairs={{0,1},{1,0},{2,3},{3,2},{4,5},{5,4},{6,7},{7,6},{8,9},{9,8},{10,11... | collective-permute-start | bytes 393224 | tf_op jit(solution)/shard_map/ppermute | solution.py:434
  57.9 0.5 collective-permute-start.12
  58.5 1.1 %collective-permute-start.17 = (f32[2,256,128]{2,1,0:T(8,128)S(1)}, f32[2,256,128]{2,1,0:T(8,128)S(1)}, u32[]{:S(2)}, u32[]{:S(2)}) collective-permute-start(f32[2,256,128]{2,1,0:T(8,128)S(1)} %get-tuple-element.99.refs_4_.rhs_ref), channel_id=1, source_target_pairs={{0,8},{8,16},{16,24},{24,0},{1,9},{9,17},{17,25},{25,1},{2,10},{10... | collective-permute-start | bytes 786440 | tf_op jit(solution)/shard_map/ppermute | solution.py:507
  59.6 3.1 %collective-permute-done.13.refs_0_ = f32[256,128]{1,0:T(8,128)S(1)} collective-permute-done((f32[256,128]{1,0:T(8,128)S(1)}, f32[256,128]{1,0:T(8,128)S(1)}, u32[]{:S(2)}, u32[]{:S(2)}) %collective-permute-start.13) | collective-permute-done | bytes 131104 | tf_op jit(solution)/shard_map/ppermute | solution.py:434
  62.7 1.3 %shard_map.86 = (f32[2,256,128]{2,1,0:T(8,128)S(1)}, f32[256,128]{1,0:T(8,128)}, f32[256,128]{1,0:T(8,128)}) custom-call(f32[256,128]{1,0:T(8,128)S(1)} %collective-permute-done.13.refs_0_, f32[256,128]{1,0:T(8,128)S(1)} %collective-permute-done.14.refs_1_, bf16[2,256,256]{2,1,0:T(8,128)(2,1)S(1)} %get-tuple-element.59.ff_ref.refs_2_, ...), custom_call_target="tpu_custom_call" | custom-call | flops 268435456 | bytes 2293760 | tf_op jit(solution)/shard_map/pallas_call | solution.py:34
  64.0 3.7 %collective-permute-start.15 = (f32[256,128]{1,0:T(8,128)}, f32[256,128]{1,0:T(8,128)S(1)}, u32[]{:S(2)}, u32[]{:S(2)}) collective-permute-start(f32[256,128]{1,0:T(8,128)} %get-tuple-element.109), channel_id=1, source_target_pairs={{0,9},{1,8},{2,11},{3,10},{4,13},{5,12},{6,15},{7,14},{8,17},{9,16... | collective-permute-start | bytes 393224 | tf_op jit(solution)/shard_map/ppermute | solution.py:434
  67.7 2.9 %shard_map.88.op_ref = f32[64,8]{1,0:T(8,128)S(1)} custom-call(s32[16]{0:T(128)} %partner_hbm.1, f32[16]{0:T(128)} %cond_hbm.1), custom_call_target="tpu_custom_call" | custom-call | flops 268435456 | bytes 2176 | tf_op jit(solution)/shard_map/pallas_call | solution.py:34
  71.2 1.0 %shard_map.89 = f32[64,128]{1,0:T(8,128)} custom-call(bf16[2,256,256]{2,1,0:T(8,128)(2,1)S(1)} %get-tuple-element.59.ff_ref.refs_2_, f32[2,256,128]{2,1,0:T(8,128)S(1)} %get-tuple-element.95.refs_3_.y_ref, f32[2,256,128]{2,1,0:T(8,128)S(1)} %get-tuple-element.99.refs_4_.rhs_ref, f32[4,128,128]{2,1,0:T(8,128)S(1)} %get-tuple-element.64.link_ref.refs_5_, ...), custom_call_target="tpu_custom_call" | custom-call | flops 268435456 | bytes 2068480 | tf_op jit(solution)/shard_map/pallas_call | solution.py:34
  72.2 5.1 %all-to-all-start = ((f32[32,2,128]{2,1,0:T(2,128)}), f32[32,2,128]{2,1,0:T(2,128)S(1)}, u32[]{:S(2)}, u32[]{:S(2)}) async-start(f32[32,2,128]{2,1,0:T(2,128)} %bitcast.1), calls=%async_computation | async-start | bytes 65536 | tf_op jit(solution)/shard_map/all_to_all | solution.py:555
  77.4 1.5 %shard_map.90.previous_ref = f32[2,512,128]{2,1,0:T(8,128)S(1)} custom-call(f32[256,128]{1,0:T(8,128)S(1)} %collective-permute-done.15.first_ref, f32[256,128]{1,0:T(8,128)} %collective-permute-done.16.second_ref, bf16[2,256,256]{2,1,0:T(8,128)(2,1)S(1)} %get-tuple-element.59.ff_ref.refs_2_, f32[2,256,128]{2,1,0:T(8,128)S(1)} %get-tuple-element.111.y_ref, ...), custom_call_target="tpu_custom_call" | custom-call | flops 268435456 | bytes 3080192 | tf_op jit(solution)/shard_map/pallas_call | solution.py:34
  78.9 5.7 %all-to-all-done.parts_ref = f32[32,2,128]{2,1,0:T(2,128)S(1)} async-done(((f32[32,2,128]{2,1,0:T(2,128)}), f32[32,2,128]{2,1,0:T(2,128)S(1)}, u32[]{:S(2)}, u32[]{:S(2)}) %all-to-all-start) | async-done | bytes 32800 | tf_op jit(solution)/shard_map/all_to_all | solution.py:555
  84.6 0.9 %shard_map.91 = f32[2,512,128]{2,1,0:T(8,128)} custom-call(f32[32,2,128]{2,1,0:T(2,128)S(1)} %all-to-all-done.parts_ref, f32[2,512,128]{2,1,0:T(8,128)S(1)} %shard_map.90.previous_ref, f32[2,512,128]{2,1,0:T(8,128)S(1)} %bitcast.5), custom_call_target="tpu_custom_call" | custom-call | flops 268435456 | bytes 1605632 | tf_op jit(solution)/shard_map/pallas_call | solution.py:34
  (29 shorter events, 1.7 us)
Async XLA Ops:
  1.9 11.6 %collective-permute-start = (f32[392,128]{1,0:T(8,128)S(1)}, f32[392,128]{1,0:T(8,128)S(1)}, u32[]{:S(2)}, u32[]{:S(2)}) collective-permute-start(f32[392,128]{1,0:T(8,128)S(1)} %get-tuple-element.60), channel_id=1, source_target_pairs={{0,1},{1,0},{2,3},{3,2},{4,5},{5,4},{6,7},{7,6},{8,9},{9,8},{10,11... | collective-permute-start | bytes 602120 | tf_op jit(solution)/shard_map/ppermute | solution.py:434
  4.9 8.5 %collective-permute-start.1 = (f32[392,128]{1,0:T(8,128)S(1)}, f32[392,128]{1,0:T(8,128)S(1)}, u32[]{:S(2)}, u32[]{:S(2)}) collective-permute-start(f32[392,128]{1,0:T(8,128)S(1)} %get-tuple-element.61), channel_id=1, source_target_pairs={{0,8},{1,2},{2,1},{3,4},{4,3},{5,6},{6,5},{7,15},{8,0},{9,10},{10,... | collective-permute-start | bytes 602120 | tf_op jit(solution)/shard_map/ppermute | solution.py:433
  14.2 7.4 %collective-permute-start.2 = (f32[264,128]{1,0:T(8,128)S(1)}, f32[264,128]{1,0:T(8,128)S(1)}, u32[]{:S(2)}, u32[]{:S(2)}) collective-permute-start(f32[264,128]{1,0:T(8,128)S(1)} %get-tuple-element.68), channel_id=1, source_target_pairs={{0,1},{1,0},{2,3},{3,2},{4,5},{5,4},{6,7},{7,6},{8,9},{9,8},{10,11... | collective-permute-start | bytes 405512 | tf_op jit(solution)/shard_map/ppermute | solution.py:434
  16.7 4.9 %collective-permute-start.3 = (f32[264,128]{1,0:T(8,128)S(1)}, f32[264,128]{1,0:T(8,128)S(1)}, u32[]{:S(2)}, u32[]{:S(2)}) collective-permute-start(f32[264,128]{1,0:T(8,128)S(1)} %get-tuple-element.69), channel_id=1, source_target_pairs={{0,8},{1,2},{2,1},{3,4},{4,3},{5,6},{6,5},{7,15},{8,0},{9,10},{10,... | collective-permute-start | bytes 405512 | tf_op jit(solution)/shard_map/ppermute | solution.py:433
  22.7 7.3 %collective-permute-start.4 = (f32[256,128]{1,0:T(8,128)S(1)}, f32[256,128]{1,0:T(8,128)S(1)}, u32[]{:S(2)}, u32[]{:S(2)}) collective-permute-start(f32[256,128]{1,0:T(8,128)S(1)} %get-tuple-element.77), channel_id=1, source_target_pairs={{0,1},{1,0},{2,3},{3,2},{4,5},{5,4},{6,7},{7,6},{8,9},{9,8},{10,11... | collective-permute-start | bytes 393224 | tf_op jit(solution)/shard_map/ppermute | solution.py:434
  25.3 4.8 %collective-permute-start.5 = (f32[256,128]{1,0:T(8,128)S(1)}, f32[256,128]{1,0:T(8,128)S(1)}, u32[]{:S(2)}, u32[]{:S(2)}) collective-permute-start(f32[256,128]{1,0:T(8,128)S(1)} %get-tuple-element.78), channel_id=1, source_target_pairs={{0,8},{1,2},{2,1},{3,4},{4,3},{5,6},{6,5},{7,15},{8,0},{9,10},{10,... | collective-permute-start | bytes 393224 | tf_op jit(solution)/shard_map/ppermute | solution.py:433
  30.6 7.3 %collective-permute-start.6 = (f32[256,128]{1,0:T(8,128)S(1)}, f32[256,128]{1,0:T(8,128)S(1)}, u32[]{:S(2)}, u32[]{:S(2)}) collective-permute-start(f32[256,128]{1,0:T(8,128)S(1)} %get-tuple-element.82), channel_id=1, source_target_pairs={{0,1},{1,0},{2,3},{3,2},{4,5},{5,4},{6,7},{7,6},{8,9},{9,8},{10,11... | collective-permute-start | bytes 393224 | tf_op jit(solution)/shard_map/ppermute | solution.py:434
  33.2 4.8 %collective-permute-start.7 = (f32[256,128]{1,0:T(8,128)S(1)}, f32[256,128]{1,0:T(8,128)S(1)}, u32[]{:S(2)}, u32[]{:S(2)}) collective-permute-start(f32[256,128]{1,0:T(8,128)S(1)} %get-tuple-element.83), channel_id=1, source_target_pairs={{0,8},{1,2},{2,1},{3,4},{4,3},{5,6},{6,5},{7,15},{8,0},{9,10},{10,... | collective-permute-start | bytes 393224 | tf_op jit(solution)/shard_map/ppermute | solution.py:433
  39.1 7.3 %collective-permute-start.8 = (f32[256,128]{1,0:T(8,128)S(1)}, f32[256,128]{1,0:T(8,128)S(1)}, u32[]{:S(2)}, u32[]{:S(2)}) collective-permute-start(f32[256,128]{1,0:T(8,128)S(1)} %get-tuple-element.86), channel_id=1, source_target_pairs={{0,1},{1,0},{2,3},{3,2},{4,5},{5,4},{6,7},{7,6},{8,9},{9,8},{10,11... | collective-permute-start | bytes 393224 | tf_op jit(solution)/shard_map/ppermute | solution.py:434
  41.6 4.8 %collective-permute-start.9 = (f32[256,128]{1,0:T(8,128)S(1)}, f32[256,128]{1,0:T(8,128)S(1)}, u32[]{:S(2)}, u32[]{:S(2)}) collective-permute-start(f32[256,128]{1,0:T(8,128)S(1)} %get-tuple-element.87), channel_id=1, source_target_pairs={{0,8},{1,2},{2,1},{3,4},{4,3},{5,6},{6,5},{7,15},{8,0},{9,10},{10,... | collective-permute-start | bytes 393224 | tf_op jit(solution)/shard_map/ppermute | solution.py:433
  47.0 7.3 %collective-permute-start.10 = (f32[256,128]{1,0:T(8,128)S(1)}, f32[256,128]{1,0:T(8,128)S(1)}, u32[]{:S(2)}, u32[]{:S(2)}) collective-permute-start(f32[256,128]{1,0:T(8,128)S(1)} %get-tuple-element.91), channel_id=1, source_target_pairs={{0,1},{1,0},{2,3},{3,2},{4,5},{5,4},{6,7},{7,6},{8,9},{9,8},{10,11... | collective-permute-start | bytes 393224 | tf_op jit(solution)/shard_map/ppermute | solution.py:434
  49.5 4.8 %collective-permute-start.11 = (f32[256,128]{1,0:T(8,128)S(1)}, f32[256,128]{1,0:T(8,128)S(1)}, u32[]{:S(2)}, u32[]{:S(2)}) collective-permute-start(f32[256,128]{1,0:T(8,128)S(1)} %get-tuple-element.92), channel_id=1, source_target_pairs={{0,8},{1,2},{2,1},{3,4},{4,3},{5,6},{6,5},{7,15},{8,0},{9,10},{10,... | collective-permute-start | bytes 393224 | tf_op jit(solution)/shard_map/ppermute | solution.py:433
  55.4 7.3 %collective-permute-start.13 = (f32[256,128]{1,0:T(8,128)S(1)}, f32[256,128]{1,0:T(8,128)S(1)}, u32[]{:S(2)}, u32[]{:S(2)}) collective-permute-start(f32[256,128]{1,0:T(8,128)S(1)} %get-tuple-element.100), channel_id=1, source_target_pairs={{0,1},{1,0},{2,3},{3,2},{4,5},{5,4},{6,7},{7,6},{8,9},{9,8},{10,11... | collective-permute-start | bytes 393224 | tf_op jit(solution)/shard_map/ppermute | solution.py:434
  57.9 4.8 %collective-permute-start.14 = (f32[256,128]{1,0:T(8,128)S(1)}, f32[256,128]{1,0:T(8,128)S(1)}, u32[]{:S(2)}, u32[]{:S(2)}) collective-permute-start(f32[256,128]{1,0:T(8,128)S(1)} %get-tuple-element.101), channel_id=1, source_target_pairs={{0,8},{1,2},{2,1},{3,4},{4,3},{5,6},{6,5},{7,15},{8,0},{9,10},{10,... | collective-permute-start | bytes 393224 | tf_op jit(solution)/shard_map/ppermute | solution.py:433
  57.9 12.9 %collective-permute-start.12 = (f32[2,256,128]{2,1,0:T(8,128)S(1)}, f32[2,256,128]{2,1,0:T(8,128)S(1)}, u32[]{:S(2)}, u32[]{:S(2)}) collective-permute-start(f32[2,256,128]{2,1,0:T(8,128)S(1)} %get-tuple-element.96.mid_ref), channel_id=1, source_target_pairs={{0,8},{8,16},{16,24},{24,0},{1,9},{9,17},{17,25},{25,1},{2,10},{10... | collective-permute-start | bytes 786440 | tf_op jit(solution)/shard_map/ppermute | solution.py:506
  58.5 18.9 %collective-permute-start.17 = (f32[2,256,128]{2,1,0:T(8,128)S(1)}, f32[2,256,128]{2,1,0:T(8,128)S(1)}, u32[]{:S(2)}, u32[]{:S(2)}) collective-permute-start(f32[2,256,128]{2,1,0:T(8,128)S(1)} %get-tuple-element.99.refs_4_.rhs_ref), channel_id=1, source_target_pairs={{0,8},{8,16},{16,24},{24,0},{1,9},{9,17},{17,25},{25,1},{2,10},{10... | collective-permute-start | bytes 786440 | tf_op jit(solution)/shard_map/ppermute | solution.py:507
  64.0 13.4 %collective-permute-start.18 = (f32[2,256,128]{2,1,0:T(8,128)S(1)}, f32[2,256,128]{2,1,0:T(8,128)S(1)}, u32[]{:S(2)}, u32[]{:S(2)}) collective-permute-start(f32[2,256,128]{2,1,0:T(8,128)S(1)} %get-tuple-element.103.faces_ref), channel_id=1, source_target_pairs={{0,8},{8,16},{16,24},{24,0},{1,9},{9,17},{17,25},{25,1},{2,10},{10... | collective-permute-start | bytes 786440 | tf_op jit(solution)/shard_map/ppermute | solution.py:542
  64.0 13.4 %collective-permute-start.15 = (f32[256,128]{1,0:T(8,128)}, f32[256,128]{1,0:T(8,128)S(1)}, u32[]{:S(2)}, u32[]{:S(2)}) collective-permute-start(f32[256,128]{1,0:T(8,128)} %get-tuple-element.109), channel_id=1, source_target_pairs={{0,9},{1,8},{2,11},{3,10},{4,13},{5,12},{6,15},{7,14},{8,17},{9,16... | collective-permute-start | bytes 393224 | tf_op jit(solution)/shard_map/ppermute | solution.py:434
  67.7 9.7 %collective-permute-start.16 = (f32[256,128]{1,0:T(8,128)}, f32[256,128]{1,0:T(8,128)}, u32[]{:S(2)}, u32[]{:S(2)}) collective-permute-start(f32[256,128]{1,0:T(8,128)} %get-tuple-element.110), channel_id=1, source_target_pairs={{0,8},{1,10},{2,9},{3,12},{4,11},{5,14},{6,13},{7,15},{8,16},{9,18... | collective-permute-start | bytes 393224 | tf_op jit(solution)/shard_map/ppermute | solution.py:433
  72.2 12.3 %all-to-all-start = ((f32[32,2,128]{2,1,0:T(2,128)}), f32[32,2,128]{2,1,0:T(2,128)S(1)}, u32[]{:S(2)}, u32[]{:S(2)}) async-start(f32[32,2,128]{2,1,0:T(2,128)} %bitcast.1), calls=%async_computation | async-start | bytes 65536 | tf_op jit(solution)/shard_map/all_to_all | solution.py:555
  77.4 7.1 %copy-start = (f32[1,2,512,128]{3,2,1,0:T(8,128)S(1)}, f32[1,2,512,128]{3,2,1,0:T(8,128)}, u32[]{:S(2)}) copy-start(f32[1,2,512,128]{3,2,1,0:T(8,128)} %param.7) | copy-start | bytes 1572868

commit v3 on v2

--- a/solution.py
+++ b/solution.py
@@ -27,7 +27,7 @@
     return lax.broadcasted_iota(jnp.int32, shape, axis)
 
 
-def call(body, out_shape, args, flops=1 << 28, stay=(), stay_out=(), scratch=()):
+def call(body, out_shape, args, flops=1 << 28, stay=(), stay_out=(), scratch=(), aliases=None):
     size = sum(a.size * a.dtype.itemsize for a in list(args) + list(out_shape))
     vmem = pl.BlockSpec(memory_space=pltpu.VMEM)
     hbm = pl.BlockSpec(memory_space=pltpu.HBM)
@@ -37,6 +37,7 @@
         in_specs=[hbm if k in stay else vmem for k in range(len(args))],
         out_specs=[hbm if k in stay_out else vmem for k in range(len(out_shape))],
         scratch_shapes=list(scratch),
+        input_output_aliases=aliases or {},
         compiler_params=pltpu.CompilerParams(vmem_limit_bytes=24 << 20),
         cost_estimate=pl.CostEstimate(flops=flops, bytes_accessed=size, transcendentals=0),
     )(*args)
@@ -175,7 +176,7 @@
 
 
 def prepare_rest(count, start_hbm, source_hbm, inverse_hbm, map_hbm,
-                 ff_ref, fm_ref, rf_ref, rm_ref, mid_ref, wells_ref, y_ref, mean_ref,
+                 ff_ref, fm_ref, pf_ref, rf_ref, pm_ref, rm_ref, mid_ref, wells_ref, y_ref, mean_ref,
                  start_ref, source_ref, inverse_ref, map_ref, sems):
     for copy in read_all(
         (start_hbm, source_hbm, inverse_hbm, map_hbm), (start_ref, source_ref, inverse_ref, map_ref), sems
@@ -192,14 +193,14 @@
             columns = dot(inverse_ref[i, :, rows], perms[side], ((1,), (1,))).astype(BF16)
             ff_ref[i, :face, to] = columns[:face]
             ff_ref[i, face:, to] = columns[width - face :]
-            rf_ref[i, 2 * face :, to] = columns[inner]
+            rf_ref[i, :, to] = columns[inner]
             wells_ref[i, to] = dot(perms[side], source_ref[i, rows])
             fm_ref[i, to] = inverse_ref[i, rows, inner]
         for side in range(2):
             to = slice(side * face, (side + 1) * face)
-            rf_ref[i, to] = dot(perms[side], ff_ref[i, to]).astype(BF16)
-            rm_ref[i, to] = dot(perms[side], fm_ref[i, to]).astype(BF16)
-        rm_ref[i, 2 * face :] = inverse_ref[i, inner, inner]
+            pf_ref[i, to] = dot(perms[side], ff_ref[i, to]).astype(BF16)
+            pm_ref[i, to] = dot(perms[side], fm_ref[i, to]).astype(BF16)
+        rm_ref[i] = inverse_ref[i, inner, inner]
         wells = source_ref[i, inner].astype(F32)
         mid_ref[i] = start_ref[i, inner] + wells
         wells_ref[i, 2 * face :] = wells
@@ -250,7 +251,7 @@
 
 
 def step_window(count, opening, first_ref, second_ref, ff_ref, y_ref, rhs_ref, link_ref, faces_ref, near_ref,
-                near_link_ref, fm_ref, rf_ref, base_ref, source_ref,
+                near_link_ref, fm_ref, pf_ref, rf_ref, base_ref, source_ref,
                 new_faces, out_first, out_second, new_rhs, new_mid, new_y, *near_share):
     face = faces_ref.shape[1] // 2
     if opening:
@@ -262,16 +263,20 @@
     for i in range(count):
         new_faces[i, :face] = low[i]
         new_faces[i, face:] = up[i]
-        rhs = base_ref[i] + dot(rf_ref[i], vectors[i]) + source_ref[i]
-        new_rhs[i] = rhs[: 2 * face]
-        new_mid[i] = rhs[2 * face :]
-        new_y[i] = dot(fm_ref[i], rhs[2 * face :].astype(BF16))
+        cut = 2 * face
+        new_rhs[i] = base_ref[i, :cut] + dot(pf_ref[i], vectors[i]) + source_ref[i, :cut]
+        rhs = base_ref[i, cut:] + dot(rf_ref[i], vectors[i]) + source_ref[i, cut:]
+        new_mid[i] = rhs
+        new_y[i] = dot(fm_ref[i], rhs.astype(BF16))
     store_messages(*outgoing(count, ff_ref, new_y, new_rhs, link_ref, low, up), out_first, out_second)
 
 
-def inner_base(count, mid_ref, rm_ref, base_ref):
-    for i in range(count):
-        base_ref[i] = dot(rm_ref[i], mid_ref[i].astype(BF16))
+def inner_base(count, mid_ref, pm_ref, rm_ref, base_ref):
+    for i in range(count):
+        cut = pm_ref.shape[1]
+        v = mid_ref[i].astype(BF16)
+        base_ref[i, :cut] = dot(pm_ref[i], v)
+        base_ref[i, cut:] = dot(rm_ref[i], v)
 
 
 def shares(count, ff_ref, rf_ref, link_ref, mass_ref, share_ref):
@@ -279,8 +284,9 @@
     mass = []
     for i in range(count):
         total = jnp.sum(ff_ref[i].astype(F32), axis=0, keepdims=True)
-        total += jnp.sum(rf_ref[i, 2 * face :].astype(F32), axis=0, keepdims=True)
-        mass.append(jnp.broadcast_to(total / rf_ref.shape[1], (8, 2 * face)))
+        total += jnp.sum(rf_ref[i].astype(F32), axis=0, keepdims=True)
+        width = 2 * face + rf_ref.shape[1]
+        mass.append(jnp.broadcast_to(total / width, (8, 2 * face)))
         for k in range(2):
             line = mass[i][:1, k * face : (k + 1) * face]
             mass_ref[i, k * face : (k + 1) * face] = transpose(jnp.broadcast_to(line, (face, face)))
@@ -301,9 +307,9 @@
             line = jnp.broadcast_to(near_share_ref[k, j : j + 1], (face, face))
             column_ref[2 * k + j] = transpose(line)
     for i in range(count):
-        inner = dot(rm_ref[i, 2 * face :], mid_ref[i].astype(BF16))
+        inner = dot(rm_ref[i], mid_ref[i].astype(BF16))
         total = jnp.sum(y_ref[i], axis=0, keepdims=True) + jnp.sum(inner, axis=0, keepdims=True)
-        out_ref[i : i + 1] = total / rm_ref.shape[1]
+        out_ref[i : i + 1] = total / (2 * face + rm_ref.shape[1])
 
 
 def means_payload(count, ff_ref, y_ref, rhs_ref, link_ref, faces_ref, near_ref, near_link_ref,
@@ -336,25 +342,33 @@
     return -(-(2 * count + 4) // 8) * 8
 
 
-def taken_base(count, mid_ref, fm_ref, rm_ref, y_ref, inner_ref):
-    face = y_ref.shape[1] // 2
+def last_window(count, first_ref, second_ref, ff_ref, rhs_hbm, link_ref, faces_hbm, near_ref,
+                near_link_ref, rf_ref, mid_hbm, fm_ref, rm_ref, start_hbm, end_ref, out_hbm,
+                y_ref, rhs_ref, faces_ref, mid_ref, start_ref, sems, out_sems):
+    copies = read_all((mid_hbm, rhs_hbm, faces_hbm, start_hbm), (mid_ref, rhs_ref, faces_ref, start_ref), sems)
+    copies[0].wait()
+    face = faces_ref.shape[1] // 2
+    width = end_ref.shape[1]
     for i in range(count):
         v = mid_ref[i].astype(BF16)
         y_ref[i] = dot(fm_ref[i], v)
-        inner_ref[i] = dot(rm_ref[i, 2 * face :], v)
-
-
-def last_window(count, first_ref, second_ref, ff_ref, y_ref, rhs_ref, link_ref, faces_ref, near_ref,
-                near_link_ref, rf_ref, inner_ref, end_ref):
-    face = faces_ref.shape[1] // 2
-    width = end_ref.shape[1]
+        end_ref[i, face : width - face] = dot(rm_ref[i], v)
+    for copy in copies[1:]:
+        copy.wait()
     vectors, low, up = window(
         count, first_ref, second_ref, ff_ref, y_ref, rhs_ref, link_ref, faces_ref, near_ref, near_link_ref
     )
+    later = lax.axis_index("cuts") > 0
+    copies = []
     for i in range(count):
         end_ref[i, :face] = low[i]
-        end_ref[i, face : width - face] = inner_ref[i] + dot(rf_ref[i, 2 * face :], vectors[i])
+        end_ref[i, face : width - face] += dot(rf_ref[i], vectors[i])
         end_ref[i, width - face :] = up[i]
+        start_ref[i] = jnp.where(later, end_ref[i], start_ref[i])
+        copies.append(pltpu.make_async_copy(start_ref.at[i], out_hbm.at[i], out_sems.at[i]))
+        copies[i].start()
+    for copy in copies:
+        copy.wait()
 
 
 def coarse_operator(count, slices, partner_hbm, cond_hbm, out_ref, partner_ref, cond_ref, sems):
@@ -404,16 +418,22 @@
         out_ref[s * n : (s + 1) * n] = total
 
 
-def correct(count, parts_ref, previous_ref, start_ref, out_hbm, out_ref, sems):
-    later = lax.axis_index("cuts") > 0
-    mine = jnp.sum(parts_ref[...], axis=0)
-    copies = []
-    for i in range(count):
-        out_ref[i] = jnp.where(later, previous_ref[i] + mine[i : i + 1], start_ref[i])
-        copies.append(pltpu.make_async_copy(out_ref.at[i], out_hbm.at[i], sems.at[i]))
-        copies[i].start()
-    for copy in copies:
-        copy.wait()
+def correct(count, pieces, parts_ref, previous_ref, early_hbm, out_hbm, out_ref, sems):
+    @pl.when(lax.axis_index("cuts") > 1)
+    def _():
+        mine = jnp.sum(parts_ref[...], axis=0)
+        size = out_ref.shape[1] // pieces
+        copies = []
+        for i in range(count):
+            for k in range(pieces):
+                rows = pl.ds(k * size, size)
+                out_ref[i, rows] = previous_ref[i, rows] + mine[i : i + 1]
+                copies.append(
+                    pltpu.make_async_copy(out_ref.at[i, rows], out_hbm.at[i, rows], sems.at[i * pieces + k])
+                )
+                copies[-1].start()
+        for copy in copies:
+            copy.wait()
 
 
 def exchange(first, second, ahead=0):
@@ -464,13 +484,15 @@
         stay=range(5),
         scratch=buffers + [row, row] + tables + [pltpu.SemaphoreType.DMA((6,))],
     )
-    ff, fm, rf, rm, mid, wells, y, mean = call(
+    ff, fm, pf, rf, pm, rm, mid, wells, y, mean = call(
         functools.partial(prepare_rest, count),
         [
             sds((count, 2 * face, 2 * face), BF16),
             sds((count, 2 * face, inner), BF16),
-            sds((count, width, 2 * face), BF16),
-            sds((count, width, inner), BF16),
+            sds((count, 2 * face, 2 * face), BF16),
+            sds((count, inner, 2 * face), BF16),
+            sds((count, 2 * face, inner), BF16),
+            sds((count, inner, inner), BF16),
             mid_shape,
             rhs_shape,
             faces_shape,
@@ -511,7 +533,7 @@
                 (mid, rm, y, near_share),
             )
         else:
-            (base,) = call(functools.partial(inner_base, count), [rhs_shape], (mid, rm))
+            (base,) = call(functools.partial(inner_base, count), [rhs_shape], (mid, pm, rm))
         for turn in range(0, SWEEPS, 2):
             ending = final and turn == SWEEPS - 2
             first, second = exchange(first, second, 1 if ending else 0)
@@ -534,36 +556,45 @@
                 outs = call(
                     functools.partial(step_window, count, step == 0),
                     outs + [share_shape] if step == 0 else outs,
-                    common + (near, near_link, fm, rf, base, wells),
+                    common + (near, near_link, fm, pf, rf, base, wells),
                 )
                 faces, first, second, rhs, mid, y = outs[:6]
                 if step == 0:
                     near_share = outs[6]
     taken_faces = lax.ppermute(faces, "cuts", ring)
-    taken_y, taken_inner = call(
-        functools.partial(taken_base, count),
-        [faces_shape, mid_shape],
-        (taken_mid, fm, rm),
-    )
-    taken_y, parts_rhs = lax.optimization_barrier((taken_y, rhs))
     (parts,) = call(
         functools.partial(means_payload, count),
         [sds((slices * blocks, scenarios), F32)],
-        (ff, y, parts_rhs, link, faces, near, near_link, near_column, mass, base_mean, mean, op),
+        (ff, y, rhs, link, faces, near, near_link, near_column, mass, base_mean, mean, op),
     )
     parts = parts.reshape(slices * sub, count, scenarios)
     parts = lax.all_to_all(parts, ("cuts", "sub"), 0, 0, tiled=True)
-    (previous,) = call(
+    taken_rhs, taken_faces, taken_mid = (
+        pltpu.with_memory_space_constraint(v, pltpu.HBM) for v in (taken_rhs, taken_faces, taken_mid)
+    )
+    previous, early = call(
         functools.partial(last_window, count),
+        [rhs_shape, rhs_shape],
+        (first, second, ff, taken_rhs, link, taken_faces, near, near_link, rf, taken_mid, fm, rm, held[0]),
+        stay=(3, 5, 9, 12),
+        stay_out=(1,),
+        scratch=[pltpu.VMEM(faces_shape.shape, F32)] * 3
+        + [
+            pltpu.VMEM(mid_shape.shape, F32),
+            pltpu.VMEM(rhs_shape.shape, F32),
+            pltpu.SemaphoreType.DMA((4,)),
+            pltpu.SemaphoreType.DMA((count,)),
+        ],
+    )
+    pieces = 2
+    (result,) = call(
+        functools.partial(correct, count, pieces),
         [rhs_shape],
-        (first, second, ff, taken_y, taken_rhs, link, taken_faces, near, near_link, rf, taken_inner),
-    )
-    (result,) = call(
-        functools.partial(correct, count),
-        [rhs_shape],
-        (parts, previous, start),
+        (parts, previous, early),
+        stay=(2,),
         stay_out=(0,),
-        scratch=[pltpu.VMEM(rhs_shape.shape, F32), pltpu.SemaphoreType.DMA((count,))],
+        scratch=[pltpu.VMEM(rhs_shape.shape, F32), pltpu.SemaphoreType.DMA((count * pieces,))],
+        aliases={2: 0},
     )
     return result[None]
 

time: 85.6 us -> 83.6 us (0.977)
  waiting for transfers between devices: 37.9 us -> 36 us
  Pallas kernels: 18.6 us -> 17.6 us
    all_to_all x1, waiting for transfers between devices: 5.65 us -> 3.73 us  [on_device(): parts = lax.all_to_all(parts, ('cuts', 'sub'), 0, 0, tiled=True)]
    pallas_call x19 -> x18, Pallas kernels: 18.6 us -> 17.6 us  [call(): pl.pallas_call(body, out_shape=out_shape, in_specs=[hbm if k in stay else...]
  transfers between devices with their start and end apart: 20 -> 20, of which waited for: 8 -> 8; matrix products, arithmetic and copies ran while one was open for 0% -> 0% of each run, Pallas kernels for 12% -> 13%
where the time goes in v3:
time: 83.6 us; the launch traced here: 83.3 us
  waiting for transfers between devices  36 us (43%)
  starting transfers between devices  28.8 us (34%)
  Pallas kernels  17.6 us (21%)
    ppermute x8, waiting for transfers between devices, exchange(): near = lax.ppermute(first, ('cuts', 'sub'), pairs)  32.3 us
    ppermute x8, starting transfers between devices, exchange(): near = lax.ppermute(first, ('cuts', 'sub'), pairs)  22 us
    pallas_call x18, Pallas kernels, call(): pl.pallas_call(body, out_shape=out_shape, in_specs=[hbm if k in stay else...  17.6 us
    all_to_all x1, starting transfers between devices, on_device(): parts = lax.all_to_all(parts, ('cuts', 'sub'), 0, 0, tiled=True)  5.14 us
    all_to_all x1, waiting for transfers between devices, on_device(): parts = lax.all_to_all(parts, ('cuts', 'sub'), 0, 0, tiled=True)  3.73 us
  transfers between devices with their start and end apart: 20, of which 8 were waited for; matrix products, arithmetic and copies ran while one was open for 0% of the time, Pallas kernels for 13%

profile of v3, /device:TPU:0, one launch (start us, length us, event | category | flops | bytes accessed | tf_op | source)
XLA Modules:
  0.0 83.3 jit_solution(9492244580736369400)
XLA Ops:
  0.0 1.9 %shard_map.74 = (f32[2,256,128]{2,1,0:T(8,128)S(1)}, f32[4,128,128]{2,1,0:T(8,128)S(1)}, f32[2,256,128]{2,1,0:T(8,128)S(1)}, f32[392,128]{1,0:T(8,128)S(1)}, f32[392,128]{1,0:T(8,128)S(1)}) custom-call(f32[2,512,128]{2,1,0:T(8,128)} %bitcast.3, bf16[2,512,128]{2,1,0:T(8,128)(2,1)} %source_hbm.3, bf16[2,512,512]{2,1,0:T(8,128)(2,1)} %inverse_hbm.3, ...), custom_call_target="tpu_custom_call" | custom-call | flops 268435456 | bytes 3026944 | tf_op jit(solution)/shard_map/pallas_call | solution.py:34
  1.9 3.0 %collective-permute-start = (f32[392,128]{1,0:T(8,128)S(1)}, f32[392,128]{1,0:T(8,128)S(1)}, u32[]{:S(2)}, u32[]{:S(2)}) collective-permute-start(f32[392,128]{1,0:T(8,128)S(1)} %get-tuple-element.60), channel_id=1, source_target_pairs={{0,1},{1,0},{2,3},{3,2},{4,5},{5,4},{6,7},{7,6},{8,9},{9,8},{10,11... | collective-permute-start | bytes 602120 | tf_op jit(solution)/shard_map/ppermute | solution.py:454
  4.9 2.2 %shard_map.73 = (bf16[2,256,256]{2,1,0:T(8,128)(2,1)S(1)}, bf16[2,256,256]{2,1,0:T(8,128)(2,1)S(1)}, bf16[2,256,256]{2,1,0:T(8,128)(2,1)S(1)}, bf16[2,256,256]{2...) custom-call(f32[2,512,128]{2,1,0:T(8,128)} %bitcast.4, ...), custom_call_target="tpu_custom_call" | custom-call | flops 268435456 | bytes 4459520 | tf_op jit(solution)/shard_map/pallas_call | solution.py:34
  7.5 6.0 %collective-permute-done.refs_0_ = f32[392,128]{1,0:T(8,128)S(1)} collective-permute-done((f32[392,128]{1,0:T(8,128)S(1)}, f32[392,128]{1,0:T(8,128)S(1)}, u32[]{:S(2)}, u32[]{:S(2)}) %collective-permute-start) | collective-permute-done | bytes 200736 | tf_op jit(solution)/shard_map/ppermute | solution.py:454
  13.5 0.7 shard_map.76
  14.2 2.5 %collective-permute-start.2 = (f32[264,128]{1,0:T(8,128)S(1)}, f32[264,128]{1,0:T(8,128)S(1)}, u32[]{:S(2)}, u32[]{:S(2)}) collective-permute-start(f32[264,128]{1,0:T(8,128)S(1)} %get-tuple-element.68), channel_id=1, source_target_pairs={{0,1},{1,0},{2,3},{3,2},{4,5},{5,4},{6,7},{7,6},{8,9},{9,8},{10,11... | collective-permute-start | bytes 405512 | tf_op jit(solution)/shard_map/ppermute | solution.py:454
  17.0 4.6 %collective-permute-done.2.first_ref = f32[264,128]{1,0:T(8,128)S(1)} collective-permute-done((f32[264,128]{1,0:T(8,128)S(1)}, f32[264,128]{1,0:T(8,128)S(1)}, u32[]{:S(2)}, u32[]{:S(2)}) %collective-permute-start.2) | collective-permute-done | bytes 135200 | tf_op jit(solution)/shard_map/ppermute | solution.py:454
  21.6 1.0 %shard_map.78 = (f32[2,256,128]{2,1,0:T(8,128)S(1)}, f32[256,128]{1,0:T(8,128)S(1)}, f32[256,128]{1,0:T(8,128)S(1)}, f32[2,256,128]{2,1,0:T(8,128)S(1)}, f32[2,2...) custom-call(f32[264,128]{1,0:T(8,128)S(1)} %collective-permute-done.2.first_ref, ...), custom_call_target="tpu_custom_call" | custom-call | flops 268435456 | bytes 4931584 | tf_op jit(solution)/shard_map/pallas_call | solution.py:34
  22.6 2.5 %collective-permute-start.4 = (f32[256,128]{1,0:T(8,128)S(1)}, f32[256,128]{1,0:T(8,128)S(1)}, u32[]{:S(2)}, u32[]{:S(2)}) collective-permute-start(f32[256,128]{1,0:T(8,128)S(1)} %get-tuple-element.79), channel_id=1, source_target_pairs={{0,1},{1,0},{2,3},{3,2},{4,5},{5,4},{6,7},{7,6},{8,9},{9,8},{10,11... | collective-permute-start | bytes 393224 | tf_op jit(solution)/shard_map/ppermute | solution.py:454
  25.2 4.8 %collective-permute-done.4.refs_0_ = f32[256,128]{1,0:T(8,128)S(1)} collective-permute-done((f32[256,128]{1,0:T(8,128)S(1)}, f32[256,128]{1,0:T(8,128)S(1)}, u32[]{:S(2)}, u32[]{:S(2)}) %collective-permute-start.4) | collective-permute-done | bytes 131104 | tf_op jit(solution)/shard_map/ppermute | solution.py:454
  30.0 0.6 shard_map.79
  30.5 2.5 %collective-permute-start.6 = (f32[256,128]{1,0:T(8,128)S(1)}, f32[256,128]{1,0:T(8,128)S(1)}, u32[]{:S(2)}, u32[]{:S(2)}) collective-permute-start(f32[256,128]{1,0:T(8,128)S(1)} %get-tuple-element.84), channel_id=1, source_target_pairs={{0,1},{1,0},{2,3},{3,2},{4,5},{5,4},{6,7},{7,6},{8,9},{9,8},{10,11... | collective-permute-start | bytes 393224 | tf_op jit(solution)/shard_map/ppermute | solution.py:454
  33.4 4.5 %collective-permute-done.6.first_ref = f32[256,128]{1,0:T(8,128)S(1)} collective-permute-done((f32[256,128]{1,0:T(8,128)S(1)}, f32[256,128]{1,0:T(8,128)S(1)}, u32[]{:S(2)}, u32[]{:S(2)}) %collective-permute-start.6) | collective-permute-done | bytes 131104 | tf_op jit(solution)/shard_map/ppermute | solution.py:454
  37.9 1.0 %shard_map.81 = (f32[2,256,128]{2,1,0:T(8,128)S(1)}, f32[256,128]{1,0:T(8,128)S(1)}, f32[256,128]{1,0:T(8,128)S(1)}, f32[2,256,128]{2,1,0:T(8,128)S(1)}, f32[2,2...) custom-call(f32[256,128]{1,0:T(8,128)S(1)} %collective-permute-done.6.first_ref, ...), custom_call_target="tpu_custom_call" | custom-call | flops 268435456 | bytes 4915200 | tf_op jit(solution)/shard_map/pallas_call | solution.py:34
  38.9 2.5 %collective-permute-start.8 = (f32[256,128]{1,0:T(8,128)S(1)}, f32[256,128]{1,0:T(8,128)S(1)}, u32[]{:S(2)}, u32[]{:S(2)}) collective-permute-start(f32[256,128]{1,0:T(8,128)S(1)} %get-tuple-element.88), channel_id=1, source_target_pairs={{0,1},{1,0},{2,3},{3,2},{4,5},{5,4},{6,7},{7,6},{8,9},{9,8},{10,11... | collective-permute-start | bytes 393224 | tf_op jit(solution)/shard_map/ppermute | solution.py:454
  41.4 4.8 %collective-permute-done.8.refs_0_ = f32[256,128]{1,0:T(8,128)S(1)} collective-permute-done((f32[256,128]{1,0:T(8,128)S(1)}, f32[256,128]{1,0:T(8,128)S(1)}, u32[]{:S(2)}, u32[]{:S(2)}) %collective-permute-start.8) | collective-permute-done | bytes 131104 | tf_op jit(solution)/shard_map/ppermute | solution.py:454
  46.2 0.6 shard_map.82
  46.8 2.5 %collective-permute-start.10 = (f32[256,128]{1,0:T(8,128)S(1)}, f32[256,128]{1,0:T(8,128)S(1)}, u32[]{:S(2)}, u32[]{:S(2)}) collective-permute-start(f32[256,128]{1,0:T(8,128)S(1)} %get-tuple-element.93), channel_id=1, source_target_pairs={{0,1},{1,0},{2,3},{3,2},{4,5},{5,4},{6,7},{7,6},{8,9},{9,8},{10,11... | collective-permute-start | bytes 393224 | tf_op jit(solution)/shard_map/ppermute | solution.py:454
  49.6 4.5 %collective-permute-done.10.first_ref = f32[256,128]{1,0:T(8,128)S(1)} collective-permute-done((f32[256,128]{1,0:T(8,128)S(1)}, f32[256,128]{1,0:T(8,128)S(1)}, u32[]{:S(2)}, u32[]{:S(2)}) %collective-permute-start.10) | collective-permute-done | bytes 131104 | tf_op jit(solution)/shard_map/ppermute | solution.py:454
  54.1 1.0 %shard_map.84 = (f32[2,256,128]{2,1,0:T(8,128)S(1)}, f32[256,128]{1,0:T(8,128)S(1)}, f32[256,128]{1,0:T(8,128)S(1)}, f32[2,256,128]{2,1,0:T(8,128)S(1)}, f32[2,2...) custom-call(f32[256,128]{1,0:T(8,128)S(1)} %collective-permute-done.10.first_ref, ...), custom_call_target="tpu_custom_call" | custom-call | flops 268435456 | bytes 4915200 | tf_op jit(solution)/shard_map/pallas_call | solution.py:34
  55.1 2.5 %collective-permute-start.12 = (f32[256,128]{1,0:T(8,128)S(1)}, f32[256,128]{1,0:T(8,128)S(1)}, u32[]{:S(2)}, u32[]{:S(2)}) collective-permute-start(f32[256,128]{1,0:T(8,128)S(1)} %get-tuple-element.99), channel_id=1, source_target_pairs={{0,1},{1,0},{2,3},{3,2},{4,5},{5,4},{6,7},{7,6},{8,9},{9,8},{10,11... | collective-permute-start | bytes 393224 | tf_op jit(solution)/shard_map/ppermute | solution.py:454
  57.7 0.5 collective-permute-start.16
  58.2 1.1 %collective-permute-start.18 = (f32[2,256,128]{2,1,0:T(8,128)S(1)}, f32[2,256,128]{2,1,0:T(8,128)S(1)}, u32[]{:S(2)}, u32[]{:S(2)}) collective-permute-start(f32[2,256,128]{2,1,0:T(8,128)S(1)} %get-tuple-element.103.mid_ref), channel_id=1, source_target_pairs={{0,8},{8,16},{16,24},{24,0},{1,9},{9,17},{17,25},{25,1},{2,10},{10... | collective-permute-start | bytes 786440 | tf_op jit(solution)/shard_map/ppermute | solution.py:528
  59.2 3.2 %collective-permute-done.12.refs_0_ = f32[256,128]{1,0:T(8,128)S(1)} collective-permute-done((f32[256,128]{1,0:T(8,128)S(1)}, f32[256,128]{1,0:T(8,128)S(1)}, u32[]{:S(2)}, u32[]{:S(2)}) %collective-permute-start.12) | collective-permute-done | bytes 131104 | tf_op jit(solution)/shard_map/ppermute | solution.py:454
  62.4 0.6 shard_map.85
  63.1 3.7 %collective-permute-start.14 = (f32[256,128]{1,0:T(8,128)S(1)}, f32[256,128]{1,0:T(8,128)S(1)}, u32[]{:S(2)}, u32[]{:S(2)}) collective-permute-start(f32[256,128]{1,0:T(8,128)S(1)} %get-tuple-element.109), channel_id=1, source_target_pairs={{0,9},{1,8},{2,11},{3,10},{4,13},{5,12},{6,15},{7,14},{8,17},{9,16... | collective-permute-start | bytes 393224 | tf_op jit(solution)/shard_map/ppermute | solution.py:454
  66.7 2.9 %shard_map.87.op_ref = f32[64,8]{1,0:T(8,128)S(1)} custom-call(s32[16]{0:T(128)} %partner_hbm.1, f32[16]{0:T(128)} %cond_hbm.1), custom_call_target="tpu_custom_call" | custom-call | flops 268435456 | bytes 2176 | tf_op jit(solution)/shard_map/pallas_call | solution.py:34
  69.9 1.1 %shard_map.88 = f32[64,128]{1,0:T(8,128)} custom-call(bf16[2,256,256]{2,1,0:T(8,128)(2,1)S(1)} %get-tuple-element.59.ff_ref.refs_2_, f32[2,256,128]{2,1,0:T(8,128)S(1)} %get-tuple-element.97.refs_3_.y_ref, f32[2,256,128]{2,1,0:T(8,128)S(1)} %get-tuple-element.98.refs_4_.rhs_ref, f32[4,128,128]{2,1,0:T(8,128)S(1)} %get-tuple-element.64.link_ref.refs_5_, ...), custom_call_target="tpu_custom_call" | custom-call | flops 268435456 | bytes 2068480 | tf_op jit(solution)/shard_map/pallas_call | solution.py:34
  71.0 5.1 %all-to-all-start = ((f32[32,2,128]{2,1,0:T(2,128)}), f32[32,2,128]{2,1,0:T(2,128)S(1)}, u32[]{:S(2)}, u32[]{:S(2)}) async-start(f32[32,2,128]{2,1,0:T(2,128)} %bitcast.1), calls=%async_computation | async-start | bytes 65536 | tf_op jit(solution)/shard_map/all_to_all | solution.py:571
  76.2 0.7 copy-done
  76.9 2.6 %shard_map.89 = (f32[2,512,128]{2,1,0:T(8,128)S(1)}, f32[2,512,128]{2,1,0:T(8,128)}) custom-call(f32[256,128]{1,0:T(8,128)S(1)} %collective-permute-done.14.first_ref, f32[256,128]{1,0:T(8,128)S(1)} %collective-permute-done.15.second_ref, bf16[2,256,256]{2,1,0:T(8,128)(2,1)S(1)} %get-tuple-element.59.ff_ref.refs_2_, f32[2,256,128]{2,1,0:T(8,128)} %copy-done, ...), custom_call_target="tpu_custom_call" | custom-call | flops 268435456 | bytes 4128768 | tf_op jit(solution)/shard_map/pallas_call | solution.py:34
  79.6 3.7 %all-to-all-done.parts_ref = f32[32,2,128]{2,1,0:T(2,128)S(1)} async-done(((f32[32,2,128]{2,1,0:T(2,128)}), f32[32,2,128]{2,1,0:T(2,128)S(1)}, u32[]{:S(2)}, u32[]{:S(2)}) %all-to-all-start) | async-done | bytes 32800 | tf_op jit(solution)/shard_map/all_to_all | solution.py:571
  (30 shorter events, 1.6 us)
Async XLA Ops:
  1.9 11.6 %collective-permute-start = (f32[392,128]{1,0:T(8,128)S(1)}, f32[392,128]{1,0:T(8,128)S(1)}, u32[]{:S(2)}, u32[]{:S(2)}) collective-permute-start(f32[392,128]{1,0:T(8,128)S(1)} %get-tuple-element.60), channel_id=1, source_target_pairs={{0,1},{1,0},{2,3},{3,2},{4,5},{5,4},{6,7},{7,6},{8,9},{9,8},{10,11... | collective-permute-start | bytes 602120 | tf_op jit(solution)/shard_map/ppermute | solution.py:454
  4.9 8.6 %collective-permute-start.1 = (f32[392,128]{1,0:T(8,128)S(1)}, f32[392,128]{1,0:T(8,128)S(1)}, u32[]{:S(2)}, u32[]{:S(2)}) collective-permute-start(f32[392,128]{1,0:T(8,128)S(1)} %get-tuple-element.61), channel_id=1, source_target_pairs={{0,8},{1,2},{2,1},{3,4},{4,3},{5,6},{6,5},{7,15},{8,0},{9,10},{10,... | collective-permute-start | bytes 602120 | tf_op jit(solution)/shard_map/ppermute | solution.py:453
  14.2 7.5 %collective-permute-start.2 = (f32[264,128]{1,0:T(8,128)S(1)}, f32[264,128]{1,0:T(8,128)S(1)}, u32[]{:S(2)}, u32[]{:S(2)}) collective-permute-start(f32[264,128]{1,0:T(8,128)S(1)} %get-tuple-element.68), channel_id=1, source_target_pairs={{0,1},{1,0},{2,3},{3,2},{4,5},{5,4},{6,7},{7,6},{8,9},{9,8},{10,11... | collective-permute-start | bytes 405512 | tf_op jit(solution)/shard_map/ppermute | solution.py:454
  16.7 4.9 %collective-permute-start.3 = (f32[264,128]{1,0:T(8,128)S(1)}, f32[264,128]{1,0:T(8,128)S(1)}, u32[]{:S(2)}, u32[]{:S(2)}) collective-permute-start(f32[264,128]{1,0:T(8,128)S(1)} %get-tuple-element.69), channel_id=1, source_target_pairs={{0,8},{1,2},{2,1},{3,4},{4,3},{5,6},{6,5},{7,15},{8,0},{9,10},{10,... | collective-permute-start | bytes 405512 | tf_op jit(solution)/shard_map/ppermute | solution.py:453
  22.6 7.3 %collective-permute-start.4 = (f32[256,128]{1,0:T(8,128)S(1)}, f32[256,128]{1,0:T(8,128)S(1)}, u32[]{:S(2)}, u32[]{:S(2)}) collective-permute-start(f32[256,128]{1,0:T(8,128)S(1)} %get-tuple-element.79), channel_id=1, source_target_pairs={{0,1},{1,0},{2,3},{3,2},{4,5},{5,4},{6,7},{7,6},{8,9},{9,8},{10,11... | collective-permute-start | bytes 393224 | tf_op jit(solution)/shard_map/ppermute | solution.py:454
  25.2 4.8 %collective-permute-start.5 = (f32[256,128]{1,0:T(8,128)S(1)}, f32[256,128]{1,0:T(8,128)S(1)}, u32[]{:S(2)}, u32[]{:S(2)}) collective-permute-start(f32[256,128]{1,0:T(8,128)S(1)} %get-tuple-element.80), channel_id=1, source_target_pairs={{0,8},{1,2},{2,1},{3,4},{4,3},{5,6},{6,5},{7,15},{8,0},{9,10},{10,... | collective-permute-start | bytes 393224 | tf_op jit(solution)/shard_map/ppermute | solution.py:453
  30.5 7.3 %collective-permute-start.6 = (f32[256,128]{1,0:T(8,128)S(1)}, f32[256,128]{1,0:T(8,128)S(1)}, u32[]{:S(2)}, u32[]{:S(2)}) collective-permute-start(f32[256,128]{1,0:T(8,128)S(1)} %get-tuple-element.84), channel_id=1, source_target_pairs={{0,1},{1,0},{2,3},{3,2},{4,5},{5,4},{6,7},{7,6},{8,9},{9,8},{10,11... | collective-permute-start | bytes 393224 | tf_op jit(solution)/shard_map/ppermute | solution.py:454
  33.1 4.8 %collective-permute-start.7 = (f32[256,128]{1,0:T(8,128)S(1)}, f32[256,128]{1,0:T(8,128)S(1)}, u32[]{:S(2)}, u32[]{:S(2)}) collective-permute-start(f32[256,128]{1,0:T(8,128)S(1)} %get-tuple-element.85), channel_id=1, source_target_pairs={{0,8},{1,2},{2,1},{3,4},{4,3},{5,6},{6,5},{7,15},{8,0},{9,10},{10,... | collective-permute-start | bytes 393224 | tf_op jit(solution)/shard_map/ppermute | solution.py:453
  38.9 7.3 %collective-permute-start.8 = (f32[256,128]{1,0:T(8,128)S(1)}, f32[256,128]{1,0:T(8,128)S(1)}, u32[]{:S(2)}, u32[]{:S(2)}) collective-permute-start(f32[256,128]{1,0:T(8,128)S(1)} %get-tuple-element.88), channel_id=1, source_target_pairs={{0,1},{1,0},{2,3},{3,2},{4,5},{5,4},{6,7},{7,6},{8,9},{9,8},{10,11... | collective-permute-start | bytes 393224 | tf_op jit(solution)/shard_map/ppermute | solution.py:454
  41.4 4.8 %collective-permute-start.9 = (f32[256,128]{1,0:T(8,128)S(1)}, f32[256,128]{1,0:T(8,128)S(1)}, u32[]{:S(2)}, u32[]{:S(2)}) collective-permute-start(f32[256,128]{1,0:T(8,128)S(1)} %get-tuple-element.89), channel_id=1, source_target_pairs={{0,8},{1,2},{2,1},{3,4},{4,3},{5,6},{6,5},{7,15},{8,0},{9,10},{10,... | collective-permute-start | bytes 393224 | tf_op jit(solution)/shard_map/ppermute | solution.py:453
  46.8 7.3 %collective-permute-start.10 = (f32[256,128]{1,0:T(8,128)S(1)}, f32[256,128]{1,0:T(8,128)S(1)}, u32[]{:S(2)}, u32[]{:S(2)}) collective-permute-start(f32[256,128]{1,0:T(8,128)S(1)} %get-tuple-element.93), channel_id=1, source_target_pairs={{0,1},{1,0},{2,3},{3,2},{4,5},{5,4},{6,7},{7,6},{8,9},{9,8},{10,11... | collective-permute-start | bytes 393224 | tf_op jit(solution)/shard_map/ppermute | solution.py:454
  49.3 4.8 %collective-permute-start.11 = (f32[256,128]{1,0:T(8,128)S(1)}, f32[256,128]{1,0:T(8,128)S(1)}, u32[]{:S(2)}, u32[]{:S(2)}) collective-permute-start(f32[256,128]{1,0:T(8,128)S(1)} %get-tuple-element.94), channel_id=1, source_target_pairs={{0,8},{1,2},{2,1},{3,4},{4,3},{5,6},{6,5},{7,15},{8,0},{9,10},{10,... | collective-permute-start | bytes 393224 | tf_op jit(solution)/shard_map/ppermute | solution.py:453
  55.1 7.3 %collective-permute-start.12 = (f32[256,128]{1,0:T(8,128)S(1)}, f32[256,128]{1,0:T(8,128)S(1)}, u32[]{:S(2)}, u32[]{:S(2)}) collective-permute-start(f32[256,128]{1,0:T(8,128)S(1)} %get-tuple-element.99), channel_id=1, source_target_pairs={{0,1},{1,0},{2,3},{3,2},{4,5},{5,4},{6,7},{7,6},{8,9},{9,8},{10,11... | collective-permute-start | bytes 393224 | tf_op jit(solution)/shard_map/ppermute | solution.py:454
  57.6 4.8 %collective-permute-start.13 = (f32[256,128]{1,0:T(8,128)S(1)}, f32[256,128]{1,0:T(8,128)S(1)}, u32[]{:S(2)}, u32[]{:S(2)}) collective-permute-start(f32[256,128]{1,0:T(8,128)S(1)} %get-tuple-element.100), channel_id=1, source_target_pairs={{0,8},{1,2},{2,1},{3,4},{4,3},{5,6},{6,5},{7,15},{8,0},{9,10},{10,... | collective-permute-start | bytes 393224 | tf_op jit(solution)/shard_map/ppermute | solution.py:453
  57.7 18.5 %collective-permute-start.16 = (f32[2,256,128]{2,1,0:T(8,128)S(1)}, f32[2,256,128]{2,1,0:T(8,128)S(1)}, u32[]{:S(2)}, u32[]{:S(2)}) collective-permute-start(f32[2,256,128]{2,1,0:T(8,128)S(1)} %get-tuple-element.98.refs_4_.rhs_ref), channel_id=1, source_target_pairs={{0,8},{8,16},{16,24},{24,0},{1,9},{9,17},{17,25},{25,1},{2,10},{10... | collective-permute-start | bytes 786440 | tf_op jit(solution)/shard_map/ppermute | solution.py:529
  58.2 18.0 %collective-permute-start.18 = (f32[2,256,128]{2,1,0:T(8,128)S(1)}, f32[2,256,128]{2,1,0:T(8,128)S(1)}, u32[]{:S(2)}, u32[]{:S(2)}) collective-permute-start(f32[2,256,128]{2,1,0:T(8,128)S(1)} %get-tuple-element.103.mid_ref), channel_id=1, source_target_pairs={{0,8},{8,16},{16,24},{24,0},{1,9},{9,17},{17,25},{25,1},{2,10},{10... | collective-permute-start | bytes 786440 | tf_op jit(solution)/shard_map/ppermute | solution.py:528
  63.0 13.2 %collective-permute-start.17 = (f32[2,256,128]{2,1,0:T(8,128)S(1)}, f32[2,256,128]{2,1,0:T(8,128)}, u32[]{:S(2)}, u32[]{:S(2)}) collective-permute-start(f32[2,256,128]{2,1,0:T(8,128)S(1)} %get-tuple-element.102.faces_ref), channel_id=1, source_target_pairs={{0,8},{8,16},{16,24},{24,0},{1,9},{9,17},{17,25},{25,1},{2,10},{10... | collective-permute-start | bytes 786440 | tf_op jit(solution)/shard_map/ppermute | solution.py:564
  63.1 13.1 %collective-permute-start.14 = (f32[256,128]{1,0:T(8,128)S(1)}, f32[256,128]{1,0:T(8,128)S(1)}, u32[]{:S(2)}, u32[]{:S(2)}) collective-permute-start(f32[256,128]{1,0:T(8,128)S(1)} %get-tuple-element.109), channel_id=1, source_target_pairs={{0,9},{1,8},{2,11},{3,10},{4,13},{5,12},{6,15},{7,14},{8,17},{9,16... | collective-permute-start | bytes 393224 | tf_op jit(solution)/shard_map/ppermute | solution.py:454
  66.7 9.4 %collective-permute-start.15 = (f32[256,128]{1,0:T(8,128)S(1)}, f32[256,128]{1,0:T(8,128)S(1)}, u32[]{:S(2)}, u32[]{:S(2)}) collective-permute-start(f32[256,128]{1,0:T(8,128)S(1)} %get-tuple-element.110), channel_id=1, source_target_pairs={{0,8},{1,10},{2,9},{3,12},{4,11},{5,14},{6,13},{7,15},{8,16},{9,18... | collective-permute-start | bytes 393224 | tf_op jit(solution)/shard_map/ppermute | solution.py:453
  71.0 12.3 %all-to-all-start = ((f32[32,2,128]{2,1,0:T(2,128)}), f32[32,2,128]{2,1,0:T(2,128)S(1)}, u32[]{:S(2)}, u32[]{:S(2)}) async-start(f32[32,2,128]{2,1,0:T(2,128)} %bitcast.1), calls=%async_computation | async-start | bytes 65536 | tf_op jit(solution)/shard_map/all_to_all | solution.py:571
  76.1 0.7 copy-start
  76.2 0.8 copy-start.1

commit v4 on v3

--- a/solution.py
+++ b/solution.py
@@ -235,7 +235,7 @@
             near_link_ref[k] = transpose(jnp.broadcast_to(part[:1], (face, face)))
     else:
         (first_ref, second_ref, ff_ref, y_ref, rhs_ref, link_ref, faces_ref, near_ref, near_link_ref,
-         new_faces, out_first, out_second) = refs
+         new_faces, out_first, out_second, *next_faces) = refs
         face = faces_ref.shape[1] // 2
     _, low, up = window(
         count, first_ref, second_ref, ff_ref, y_ref, rhs_ref, link_ref, faces_ref, near_ref, near_link_ref
@@ -243,7 +243,15 @@
     for i in range(count):
         new_faces[i, :face] = low[i]
         new_faces[i, face:] = up[i]
-    upward, downward = outgoing(count, ff_ref, y_ref, rhs_ref, link_ref, low, up)
+    if not opening and next_faces:
+        zero = jnp.zeros_like(low[0])
+        _, next_low, next_up = face_sweep(count, ff_ref, y_ref, rhs_ref, link_ref, low, up, zero, zero)
+        for i in range(count):
+            next_faces[0][i, :face] = next_low[i]
+            next_faces[0][i, face:] = next_up[i]
+        upward, downward = (up[-1], next_up[-1]), (low[0], next_low[0])
+    else:
+        upward, downward = outgoing(count, ff_ref, y_ref, rhs_ref, link_ref, low, up)
     if opening:
         upward += (share_ref[1],)
         downward += (share_ref[0],)
@@ -312,26 +320,27 @@
         out_ref[i : i + 1] = total / (2 * face + rm_ref.shape[1])
 
 
-def means_payload(count, ff_ref, y_ref, rhs_ref, link_ref, faces_ref, near_ref, near_link_ref,
+def means_payload(count, rhs_ref, link_ref, faces_ref, next_ref, near_ref, near_link_ref,
                   column_ref, mass_ref, base_mean_ref, mean_ref, op_ref, parts_ref):
     low, up = load_faces(count, faces_ref)
-    zero = jnp.zeros_like(low[0])
+    next_low, next_up = load_faces(count, next_ref)
     last = count - 1
     next_below = dot(near_ref[0], (near_link_ref[0] * low[0]).astype(BF16))
     next_above = dot(near_ref[1], (near_link_ref[1] * up[last]).astype(BF16))
-    _, next_low, next_up = face_sweep(count, ff_ref, y_ref, rhs_ref, link_ref, low, up, zero, zero)
     rows = []
     for i in range(count):
-        v = jnp.concatenate(
-            face_vector(i, count, rhs_ref, link_ref, next_low, next_up, next_below, next_above), axis=0
-        )
-        rows.append(base_mean_ref[i : i + 1] + weighted(mass_ref[i], v.astype(F32)))
+        v_low, v_up = face_vector(i, count, rhs_ref, link_ref, next_low, next_up, next_below, next_above)
+        face = v_low.shape[0]
+        own = weighted(mass_ref[i, :face], v_low.astype(F32)) + weighted(mass_ref[i, face:], v_up.astype(F32))
+        rows.append(base_mean_ref[i : i + 1] + own)
     rows += [mean_ref[i : i + 1] for i in range(count)]
     for k, (two, one) in ((1, (up[last], next_up[last])), (0, (low[0], next_low[0]))):
         rows.append(weighted(column_ref[2 * k], one))
         rows.append(weighted(column_ref[2 * k + 1], two))
-    rows += [zero[:1]] * (payload_rows(count) - len(rows))
-    parts_ref[...] = dot(op_ref[...], jnp.concatenate(rows, axis=0), precision=HIGH)
+    total = op_ref[0] * rows[0]
+    for k in range(1, len(rows)):
+        total += op_ref[k] * rows[k]
+    parts_ref[...] = total
 
 
 def weighted(column, x):
@@ -396,7 +405,7 @@
         inner = jnp.where(col == i, -column * pivot, m - column * line)
         m = jnp.where(row == i, jnp.where(col == i, pivot, line), inner)
     here, me = lax.axis_index("cuts"), lax.axis_index("sub")
-    shape = (n, out_ref.shape[1])
+    shape = (n, payload_rows(count))
     block, item = iota(shape, 0) - me * count, iota(shape, 1)
     own = (item < count) & (block == item)
     above = (item >= 2 * count) & (item < 2 * count + 2) & (block == item - count)
@@ -415,7 +424,8 @@
                 total += jnp.where(here == s - 1 - k, ends[k - 1], 0.0)
             if s - k >= 1:
                 total -= jnp.where(here == s - k, starts[k - 1], 0.0)
-        out_ref[s * n : (s + 1) * n] = total
+        for k in range(out_ref.shape[0]):
+            out_ref[k, s * n : (s + 1) * n] = jnp.broadcast_to(total[:, k : k + 1], (n, out_ref.shape[2]))
 
 
 def correct(count, pieces, parts_ref, previous_ref, early_hbm, out_hbm, out_ref, sems):
@@ -466,7 +476,6 @@
     opening = sds((3 * face + 8, scenarios), F32)
     sharing = sds((2 * face + 8, scenarios), F32)
     share_shape = sds((2, 8, face), F32)
-    per = payload_rows(count)
     faces_shape = sds((count, 2 * face, scenarios), F32)
     rhs_shape = sds((count, width, scenarios), F32)
     held = [
@@ -506,7 +515,7 @@
     blocks = partner.shape[0]
     (op,) = call(
         functools.partial(coarse_operator, count, slices),
-        [sds((slices * blocks, per), F32)],
+        [sds((2 * count + 4, slices * blocks, scenarios), F32)],
         [pltpu.with_memory_space_constraint(v, pltpu.HBM) for v in (partner, fracture_cond)],
         stay=range(2),
         scratch=[
@@ -546,9 +555,9 @@
                         common + (share,),
                     )
                 else:
-                    faces, first, second = call(
+                    faces, first, second, *ahead = call(
                         functools.partial(middle_window, count, False),
-                        [faces_shape, message, message],
+                        [faces_shape, message, message] + [faces_shape] * final,
                         common + (near, near_link),
                     )
             elif not ending:
@@ -565,7 +574,7 @@
     (parts,) = call(
         functools.partial(means_payload, count),
         [sds((slices * blocks, scenarios), F32)],
-        (ff, y, rhs, link, faces, near, near_link, near_column, mass, base_mean, mean, op),
+        (rhs, link, faces, ahead[0], near, near_link, near_column, mass, base_mean, mean, op),
     )
     parts = parts.reshape(slices * sub, count, scenarios)
     parts = lax.all_to_all(parts, ("cuts", "sub"), 0, 0, tiled=True)

time: 83.6 us -> 83.5 us (level)
  no operation moved by 1% of the time
where the time goes in v4:
time: 83.5 us; the launch traced here: 83.3 us
  waiting for transfers between devices  36 us (43%)
  starting transfers between devices  28.8 us (34%)
  Pallas kernels  17.5 us (21%)
    ppermute x8, waiting for transfers between devices, exchange(): near = lax.ppermute(first, ('cuts', 'sub'), pairs)  32.2 us
    ppermute x8, starting transfers between devices, exchange(): near = lax.ppermute(first, ('cuts', 'sub'), pairs)  22 us
    pallas_call x18, Pallas kernels, call(): pl.pallas_call(body, out_shape=out_shape, in_specs=[hbm if k in stay else...  17.5 us
    all_to_all x1, starting transfers between devices, on_device(): parts = lax.all_to_all(parts, ('cuts', 'sub'), 0, 0, tiled=True)  5.14 us
    all_to_all x1, waiting for transfers between devices, on_device(): parts = lax.all_to_all(parts, ('cuts', 'sub'), 0, 0, tiled=True)  3.73 us
  transfers between devices with their start and end apart: 20, of which 8 were waited for; matrix products, arithmetic and copies ran while one was open for 0% of the time, Pallas kernels for 13%

profile of v4, /device:TPU:0, one launch (start us, length us, event | category | flops | bytes accessed | tf_op | source)
XLA Modules:
  0.0 83.3 jit_solution(9619406942482020017)
XLA Ops:
  0.0 1.9 %shard_map.73 = (f32[2,256,128]{2,1,0:T(8,128)S(1)}, f32[4,128,128]{2,1,0:T(8,128)S(1)}, f32[2,256,128]{2,1,0:T(8,128)S(1)}, f32[392,128]{1,0:T(8,128)S(1)}, f32[392,128]{1,0:T(8,128)S(1)}) custom-call(f32[2,512,128]{2,1,0:T(8,128)} %bitcast.3, bf16[2,512,128]{2,1,0:T(8,128)(2,1)} %source_hbm.3, bf16[2,512,512]{2,1,0:T(8,128)(2,1)} %inverse_hbm.3, ...), custom_call_target="tpu_custom_call" | custom-call | flops 268435456 | bytes 3026944 | tf_op jit(solution)/shard_map/pallas_call | solution.py:34
  1.9 3.0 %collective-permute-start = (f32[392,128]{1,0:T(8,128)S(1)}, f32[392,128]{1,0:T(8,128)S(1)}, u32[]{:S(2)}, u32[]{:S(2)}) collective-permute-start(f32[392,128]{1,0:T(8,128)S(1)} %get-tuple-element.60), channel_id=1, source_target_pairs={{0,1},{1,0},{2,3},{3,2},{4,5},{5,4},{6,7},{7,6},{8,9},{9,8},{10,11... | collective-permute-start | bytes 602120 | tf_op jit(solution)/shard_map/ppermute | solution.py:464
  4.9 2.2 %shard_map.74 = (bf16[2,256,256]{2,1,0:T(8,128)(2,1)S(1)}, bf16[2,256,256]{2,1,0:T(8,128)(2,1)S(1)}, bf16[2,256,256]{2,1,0:T(8,128)(2,1)S(1)}, bf16[2,256,256]{2...) custom-call(f32[2,512,128]{2,1,0:T(8,128)} %bitcast.4, ...), custom_call_target="tpu_custom_call" | custom-call | flops 268435456 | bytes 4459520 | tf_op jit(solution)/shard_map/pallas_call | solution.py:34
  7.5 6.0 %collective-permute-done.refs_0_ = f32[392,128]{1,0:T(8,128)S(1)} collective-permute-done((f32[392,128]{1,0:T(8,128)S(1)}, f32[392,128]{1,0:T(8,128)S(1)}, u32[]{:S(2)}, u32[]{:S(2)}) %collective-permute-start) | collective-permute-done | bytes 200736 | tf_op jit(solution)/shard_map/ppermute | solution.py:464
  13.5 0.7 shard_map.76
  14.2 2.5 %collective-permute-start.2 = (f32[264,128]{1,0:T(8,128)S(1)}, f32[264,128]{1,0:T(8,128)S(1)}, u32[]{:S(2)}, u32[]{:S(2)}) collective-permute-start(f32[264,128]{1,0:T(8,128)S(1)} %get-tuple-element.69), channel_id=1, source_target_pairs={{0,1},{1,0},{2,3},{3,2},{4,5},{5,4},{6,7},{7,6},{8,9},{9,8},{10,11... | collective-permute-start | bytes 405512 | tf_op jit(solution)/shard_map/ppermute | solution.py:464
  17.0 4.6 %collective-permute-done.2.first_ref = f32[264,128]{1,0:T(8,128)S(1)} collective-permute-done((f32[264,128]{1,0:T(8,128)S(1)}, f32[264,128]{1,0:T(8,128)S(1)}, u32[]{:S(2)}, u32[]{:S(2)}) %collective-permute-start.2) | collective-permute-done | bytes 135200 | tf_op jit(solution)/shard_map/ppermute | solution.py:464
  21.6 1.0 %shard_map.78 = (f32[2,256,128]{2,1,0:T(8,128)S(1)}, f32[256,128]{1,0:T(8,128)S(1)}, f32[256,128]{1,0:T(8,128)S(1)}, f32[2,256,128]{2,1,0:T(8,128)S(1)}, f32[2,2...) custom-call(f32[264,128]{1,0:T(8,128)S(1)} %collective-permute-done.2.first_ref, ...), custom_call_target="tpu_custom_call" | custom-call | flops 268435456 | bytes 4931584 | tf_op jit(solution)/shard_map/pallas_call | solution.py:34
  22.6 2.5 %collective-permute-start.4 = (f32[256,128]{1,0:T(8,128)S(1)}, f32[256,128]{1,0:T(8,128)S(1)}, u32[]{:S(2)}, u32[]{:S(2)}) collective-permute-start(f32[256,128]{1,0:T(8,128)S(1)} %get-tuple-element.80), channel_id=1, source_target_pairs={{0,1},{1,0},{2,3},{3,2},{4,5},{5,4},{6,7},{7,6},{8,9},{9,8},{10,11... | collective-permute-start | bytes 393224 | tf_op jit(solution)/shard_map/ppermute | solution.py:464
  25.2 4.7 %collective-permute-done.4.refs_0_ = f32[256,128]{1,0:T(8,128)S(1)} collective-permute-done((f32[256,128]{1,0:T(8,128)S(1)}, f32[256,128]{1,0:T(8,128)S(1)}, u32[]{:S(2)}, u32[]{:S(2)}) %collective-permute-start.4) | collective-permute-done | bytes 131104 | tf_op jit(solution)/shard_map/ppermute | solution.py:464
  29.9 0.6 shard_map.79
  30.5 2.5 %collective-permute-start.6 = (f32[256,128]{1,0:T(8,128)S(1)}, f32[256,128]{1,0:T(8,128)S(1)}, u32[]{:S(2)}, u32[]{:S(2)}) collective-permute-start(f32[256,128]{1,0:T(8,128)S(1)} %get-tuple-element.85), channel_id=1, source_target_pairs={{0,1},{1,0},{2,3},{3,2},{4,5},{5,4},{6,7},{7,6},{8,9},{9,8},{10,11... | collective-permute-start | bytes 393224 | tf_op jit(solution)/shard_map/ppermute | solution.py:464
  33.4 4.5 %collective-permute-done.6.first_ref = f32[256,128]{1,0:T(8,128)S(1)} collective-permute-done((f32[256,128]{1,0:T(8,128)S(1)}, f32[256,128]{1,0:T(8,128)S(1)}, u32[]{:S(2)}, u32[]{:S(2)}) %collective-permute-start.6) | collective-permute-done | bytes 131104 | tf_op jit(solution)/shard_map/ppermute | solution.py:464
  37.9 1.0 %shard_map.81 = (f32[2,256,128]{2,1,0:T(8,128)S(1)}, f32[256,128]{1,0:T(8,128)S(1)}, f32[256,128]{1,0:T(8,128)S(1)}, f32[2,256,128]{2,1,0:T(8,128)S(1)}, f32[2,2...) custom-call(f32[256,128]{1,0:T(8,128)S(1)} %collective-permute-done.6.first_ref, ...), custom_call_target="tpu_custom_call" | custom-call | flops 268435456 | bytes 4915200 | tf_op jit(solution)/shard_map/pallas_call | solution.py:34
  38.9 2.5 %collective-permute-start.8 = (f32[256,128]{1,0:T(8,128)S(1)}, f32[256,128]{1,0:T(8,128)S(1)}, u32[]{:S(2)}, u32[]{:S(2)}) collective-permute-start(f32[256,128]{1,0:T(8,128)S(1)} %get-tuple-element.89), channel_id=1, source_target_pairs={{0,1},{1,0},{2,3},{3,2},{4,5},{5,4},{6,7},{7,6},{8,9},{9,8},{10,11... | collective-permute-start | bytes 393224 | tf_op jit(solution)/shard_map/ppermute | solution.py:464
  41.4 4.8 %collective-permute-done.8.refs_0_ = f32[256,128]{1,0:T(8,128)S(1)} collective-permute-done((f32[256,128]{1,0:T(8,128)S(1)}, f32[256,128]{1,0:T(8,128)S(1)}, u32[]{:S(2)}, u32[]{:S(2)}) %collective-permute-start.8) | collective-permute-done | bytes 131104 | tf_op jit(solution)/shard_map/ppermute | solution.py:464
  46.2 0.6 shard_map.82
  46.8 2.5 %collective-permute-start.10 = (f32[256,128]{1,0:T(8,128)S(1)}, f32[256,128]{1,0:T(8,128)S(1)}, u32[]{:S(2)}, u32[]{:S(2)}) collective-permute-start(f32[256,128]{1,0:T(8,128)S(1)} %get-tuple-element.94), channel_id=1, source_target_pairs={{0,1},{1,0},{2,3},{3,2},{4,5},{5,4},{6,7},{7,6},{8,9},{9,8},{10,11... | collective-permute-start | bytes 393224 | tf_op jit(solution)/shard_map/ppermute | solution.py:464
  49.6 4.5 %collective-permute-done.10.first_ref = f32[256,128]{1,0:T(8,128)S(1)} collective-permute-done((f32[256,128]{1,0:T(8,128)S(1)}, f32[256,128]{1,0:T(8,128)S(1)}, u32[]{:S(2)}, u32[]{:S(2)}) %collective-permute-start.10) | collective-permute-done | bytes 131104 | tf_op jit(solution)/shard_map/ppermute | solution.py:464
  54.1 1.0 %shard_map.84 = (f32[2,256,128]{2,1,0:T(8,128)S(1)}, f32[256,128]{1,0:T(8,128)S(1)}, f32[256,128]{1,0:T(8,128)S(1)}, f32[2,256,128]{2,1,0:T(8,128)S(1)}, f32[2,2...) custom-call(f32[256,128]{1,0:T(8,128)S(1)} %collective-permute-done.10.first_ref, ...), custom_call_target="tpu_custom_call" | custom-call | flops 268435456 | bytes 4915200 | tf_op jit(solution)/shard_map/pallas_call | solution.py:34
  55.1 2.5 %collective-permute-start.12 = (f32[256,128]{1,0:T(8,128)S(1)}, f32[256,128]{1,0:T(8,128)S(1)}, u32[]{:S(2)}, u32[]{:S(2)}) collective-permute-start(f32[256,128]{1,0:T(8,128)S(1)} %get-tuple-element.99), channel_id=1, source_target_pairs={{0,1},{1,0},{2,3},{3,2},{4,5},{5,4},{6,7},{7,6},{8,9},{9,8},{10,11... | collective-permute-start | bytes 393224 | tf_op jit(solution)/shard_map/ppermute | solution.py:464
  57.6 0.5 collective-permute-start.16
  58.1 1.1 %collective-permute-start.18 = (f32[2,256,128]{2,1,0:T(8,128)S(1)}, f32[2,256,128]{2,1,0:T(8,128)S(1)}, u32[]{:S(2)}, u32[]{:S(2)}) collective-permute-start(f32[2,256,128]{2,1,0:T(8,128)S(1)} %get-tuple-element.105.mid_ref), channel_id=1, source_target_pairs={{0,8},{8,16},{16,24},{24,0},{1,9},{9,17},{17,25},{25,1},{2,10},{10... | collective-permute-start | bytes 786440 | tf_op jit(solution)/shard_map/ppermute | solution.py:537
  59.2 3.2 %collective-permute-done.12.refs_0_ = f32[256,128]{1,0:T(8,128)S(1)} collective-permute-done((f32[256,128]{1,0:T(8,128)S(1)}, f32[256,128]{1,0:T(8,128)S(1)}, u32[]{:S(2)}, u32[]{:S(2)}) %collective-permute-start.12) | collective-permute-done | bytes 131104 | tf_op jit(solution)/shard_map/ppermute | solution.py:464
  62.4 0.6 shard_map.85
  63.1 3.7 %collective-permute-start.14 = (f32[256,128]{1,0:T(8,128)S(1)}, f32[256,128]{1,0:T(8,128)S(1)}, u32[]{:S(2)}, u32[]{:S(2)}) collective-permute-start(f32[256,128]{1,0:T(8,128)S(1)} %get-tuple-element.111), channel_id=1, source_target_pairs={{0,9},{1,8},{2,11},{3,10},{4,13},{5,12},{6,15},{7,14},{8,17},{9,16... | collective-permute-start | bytes 393224 | tf_op jit(solution)/shard_map/ppermute | solution.py:464
  66.8 3.0 %shard_map.87.op_ref = f32[8,64,128]{2,1,0:T(8,128)S(1)} custom-call(s32[16]{0:T(128)} %partner_hbm.1, f32[16]{0:T(128)} %cond_hbm.1), custom_call_target="tpu_custom_call" | custom-call | flops 268435456 | bytes 262272 | tf_op jit(solution)/shard_map/pallas_call | solution.py:34
  70.1 0.8 shard_map.88
  70.9 5.1 %all-to-all-start = ((f32[32,2,128]{2,1,0:T(2,128)}), f32[32,2,128]{2,1,0:T(2,128)S(1)}, u32[]{:S(2)}, u32[]{:S(2)}) async-start(f32[32,2,128]{2,1,0:T(2,128)} %bitcast.1), calls=%async_computation | async-start | bytes 65536 | tf_op jit(solution)/shard_map/all_to_all | solution.py:580
  76.1 0.7 copy-done
  76.9 2.6 %shard_map.89 = (f32[2,512,128]{2,1,0:T(8,128)S(1)}, f32[2,512,128]{2,1,0:T(8,128)}) custom-call(f32[256,128]{1,0:T(8,128)S(1)} %collective-permute-done.14.first_ref, f32[256,128]{1,0:T(8,128)S(1)} %collective-permute-done.15.second_ref, bf16[2,256,256]{2,1,0:T(8,128)(2,1)S(1)} %get-tuple-element.62.ff_ref.refs_2_, f32[2,256,128]{2,1,0:T(8,128)} %copy-done, ...), custom_call_target="tpu_custom_call" | custom-call | flops 268435456 | bytes 4128768 | tf_op jit(solution)/shard_map/pallas_call | solution.py:34
  79.5 3.7 %all-to-all-done.parts_ref = f32[32,2,128]{2,1,0:T(2,128)S(1)} async-done(((f32[32,2,128]{2,1,0:T(2,128)}), f32[32,2,128]{2,1,0:T(2,128)S(1)}, u32[]{:S(2)}, u32[]{:S(2)}) %all-to-all-start) | async-done | bytes 32800 | tf_op jit(solution)/shard_map/all_to_all | solution.py:580
  (30 shorter events, 1.6 us)
Async XLA Ops:
  1.9 11.6 %collective-permute-start = (f32[392,128]{1,0:T(8,128)S(1)}, f32[392,128]{1,0:T(8,128)S(1)}, u32[]{:S(2)}, u32[]{:S(2)}) collective-permute-start(f32[392,128]{1,0:T(8,128)S(1)} %get-tuple-element.60), channel_id=1, source_target_pairs={{0,1},{1,0},{2,3},{3,2},{4,5},{5,4},{6,7},{7,6},{8,9},{9,8},{10,11... | collective-permute-start | bytes 602120 | tf_op jit(solution)/shard_map/ppermute | solution.py:464
  4.9 8.5 %collective-permute-start.1 = (f32[392,128]{1,0:T(8,128)S(1)}, f32[392,128]{1,0:T(8,128)S(1)}, u32[]{:S(2)}, u32[]{:S(2)}) collective-permute-start(f32[392,128]{1,0:T(8,128)S(1)} %get-tuple-element.61), channel_id=1, source_target_pairs={{0,8},{1,2},{2,1},{3,4},{4,3},{5,6},{6,5},{7,15},{8,0},{9,10},{10,... | collective-permute-start | bytes 602120 | tf_op jit(solution)/shard_map/ppermute | solution.py:463
  14.2 7.4 %collective-permute-start.2 = (f32[264,128]{1,0:T(8,128)S(1)}, f32[264,128]{1,0:T(8,128)S(1)}, u32[]{:S(2)}, u32[]{:S(2)}) collective-permute-start(f32[264,128]{1,0:T(8,128)S(1)} %get-tuple-element.69), channel_id=1, source_target_pairs={{0,1},{1,0},{2,3},{3,2},{4,5},{5,4},{6,7},{7,6},{8,9},{9,8},{10,11... | collective-permute-start | bytes 405512 | tf_op jit(solution)/shard_map/ppermute | solution.py:464
  16.7 4.9 %collective-permute-start.3 = (f32[264,128]{1,0:T(8,128)S(1)}, f32[264,128]{1,0:T(8,128)S(1)}, u32[]{:S(2)}, u32[]{:S(2)}) collective-permute-start(f32[264,128]{1,0:T(8,128)S(1)} %get-tuple-element.70), channel_id=1, source_target_pairs={{0,8},{1,2},{2,1},{3,4},{4,3},{5,6},{6,5},{7,15},{8,0},{9,10},{10,... | collective-permute-start | bytes 405512 | tf_op jit(solution)/shard_map/ppermute | solution.py:463
  22.6 7.3 %collective-permute-start.4 = (f32[256,128]{1,0:T(8,128)S(1)}, f32[256,128]{1,0:T(8,128)S(1)}, u32[]{:S(2)}, u32[]{:S(2)}) collective-permute-start(f32[256,128]{1,0:T(8,128)S(1)} %get-tuple-element.80), channel_id=1, source_target_pairs={{0,1},{1,0},{2,3},{3,2},{4,5},{5,4},{6,7},{7,6},{8,9},{9,8},{10,11... | collective-permute-start | bytes 393224 | tf_op jit(solution)/shard_map/ppermute | solution.py:464
  25.2 4.8 %collective-permute-start.5 = (f32[256,128]{1,0:T(8,128)S(1)}, f32[256,128]{1,0:T(8,128)S(1)}, u32[]{:S(2)}, u32[]{:S(2)}) collective-permute-start(f32[256,128]{1,0:T(8,128)S(1)} %get-tuple-element.81), channel_id=1, source_target_pairs={{0,8},{1,2},{2,1},{3,4},{4,3},{5,6},{6,5},{7,15},{8,0},{9,10},{10,... | collective-permute-start | bytes 393224 | tf_op jit(solution)/shard_map/ppermute | solution.py:463
  30.5 7.3 %collective-permute-start.6 = (f32[256,128]{1,0:T(8,128)S(1)}, f32[256,128]{1,0:T(8,128)S(1)}, u32[]{:S(2)}, u32[]{:S(2)}) collective-permute-start(f32[256,128]{1,0:T(8,128)S(1)} %get-tuple-element.85), channel_id=1, source_target_pairs={{0,1},{1,0},{2,3},{3,2},{4,5},{5,4},{6,7},{7,6},{8,9},{9,8},{10,11... | collective-permute-start | bytes 393224 | tf_op jit(solution)/shard_map/ppermute | solution.py:464
  33.1 4.8 %collective-permute-start.7 = (f32[256,128]{1,0:T(8,128)S(1)}, f32[256,128]{1,0:T(8,128)S(1)}, u32[]{:S(2)}, u32[]{:S(2)}) collective-permute-start(f32[256,128]{1,0:T(8,128)S(1)} %get-tuple-element.86), channel_id=1, source_target_pairs={{0,8},{1,2},{2,1},{3,4},{4,3},{5,6},{6,5},{7,15},{8,0},{9,10},{10,... | collective-permute-start | bytes 393224 | tf_op jit(solution)/shard_map/ppermute | solution.py:463
  38.9 7.3 %collective-permute-start.8 = (f32[256,128]{1,0:T(8,128)S(1)}, f32[256,128]{1,0:T(8,128)S(1)}, u32[]{:S(2)}, u32[]{:S(2)}) collective-permute-start(f32[256,128]{1,0:T(8,128)S(1)} %get-tuple-element.89), channel_id=1, source_target_pairs={{0,1},{1,0},{2,3},{3,2},{4,5},{5,4},{6,7},{7,6},{8,9},{9,8},{10,11... | collective-permute-start | bytes 393224 | tf_op jit(solution)/shard_map/ppermute | solution.py:464
  41.4 4.8 %collective-permute-start.9 = (f32[256,128]{1,0:T(8,128)S(1)}, f32[256,128]{1,0:T(8,128)S(1)}, u32[]{:S(2)}, u32[]{:S(2)}) collective-permute-start(f32[256,128]{1,0:T(8,128)S(1)} %get-tuple-element.90), channel_id=1, source_target_pairs={{0,8},{1,2},{2,1},{3,4},{4,3},{5,6},{6,5},{7,15},{8,0},{9,10},{10,... | collective-permute-start | bytes 393224 | tf_op jit(solution)/shard_map/ppermute | solution.py:463
  46.8 7.3 %collective-permute-start.10 = (f32[256,128]{1,0:T(8,128)S(1)}, f32[256,128]{1,0:T(8,128)S(1)}, u32[]{:S(2)}, u32[]{:S(2)}) collective-permute-start(f32[256,128]{1,0:T(8,128)S(1)} %get-tuple-element.94), channel_id=1, source_target_pairs={{0,1},{1,0},{2,3},{3,2},{4,5},{5,4},{6,7},{7,6},{8,9},{9,8},{10,11... | collective-permute-start | bytes 393224 | tf_op jit(solution)/shard_map/ppermute | solution.py:464
  49.3 4.8 %collective-permute-start.11 = (f32[256,128]{1,0:T(8,128)S(1)}, f32[256,128]{1,0:T(8,128)S(1)}, u32[]{:S(2)}, u32[]{:S(2)}) collective-permute-start(f32[256,128]{1,0:T(8,128)S(1)} %get-tuple-element.95), channel_id=1, source_target_pairs={{0,8},{1,2},{2,1},{3,4},{4,3},{5,6},{6,5},{7,15},{8,0},{9,10},{10,... | collective-permute-start | bytes 393224 | tf_op jit(solution)/shard_map/ppermute | solution.py:463
  55.1 7.3 %collective-permute-start.12 = (f32[256,128]{1,0:T(8,128)S(1)}, f32[256,128]{1,0:T(8,128)S(1)}, u32[]{:S(2)}, u32[]{:S(2)}) collective-permute-start(f32[256,128]{1,0:T(8,128)S(1)} %get-tuple-element.99), channel_id=1, source_target_pairs={{0,1},{1,0},{2,3},{3,2},{4,5},{5,4},{6,7},{7,6},{8,9},{9,8},{10,11... | collective-permute-start | bytes 393224 | tf_op jit(solution)/shard_map/ppermute | solution.py:464
  57.6 4.8 %collective-permute-start.13 = (f32[256,128]{1,0:T(8,128)S(1)}, f32[256,128]{1,0:T(8,128)S(1)}, u32[]{:S(2)}, u32[]{:S(2)}) collective-permute-start(f32[256,128]{1,0:T(8,128)S(1)} %get-tuple-element.100), channel_id=1, source_target_pairs={{0,8},{1,2},{2,1},{3,4},{4,3},{5,6},{6,5},{7,15},{8,0},{9,10},{10,... | collective-permute-start | bytes 393224 | tf_op jit(solution)/shard_map/ppermute | solution.py:463
  57.6 18.4 %collective-permute-start.16 = (f32[2,256,128]{2,1,0:T(8,128)S(1)}, f32[2,256,128]{2,1,0:T(8,128)S(1)}, u32[]{:S(2)}, u32[]{:S(2)}) collective-permute-start(f32[2,256,128]{2,1,0:T(8,128)S(1)} %get-tuple-element.98.refs_4_.rhs_ref), channel_id=1, source_target_pairs={{0,8},{8,16},{16,24},{24,0},{1,9},{9,17},{17,25},{25,1},{2,10},{10... | collective-permute-start | bytes 786440 | tf_op jit(solution)/shard_map/ppermute | solution.py:538
  58.1 17.9 %collective-permute-start.18 = (f32[2,256,128]{2,1,0:T(8,128)S(1)}, f32[2,256,128]{2,1,0:T(8,128)S(1)}, u32[]{:S(2)}, u32[]{:S(2)}) collective-permute-start(f32[2,256,128]{2,1,0:T(8,128)S(1)} %get-tuple-element.105.mid_ref), channel_id=1, source_target_pairs={{0,8},{8,16},{16,24},{24,0},{1,9},{9,17},{17,25},{25,1},{2,10},{10... | collective-permute-start | bytes 786440 | tf_op jit(solution)/shard_map/ppermute | solution.py:537
  63.0 13.1 %collective-permute-start.17 = (f32[2,256,128]{2,1,0:T(8,128)S(1)}, f32[2,256,128]{2,1,0:T(8,128)}, u32[]{:S(2)}, u32[]{:S(2)}) collective-permute-start(f32[2,256,128]{2,1,0:T(8,128)S(1)} %get-tuple-element.103.faces_ref), channel_id=1, source_target_pairs={{0,8},{8,16},{16,24},{24,0},{1,9},{9,17},{17,25},{25,1},{2,10},{10... | collective-permute-start | bytes 786440 | tf_op jit(solution)/shard_map/ppermute | solution.py:573
  63.1 12.9 %collective-permute-start.14 = (f32[256,128]{1,0:T(8,128)S(1)}, f32[256,128]{1,0:T(8,128)S(1)}, u32[]{:S(2)}, u32[]{:S(2)}) collective-permute-start(f32[256,128]{1,0:T(8,128)S(1)} %get-tuple-element.111), channel_id=1, source_target_pairs={{0,9},{1,8},{2,11},{3,10},{4,13},{5,12},{6,15},{7,14},{8,17},{9,16... | collective-permute-start | bytes 393224 | tf_op jit(solution)/shard_map/ppermute | solution.py:464
  66.8 9.3 %collective-permute-start.15 = (f32[256,128]{1,0:T(8,128)S(1)}, f32[256,128]{1,0:T(8,128)S(1)}, u32[]{:S(2)}, u32[]{:S(2)}) collective-permute-start(f32[256,128]{1,0:T(8,128)S(1)} %get-tuple-element.112), channel_id=1, source_target_pairs={{0,8},{1,10},{2,9},{3,12},{4,11},{5,14},{6,13},{7,15},{8,16},{9,18... | collective-permute-start | bytes 393224 | tf_op jit(solution)/shard_map/ppermute | solution.py:463
  70.9 12.3 %all-to-all-start = ((f32[32,2,128]{2,1,0:T(2,128)}), f32[32,2,128]{2,1,0:T(2,128)S(1)}, u32[]{:S(2)}, u32[]{:S(2)}) async-start(f32[32,2,128]{2,1,0:T(2,128)} %bitcast.1), calls=%async_computation | async-start | bytes 65536 | tf_op jit(solution)/shard_map/all_to_all | solution.py:580
  76.1 0.7 copy-start
  76.1 0.8 copy-start.1

commit v5 on v4

--- a/solution.py
+++ b/solution.py
@@ -64,14 +64,14 @@
     return vectors, new_low, new_up
 
 
-def outgoing(count, ff_ref, y_ref, rhs_ref, link_ref, low, up):
+def outgoing(count, ff_ref, y_low, y_up, rhs_ref, link_ref, low, up):
     face = low[0].shape[0]
     last = count - 1
     zero = jnp.zeros_like(low[0])
     v = jnp.concatenate(face_vector(last, count, rhs_ref, link_ref, low, up, zero, zero), axis=0)
-    next_up = y_ref[last, face:] + dot(ff_ref[last, face:], v)
+    next_up = y_up + dot(ff_ref[last, face:], v)
     v = jnp.concatenate(face_vector(0, count, rhs_ref, link_ref, low, up, zero, zero), axis=0)
-    next_low = y_ref[0, :face] + dot(ff_ref[0, :face], v)
+    next_low = y_low + dot(ff_ref[0, :face], v)
     return (up[last], next_up), (low[0], next_low)
 
 
@@ -176,7 +176,7 @@
 
 
 def prepare_rest(count, start_hbm, source_hbm, inverse_hbm, map_hbm,
-                 ff_ref, fm_ref, pf_ref, rf_ref, pm_ref, rm_ref, mid_ref, wells_ref, y_ref, mean_ref,
+                 ff_ref, fm_ref, pf_ref, rf_ref, pm_ref, rm_ref, mid_ref, wells_ref, mean_ref,
                  start_ref, source_ref, inverse_ref, map_ref, sems):
     for copy in read_all(
         (start_hbm, source_hbm, inverse_hbm, map_hbm), (start_ref, source_ref, inverse_ref, map_ref), sems
@@ -205,7 +205,6 @@
         mid_ref[i] = start_ref[i, inner] + wells
         wells_ref[i, 2 * face :] = wells
         mean_ref[i : i + 1] = jnp.sum(start_ref[i], axis=0, keepdims=True) / width
-        y_ref[i] = dot(fm_ref[i], mid_ref[i].astype(BF16))
 
 
 def load_faces(count, faces_ref):
@@ -251,7 +250,7 @@
             next_faces[0][i, face:] = next_up[i]
         upward, downward = (up[-1], next_up[-1]), (low[0], next_low[0])
     else:
-        upward, downward = outgoing(count, ff_ref, y_ref, rhs_ref, link_ref, low, up)
+        upward, downward = outgoing(count, ff_ref, y_ref[0, :face], y_ref[count - 1, face:], rhs_ref, link_ref, low, up)
     if opening:
         upward += (share_ref[1],)
         downward += (share_ref[0],)
@@ -260,7 +259,7 @@
 
 def step_window(count, opening, first_ref, second_ref, ff_ref, y_ref, rhs_ref, link_ref, faces_ref, near_ref,
                 near_link_ref, fm_ref, pf_ref, rf_ref, base_ref, source_ref,
-                new_faces, out_first, out_second, new_rhs, new_mid, new_y, *near_share):
+                new_faces, out_first, out_second, new_rhs, new_mid, *near_share):
     face = faces_ref.shape[1] // 2
     if opening:
         for k, part in enumerate(received(first_ref, second_ref, slice(2 * face, 2 * face + 8))):
@@ -275,16 +274,20 @@
         new_rhs[i] = base_ref[i, :cut] + dot(pf_ref[i], vectors[i]) + source_ref[i, :cut]
         rhs = base_ref[i, cut:] + dot(rf_ref[i], vectors[i]) + source_ref[i, cut:]
         new_mid[i] = rhs
-        new_y[i] = dot(fm_ref[i], rhs.astype(BF16))
-    store_messages(*outgoing(count, ff_ref, new_y, new_rhs, link_ref, low, up), out_first, out_second)
-
-
-def inner_base(count, mid_ref, pm_ref, rm_ref, base_ref):
+        if i == 0:
+            y_low = dot(fm_ref[i, :face], rhs.astype(BF16))
+        if i == count - 1:
+            y_up = dot(fm_ref[i, face:], rhs.astype(BF16))
+    store_messages(*outgoing(count, ff_ref, y_low, y_up, new_rhs, link_ref, low, up), out_first, out_second)
+
+
+def inner_base(count, mid_ref, pm_ref, rm_ref, fm_ref, base_ref, y_ref):
     for i in range(count):
         cut = pm_ref.shape[1]
         v = mid_ref[i].astype(BF16)
         base_ref[i, :cut] = dot(pm_ref[i], v)
         base_ref[i, cut:] = dot(rm_ref[i], v)
+        y_ref[i] = dot(fm_ref[i], v)
 
 
 def shares(count, ff_ref, rf_ref, link_ref, mass_ref, share_ref):
@@ -308,15 +311,18 @@
         share_ref[k] = jnp.where(iota(one.shape, 0) == 0, one, two)
 
 
-def end_mean(count, mid_ref, rm_ref, y_ref, near_share_ref, out_ref, column_ref):
+def end_mean(count, mid_ref, rm_ref, fm_ref, near_share_ref, out_ref, column_ref, y_ref):
     face = y_ref.shape[1] // 2
     for k in range(2):
         for j in range(2):
             line = jnp.broadcast_to(near_share_ref[k, j : j + 1], (face, face))
             column_ref[2 * k + j] = transpose(line)
     for i in range(count):
-        inner = dot(rm_ref[i], mid_ref[i].astype(BF16))
-        total = jnp.sum(y_ref[i], axis=0, keepdims=True) + jnp.sum(inner, axis=0, keepdims=True)
+        v = mid_ref[i].astype(BF16)
+        y = dot(fm_ref[i], v)
+        y_ref[i] = y
+        inner = dot(rm_ref[i], v)
+        total = jnp.sum(y, axis=0, keepdims=True) + jnp.sum(inner, axis=0, keepdims=True)
         out_ref[i : i + 1] = total / (2 * face + rm_ref.shape[1])
 
 
@@ -493,7 +499,7 @@
         stay=range(5),
         scratch=buffers + [row, row] + tables + [pltpu.SemaphoreType.DMA((6,))],
     )
-    ff, fm, pf, rf, pm, rm, mid, wells, y, mean = call(
+    ff, fm, pf, rf, pm, rm, mid, wells, mean = call(
         functools.partial(prepare_rest, count),
         [
             sds((count, 2 * face, 2 * face), BF16),
@@ -504,7 +510,6 @@
             sds((count, inner, inner), BF16),
             mid_shape,
             rhs_shape,
-            faces_shape,
             sds((count, scenarios), F32),
         ],
         held[:4],
@@ -536,13 +541,13 @@
         if final:
             taken_mid = lax.ppermute(mid, "cuts", ring)
             taken_rhs = lax.ppermute(rhs, "cuts", ring)
-            base_mean, near_column = call(
+            base_mean, near_column, y = call(
                 functools.partial(end_mean, count),
-                [sds((count, scenarios), F32), sds((4, face, scenarios), F32)],
-                (mid, rm, y, near_share),
+                [sds((count, scenarios), F32), sds((4, face, scenarios), F32), faces_shape],
+                (mid, rm, fm, near_share),
             )
         else:
-            (base,) = call(functools.partial(inner_base, count), [rhs_shape], (mid, pm, rm))
+            base, y = call(functools.partial(inner_base, count), [rhs_shape, faces_shape], (mid, pm, rm, fm))
         for turn in range(0, SWEEPS, 2):
             ending = final and turn == SWEEPS - 2
             first, second = exchange(first, second, 1 if ending else 0)
@@ -561,15 +566,15 @@
                         common + (near, near_link),
                     )
             elif not ending:
-                outs = [faces_shape, message, message, faces_shape, mid_shape, faces_shape]
+                outs = [faces_shape, message, message, faces_shape, mid_shape]
                 outs = call(
                     functools.partial(step_window, count, step == 0),
                     outs + [share_shape] if step == 0 else outs,
                     common + (near, near_link, fm, pf, rf, base, wells),
                 )
-                faces, first, second, rhs, mid, y = outs[:6]
+                faces, first, second, rhs, mid = outs[:5]
                 if step == 0:
-                    near_share = outs[6]
+                    near_share = outs[5]
     taken_faces = lax.ppermute(faces, "cuts", ring)
     (parts,) = call(
         functools.partial(means_payload, count),

time: 83.5 us -> 82.6 us (0.989)
  no operation moved by 1% of the time
where the time goes in v5:
time: 82.6 us; the launch traced here: 82.3 us
  waiting for transfers between devices  35.5 us (43%)
  starting transfers between devices  28.8 us (35%)
  Pallas kernels  17.1 us (21%)
    ppermute x8, waiting for transfers between devices, exchange(): near = lax.ppermute(first, ('cuts', 'sub'), pairs)  31.8 us
    ppermute x8, starting transfers between devices, exchange(): near = lax.ppermute(first, ('cuts', 'sub'), pairs)  22 us
    pallas_call x18, Pallas kernels, call(): pl.pallas_call(body, out_shape=out_shape, in_specs=[hbm if k in stay else...  17.1 us
    all_to_all x1, starting transfers between devices, on_device(): parts = lax.all_to_all(parts, ('cuts', 'sub'), 0, 0, tiled=True)  5.14 us
    all_to_all x1, waiting for transfers between devices, on_device(): parts = lax.all_to_all(parts, ('cuts', 'sub'), 0, 0, tiled=True)  3.75 us
  transfers between devices with their start and end apart: 20, of which 8 were waited for; matrix products, arithmetic and copies ran while one was open for 0% of the time, Pallas kernels for 13%

profile of v5, /device:TPU:0, one launch (start us, length us, event | category | flops | bytes accessed | tf_op | source)
XLA Modules:
  0.0 82.3 jit_solution(960620204525431873)
XLA Ops:
  0.0 1.9 %shard_map.73 = (f32[2,256,128]{2,1,0:T(8,128)S(1)}, f32[4,128,128]{2,1,0:T(8,128)S(1)}, f32[2,256,128]{2,1,0:T(8,128)S(1)}, f32[392,128]{1,0:T(8,128)S(1)}, f32[392,128]{1,0:T(8,128)S(1)}) custom-call(f32[2,512,128]{2,1,0:T(8,128)} %bitcast.3, bf16[2,512,128]{2,1,0:T(8,128)(2,1)} %source_hbm.3, bf16[2,512,512]{2,1,0:T(8,128)(2,1)} %inverse_hbm.3, ...), custom_call_target="tpu_custom_call" | custom-call | flops 268435456 | bytes 3026944 | tf_op jit(solution)/shard_map/pallas_call | solution.py:34
  1.9 3.0 %collective-permute-start = (f32[392,128]{1,0:T(8,128)S(1)}, f32[392,128]{1,0:T(8,128)S(1)}, u32[]{:S(2)}, u32[]{:S(2)}) collective-permute-start(f32[392,128]{1,0:T(8,128)S(1)} %get-tuple-element.63), channel_id=1, source_target_pairs={{0,1},{1,0},{2,3},{3,2},{4,5},{5,4},{6,7},{7,6},{8,9},{9,8},{10,11... | collective-permute-start | bytes 602120 | tf_op jit(solution)/shard_map/ppermute | solution.py:470
  4.9 2.2 %shard_map.74 = (bf16[2,256,256]{2,1,0:T(8,128)(2,1)S(1)}, bf16[2,256,256]{2,1,0:T(8,128)(2,1)S(1)}, bf16[2,256,256]{2,1,0:T(8,128)(2,1)S(1)}, bf16[2,256,256]{2...) custom-call(f32[2,512,128]{2,1,0:T(8,128)} %bitcast.4, ...), custom_call_target="tpu_custom_call" | custom-call | flops 268435456 | bytes 4197376 | tf_op jit(solution)/shard_map/pallas_call | solution.py:34
  7.8 5.6 %collective-permute-done.refs_0_ = f32[392,128]{1,0:T(8,128)S(1)} collective-permute-done((f32[392,128]{1,0:T(8,128)S(1)}, f32[392,128]{1,0:T(8,128)S(1)}, u32[]{:S(2)}, u32[]{:S(2)}) %collective-permute-start) | collective-permute-done | bytes 200736 | tf_op jit(solution)/shard_map/ppermute | solution.py:470
  13.5 0.7 shard_map.77
  14.2 2.5 %collective-permute-start.2 = (f32[264,128]{1,0:T(8,128)S(1)}, f32[264,128]{1,0:T(8,128)S(1)}, u32[]{:S(2)}, u32[]{:S(2)}) collective-permute-start(f32[264,128]{1,0:T(8,128)S(1)} %get-tuple-element.76), channel_id=1, source_target_pairs={{0,1},{1,0},{2,3},{3,2},{4,5},{5,4},{6,7},{7,6},{8,9},{9,8},{10,11... | collective-permute-start | bytes 405512 | tf_op jit(solution)/shard_map/ppermute | solution.py:470
  16.7 4.9 %collective-permute-done.2.first_ref = f32[264,128]{1,0:T(8,128)S(1)} collective-permute-done((f32[264,128]{1,0:T(8,128)S(1)}, f32[264,128]{1,0:T(8,128)S(1)}, u32[]{:S(2)}, u32[]{:S(2)}) %collective-permute-start.2) | collective-permute-done | bytes 135200 | tf_op jit(solution)/shard_map/ppermute | solution.py:470
  21.6 0.8 shard_map.78
  22.4 2.5 %collective-permute-start.4 = (f32[256,128]{1,0:T(8,128)S(1)}, f32[256,128]{1,0:T(8,128)S(1)}, u32[]{:S(2)}, u32[]{:S(2)}) collective-permute-start(f32[256,128]{1,0:T(8,128)S(1)} %get-tuple-element.84), channel_id=1, source_target_pairs={{0,1},{1,0},{2,3},{3,2},{4,5},{5,4},{6,7},{7,6},{8,9},{9,8},{10,11... | collective-permute-start | bytes 393224 | tf_op jit(solution)/shard_map/ppermute | solution.py:470
  25.4 4.4 %collective-permute-done.4.refs_0_ = f32[256,128]{1,0:T(8,128)S(1)} collective-permute-done((f32[256,128]{1,0:T(8,128)S(1)}, f32[256,128]{1,0:T(8,128)S(1)}, u32[]{:S(2)}, u32[]{:S(2)}) %collective-permute-start.4) | collective-permute-done | bytes 131104 | tf_op jit(solution)/shard_map/ppermute | solution.py:470
  29.8 0.6 shard_map.80
  30.3 2.5 %collective-permute-start.6 = (f32[256,128]{1,0:T(8,128)S(1)}, f32[256,128]{1,0:T(8,128)S(1)}, u32[]{:S(2)}, u32[]{:S(2)}) collective-permute-start(f32[256,128]{1,0:T(8,128)S(1)} %get-tuple-element.90), channel_id=1, source_target_pairs={{0,1},{1,0},{2,3},{3,2},{4,5},{5,4},{6,7},{7,6},{8,9},{9,8},{10,11... | collective-permute-start | bytes 393224 | tf_op jit(solution)/shard_map/ppermute | solution.py:470
  32.9 4.8 %collective-permute-done.6.first_ref = f32[256,128]{1,0:T(8,128)S(1)} collective-permute-done((f32[256,128]{1,0:T(8,128)S(1)}, f32[256,128]{1,0:T(8,128)S(1)}, u32[]{:S(2)}, u32[]{:S(2)}) %collective-permute-start.6) | collective-permute-done | bytes 131104 | tf_op jit(solution)/shard_map/ppermute | solution.py:470
  37.7 0.8 shard_map.81
  38.5 2.5 %collective-permute-start.8 = (f32[256,128]{1,0:T(8,128)S(1)}, f32[256,128]{1,0:T(8,128)S(1)}, u32[]{:S(2)}, u32[]{:S(2)}) collective-permute-start(f32[256,128]{1,0:T(8,128)S(1)} %get-tuple-element.94), channel_id=1, source_target_pairs={{0,1},{1,0},{2,3},{3,2},{4,5},{5,4},{6,7},{7,6},{8,9},{9,8},{10,11... | collective-permute-start | bytes 393224 | tf_op jit(solution)/shard_map/ppermute | solution.py:470
  41.4 4.4 %collective-permute-done.8.refs_0_ = f32[256,128]{1,0:T(8,128)S(1)} collective-permute-done((f32[256,128]{1,0:T(8,128)S(1)}, f32[256,128]{1,0:T(8,128)S(1)}, u32[]{:S(2)}, u32[]{:S(2)}) %collective-permute-start.8) | collective-permute-done | bytes 131104 | tf_op jit(solution)/shard_map/ppermute | solution.py:470
  45.8 0.6 shard_map.83
  46.4 2.5 %collective-permute-start.10 = (f32[256,128]{1,0:T(8,128)S(1)}, f32[256,128]{1,0:T(8,128)S(1)}, u32[]{:S(2)}, u32[]{:S(2)}) collective-permute-start(f32[256,128]{1,0:T(8,128)S(1)} %get-tuple-element.100), channel_id=1, source_target_pairs={{0,1},{1,0},{2,3},{3,2},{4,5},{5,4},{6,7},{7,6},{8,9},{9,8},{10,11... | collective-permute-start | bytes 393224 | tf_op jit(solution)/shard_map/ppermute | solution.py:470
  48.9 4.8 %collective-permute-done.10.first_ref = f32[256,128]{1,0:T(8,128)S(1)} collective-permute-done((f32[256,128]{1,0:T(8,128)S(1)}, f32[256,128]{1,0:T(8,128)S(1)}, u32[]{:S(2)}, u32[]{:S(2)}) %collective-permute-start.10) | collective-permute-done | bytes 131104 | tf_op jit(solution)/shard_map/ppermute | solution.py:470
  53.7 0.8 shard_map.84
  54.5 2.5 %collective-permute-start.12 = (f32[256,128]{1,0:T(8,128)S(1)}, f32[256,128]{1,0:T(8,128)S(1)}, u32[]{:S(2)}, u32[]{:S(2)}) collective-permute-start(f32[256,128]{1,0:T(8,128)S(1)} %get-tuple-element.105), channel_id=1, source_target_pairs={{0,1},{1,0},{2,3},{3,2},{4,5},{5,4},{6,7},{7,6},{8,9},{9,8},{10,11... | collective-permute-start | bytes 393224 | tf_op jit(solution)/shard_map/ppermute | solution.py:470
  57.0 0.5 collective-permute-start.16
  57.5 1.1 %collective-permute-start.18 = (f32[2,256,128]{2,1,0:T(8,128)S(1)}, f32[2,256,128]{2,1,0:T(8,128)S(1)}, u32[]{:S(2)}, u32[]{:S(2)}) collective-permute-start(f32[2,256,128]{2,1,0:T(8,128)S(1)} %get-tuple-element.107.mid_ref), channel_id=1, source_target_pairs={{0,8},{8,16},{16,24},{24,0},{1,9},{9,17},{17,25},{25,1},{2,10},{10... | collective-permute-start | bytes 786440 | tf_op jit(solution)/shard_map/ppermute | solution.py:542
  58.9 2.9 %collective-permute-done.12.refs_0_ = f32[256,128]{1,0:T(8,128)S(1)} collective-permute-done((f32[256,128]{1,0:T(8,128)S(1)}, f32[256,128]{1,0:T(8,128)S(1)}, u32[]{:S(2)}, u32[]{:S(2)}) %collective-permute-start.12) | collective-permute-done | bytes 131104 | tf_op jit(solution)/shard_map/ppermute | solution.py:470
  61.8 0.6 shard_map.86
  62.5 3.7 %collective-permute-start.14 = (f32[256,128]{1,0:T(8,128)S(1)}, f32[256,128]{1,0:T(8,128)S(1)}, u32[]{:S(2)}, u32[]{:S(2)}) collective-permute-start(f32[256,128]{1,0:T(8,128)S(1)} %get-tuple-element.117), channel_id=1, source_target_pairs={{0,9},{1,8},{2,11},{3,10},{4,13},{5,12},{6,15},{7,14},{8,17},{9,16... | collective-permute-start | bytes 393224 | tf_op jit(solution)/shard_map/ppermute | solution.py:470
  66.1 3.0 %shard_map.87.op_ref = f32[8,64,128]{2,1,0:T(8,128)S(1)} custom-call(s32[16]{0:T(128)} %partner_hbm.1, f32[16]{0:T(128)} %cond_hbm.1), custom_call_target="tpu_custom_call" | custom-call | flops 268435456 | bytes 262272 | tf_op jit(solution)/shard_map/pallas_call | solution.py:34
  69.2 0.8 shard_map.88
  70.0 5.1 %all-to-all-start = ((f32[32,2,128]{2,1,0:T(2,128)}), f32[32,2,128]{2,1,0:T(2,128)S(1)}, u32[]{:S(2)}, u32[]{:S(2)}) async-start(f32[32,2,128]{2,1,0:T(2,128)} %bitcast.1), calls=%async_computation | async-start | bytes 65536 | tf_op jit(solution)/shard_map/all_to_all | solution.py:585
  75.2 0.7 copy-done
  75.9 2.6 %shard_map.89 = (f32[2,512,128]{2,1,0:T(8,128)S(1)}, f32[2,512,128]{2,1,0:T(8,128)}) custom-call(f32[256,128]{1,0:T(8,128)S(1)} %collective-permute-done.14.first_ref, f32[256,128]{1,0:T(8,128)S(1)} %collective-permute-done.15.second_ref, bf16[2,256,256]{2,1,0:T(8,128)(2,1)S(1)} %get-tuple-element.65.ff_ref.refs_2_, f32[2,256,128]{2,1,0:T(8,128)} %copy-done, ...), custom_call_target="tpu_custom_call" | custom-call | flops 268435456 | bytes 4128768 | tf_op jit(solution)/shard_map/pallas_call | solution.py:34
  78.6 3.7 %all-to-all-done.parts_ref = f32[32,2,128]{2,1,0:T(2,128)S(1)} async-done(((f32[32,2,128]{2,1,0:T(2,128)}), f32[32,2,128]{2,1,0:T(2,128)S(1)}, u32[]{:S(2)}, u32[]{:S(2)}) %all-to-all-start) | async-done | bytes 32800 | tf_op jit(solution)/shard_map/all_to_all | solution.py:585
  (30 shorter events, 1.9 us)
Async XLA Ops:
  1.9 11.6 %collective-permute-start = (f32[392,128]{1,0:T(8,128)S(1)}, f32[392,128]{1,0:T(8,128)S(1)}, u32[]{:S(2)}, u32[]{:S(2)}) collective-permute-start(f32[392,128]{1,0:T(8,128)S(1)} %get-tuple-element.63), channel_id=1, source_target_pairs={{0,1},{1,0},{2,3},{3,2},{4,5},{5,4},{6,7},{7,6},{8,9},{9,8},{10,11... | collective-permute-start | bytes 602120 | tf_op jit(solution)/shard_map/ppermute | solution.py:470
  4.9 8.6 %collective-permute-start.1 = (f32[392,128]{1,0:T(8,128)S(1)}, f32[392,128]{1,0:T(8,128)S(1)}, u32[]{:S(2)}, u32[]{:S(2)}) collective-permute-start(f32[392,128]{1,0:T(8,128)S(1)} %get-tuple-element.64), channel_id=1, source_target_pairs={{0,8},{1,2},{2,1},{3,4},{4,3},{5,6},{6,5},{7,15},{8,0},{9,10},{10,... | collective-permute-start | bytes 602120 | tf_op jit(solution)/shard_map/ppermute | solution.py:469
  14.2 7.5 %collective-permute-start.2 = (f32[264,128]{1,0:T(8,128)S(1)}, f32[264,128]{1,0:T(8,128)S(1)}, u32[]{:S(2)}, u32[]{:S(2)}) collective-permute-start(f32[264,128]{1,0:T(8,128)S(1)} %get-tuple-element.76), channel_id=1, source_target_pairs={{0,1},{1,0},{2,3},{3,2},{4,5},{5,4},{6,7},{7,6},{8,9},{9,8},{10,11... | collective-permute-start | bytes 405512 | tf_op jit(solution)/shard_map/ppermute | solution.py:470
  16.7 4.9 %collective-permute-start.3 = (f32[264,128]{1,0:T(8,128)S(1)}, f32[264,128]{1,0:T(8,128)S(1)}, u32[]{:S(2)}, u32[]{:S(2)}) collective-permute-start(f32[264,128]{1,0:T(8,128)S(1)} %get-tuple-element.77), channel_id=1, source_target_pairs={{0,8},{1,2},{2,1},{3,4},{4,3},{5,6},{6,5},{7,15},{8,0},{9,10},{10,... | collective-permute-start | bytes 405512 | tf_op jit(solution)/shard_map/ppermute | solution.py:469
  22.4 7.3 %collective-permute-start.4 = (f32[256,128]{1,0:T(8,128)S(1)}, f32[256,128]{1,0:T(8,128)S(1)}, u32[]{:S(2)}, u32[]{:S(2)}) collective-permute-start(f32[256,128]{1,0:T(8,128)S(1)} %get-tuple-element.84), channel_id=1, source_target_pairs={{0,1},{1,0},{2,3},{3,2},{4,5},{5,4},{6,7},{7,6},{8,9},{9,8},{10,11... | collective-permute-start | bytes 393224 | tf_op jit(solution)/shard_map/ppermute | solution.py:470
  25.0 4.8 %collective-permute-start.5 = (f32[256,128]{1,0:T(8,128)S(1)}, f32[256,128]{1,0:T(8,128)S(1)}, u32[]{:S(2)}, u32[]{:S(2)}) collective-permute-start(f32[256,128]{1,0:T(8,128)S(1)} %get-tuple-element.85), channel_id=1, source_target_pairs={{0,8},{1,2},{2,1},{3,4},{4,3},{5,6},{6,5},{7,15},{8,0},{9,10},{10,... | collective-permute-start | bytes 393224 | tf_op jit(solution)/shard_map/ppermute | solution.py:469
  30.3 7.3 %collective-permute-start.6 = (f32[256,128]{1,0:T(8,128)S(1)}, f32[256,128]{1,0:T(8,128)S(1)}, u32[]{:S(2)}, u32[]{:S(2)}) collective-permute-start(f32[256,128]{1,0:T(8,128)S(1)} %get-tuple-element.90), channel_id=1, source_target_pairs={{0,1},{1,0},{2,3},{3,2},{4,5},{5,4},{6,7},{7,6},{8,9},{9,8},{10,11... | collective-permute-start | bytes 393224 | tf_op jit(solution)/shard_map/ppermute | solution.py:470
  32.9 4.8 %collective-permute-start.7 = (f32[256,128]{1,0:T(8,128)S(1)}, f32[256,128]{1,0:T(8,128)S(1)}, u32[]{:S(2)}, u32[]{:S(2)}) collective-permute-start(f32[256,128]{1,0:T(8,128)S(1)} %get-tuple-element.91), channel_id=1, source_target_pairs={{0,8},{1,2},{2,1},{3,4},{4,3},{5,6},{6,5},{7,15},{8,0},{9,10},{10,... | collective-permute-start | bytes 393224 | tf_op jit(solution)/shard_map/ppermute | solution.py:469
  38.5 7.3 %collective-permute-start.8 = (f32[256,128]{1,0:T(8,128)S(1)}, f32[256,128]{1,0:T(8,128)S(1)}, u32[]{:S(2)}, u32[]{:S(2)}) collective-permute-start(f32[256,128]{1,0:T(8,128)S(1)} %get-tuple-element.94), channel_id=1, source_target_pairs={{0,1},{1,0},{2,3},{3,2},{4,5},{5,4},{6,7},{7,6},{8,9},{9,8},{10,11... | collective-permute-start | bytes 393224 | tf_op jit(solution)/shard_map/ppermute | solution.py:470
  41.0 4.8 %collective-permute-start.9 = (f32[256,128]{1,0:T(8,128)S(1)}, f32[256,128]{1,0:T(8,128)S(1)}, u32[]{:S(2)}, u32[]{:S(2)}) collective-permute-start(f32[256,128]{1,0:T(8,128)S(1)} %get-tuple-element.95), channel_id=1, source_target_pairs={{0,8},{1,2},{2,1},{3,4},{4,3},{5,6},{6,5},{7,15},{8,0},{9,10},{10,... | collective-permute-start | bytes 393224 | tf_op jit(solution)/shard_map/ppermute | solution.py:469
  46.4 7.3 %collective-permute-start.10 = (f32[256,128]{1,0:T(8,128)S(1)}, f32[256,128]{1,0:T(8,128)S(1)}, u32[]{:S(2)}, u32[]{:S(2)}) collective-permute-start(f32[256,128]{1,0:T(8,128)S(1)} %get-tuple-element.100), channel_id=1, source_target_pairs={{0,1},{1,0},{2,3},{3,2},{4,5},{5,4},{6,7},{7,6},{8,9},{9,8},{10,11... | collective-permute-start | bytes 393224 | tf_op jit(solution)/shard_map/ppermute | solution.py:470
  48.9 4.8 %collective-permute-start.11 = (f32[256,128]{1,0:T(8,128)S(1)}, f32[256,128]{1,0:T(8,128)S(1)}, u32[]{:S(2)}, u32[]{:S(2)}) collective-permute-start(f32[256,128]{1,0:T(8,128)S(1)} %get-tuple-element.101), channel_id=1, source_target_pairs={{0,8},{1,2},{2,1},{3,4},{4,3},{5,6},{6,5},{7,15},{8,0},{9,10},{10,... | collective-permute-start | bytes 393224 | tf_op jit(solution)/shard_map/ppermute | solution.py:469
  54.5 7.3 %collective-permute-start.12 = (f32[256,128]{1,0:T(8,128)S(1)}, f32[256,128]{1,0:T(8,128)S(1)}, u32[]{:S(2)}, u32[]{:S(2)}) collective-permute-start(f32[256,128]{1,0:T(8,128)S(1)} %get-tuple-element.105), channel_id=1, source_target_pairs={{0,1},{1,0},{2,3},{3,2},{4,5},{5,4},{6,7},{7,6},{8,9},{9,8},{10,11... | collective-permute-start | bytes 393224 | tf_op jit(solution)/shard_map/ppermute | solution.py:470
  57.0 4.8 %collective-permute-start.13 = (f32[256,128]{1,0:T(8,128)S(1)}, f32[256,128]{1,0:T(8,128)S(1)}, u32[]{:S(2)}, u32[]{:S(2)}) collective-permute-start(f32[256,128]{1,0:T(8,128)S(1)} %get-tuple-element.106), channel_id=1, source_target_pairs={{0,8},{1,2},{2,1},{3,4},{4,3},{5,6},{6,5},{7,15},{8,0},{9,10},{10,... | collective-permute-start | bytes 393224 | tf_op jit(solution)/shard_map/ppermute | solution.py:469
  57.0 18.1 %collective-permute-start.16 = (f32[2,256,128]{2,1,0:T(8,128)S(1)}, f32[2,256,128]{2,1,0:T(8,128)S(1)}, u32[]{:S(2)}, u32[]{:S(2)}) collective-permute-start(f32[2,256,128]{2,1,0:T(8,128)S(1)} %get-tuple-element.104.refs_4_.rhs_ref), channel_id=1, source_target_pairs={{0,8},{8,16},{16,24},{24,0},{1,9},{9,17},{17,25},{25,1},{2,10},{10... | collective-permute-start | bytes 786440 | tf_op jit(solution)/shard_map/ppermute | solution.py:543
  57.5 17.6 %collective-permute-start.18 = (f32[2,256,128]{2,1,0:T(8,128)S(1)}, f32[2,256,128]{2,1,0:T(8,128)S(1)}, u32[]{:S(2)}, u32[]{:S(2)}) collective-permute-start(f32[2,256,128]{2,1,0:T(8,128)S(1)} %get-tuple-element.107.mid_ref), channel_id=1, source_target_pairs={{0,8},{8,16},{16,24},{24,0},{1,9},{9,17},{17,25},{25,1},{2,10},{10... | collective-permute-start | bytes 786440 | tf_op jit(solution)/shard_map/ppermute | solution.py:542
  62.4 12.8 %collective-permute-start.17 = (f32[2,256,128]{2,1,0:T(8,128)S(1)}, f32[2,256,128]{2,1,0:T(8,128)}, u32[]{:S(2)}, u32[]{:S(2)}) collective-permute-start(f32[2,256,128]{2,1,0:T(8,128)S(1)} %get-tuple-element.111.faces_ref), channel_id=1, source_target_pairs={{0,8},{8,16},{16,24},{24,0},{1,9},{9,17},{17,25},{25,1},{2,10},{10... | collective-permute-start | bytes 786440 | tf_op jit(solution)/shard_map/ppermute | solution.py:578
  62.5 12.7 %collective-permute-start.14 = (f32[256,128]{1,0:T(8,128)S(1)}, f32[256,128]{1,0:T(8,128)S(1)}, u32[]{:S(2)}, u32[]{:S(2)}) collective-permute-start(f32[256,128]{1,0:T(8,128)S(1)} %get-tuple-element.117), channel_id=1, source_target_pairs={{0,9},{1,8},{2,11},{3,10},{4,13},{5,12},{6,15},{7,14},{8,17},{9,16... | collective-permute-start | bytes 393224 | tf_op jit(solution)/shard_map/ppermute | solution.py:470
  66.1 9.0 %collective-permute-start.15 = (f32[256,128]{1,0:T(8,128)S(1)}, f32[256,128]{1,0:T(8,128)S(1)}, u32[]{:S(2)}, u32[]{:S(2)}) collective-permute-start(f32[256,128]{1,0:T(8,128)S(1)} %get-tuple-element.118), channel_id=1, source_target_pairs={{0,8},{1,10},{2,9},{3,12},{4,11},{5,14},{6,13},{7,15},{8,16},{9,18... | collective-permute-start | bytes 393224 | tf_op jit(solution)/shard_map/ppermute | solution.py:469
  70.0 12.3 %all-to-all-start = ((f32[32,2,128]{2,1,0:T(2,128)}), f32[32,2,128]{2,1,0:T(2,128)S(1)}, u32[]{:S(2)}, u32[]{:S(2)}) async-start(f32[32,2,128]{2,1,0:T(2,128)} %bitcast.1), calls=%async_computation | async-start | bytes 65536 | tf_op jit(solution)/shard_map/all_to_all | solution.py:585
  75.1 0.7 copy-start
  75.2 0.8 copy-start.1

commit v6 on v5

--- a/solution.py
+++ b/solution.py
@@ -380,6 +380,7 @@
         end_ref[i, face : width - face] += dot(rf_ref[i], vectors[i])
         end_ref[i, width - face :] = up[i]
         start_ref[i] = jnp.where(later, end_ref[i], start_ref[i])
+    for i in range(count):
         copies.append(pltpu.make_async_copy(start_ref.at[i], out_hbm.at[i], out_sems.at[i]))
         copies[i].start()
     for copy in copies:
@@ -434,20 +435,15 @@
             out_ref[k, s * n : (s + 1) * n] = jnp.broadcast_to(total[:, k : k + 1], (n, out_ref.shape[2]))
 
 
-def correct(count, pieces, parts_ref, previous_ref, early_hbm, out_hbm, out_ref, sems):
+def correct(count, parts_ref, previous_ref, early_hbm, out_hbm, out_ref, sems):
     @pl.when(lax.axis_index("cuts") > 1)
     def _():
         mine = jnp.sum(parts_ref[...], axis=0)
-        size = out_ref.shape[1] // pieces
-        copies = []
         for i in range(count):
-            for k in range(pieces):
-                rows = pl.ds(k * size, size)
-                out_ref[i, rows] = previous_ref[i, rows] + mine[i : i + 1]
-                copies.append(
-                    pltpu.make_async_copy(out_ref.at[i, rows], out_hbm.at[i, rows], sems.at[i * pieces + k])
-                )
-                copies[-1].start()
+            out_ref[i] = previous_ref[i] + mine[i : i + 1]
+        copies = [pltpu.make_async_copy(out_ref.at[i], out_hbm.at[i], sems.at[i]) for i in range(count)]
+        for copy in copies:
+            copy.start()
         for copy in copies:
             copy.wait()
 
@@ -600,14 +596,13 @@
             pltpu.SemaphoreType.DMA((count,)),
         ],
     )
-    pieces = 2
     (result,) = call(
-        functools.partial(correct, count, pieces),
+        functools.partial(correct, count),
         [rhs_shape],
         (parts, previous, early),
         stay=(2,),
         stay_out=(0,),
-        scratch=[pltpu.VMEM(rhs_shape.shape, F32), pltpu.SemaphoreType.DMA((count * pieces,))],
+        scratch=[pltpu.VMEM(rhs_shape.shape, F32), pltpu.SemaphoreType.DMA((count,))],
         aliases={2: 0},
     )
     return result[None]

time: 82.6 us -> 82.6 us (level)
  no operation moved by 1% of the time
where the time goes in v6:
time: 82.6 us; the launch traced here: 82.3 us
  waiting for transfers between devices  35.5 us (43%)
  starting transfers between devices  28.8 us (35%)
  Pallas kernels  17.1 us (21%)
    ppermute x8, waiting for transfers between devices, exchange(): near = lax.ppermute(first, ('cuts', 'sub'), pairs)  31.8 us
    ppermute x8, starting transfers between devices, exchange(): near = lax.ppermute(first, ('cuts', 'sub'), pairs)  22 us
    pallas_call x18, Pallas kernels, call(): pl.pallas_call(body, out_shape=out_shape, in_specs=[hbm if k in stay else...  17.1 us
    all_to_all x1, starting transfers between devices, on_device(): parts = lax.all_to_all(parts, ('cuts', 'sub'), 0, 0, tiled=True)  5.14 us
    all_to_all x1, waiting for transfers between devices, on_device(): parts = lax.all_to_all(parts, ('cuts', 'sub'), 0, 0, tiled=True)  3.71 us
  transfers between devices with their start and end apart: 20, of which 8 were waited for; matrix products, arithmetic and copies ran while one was open for 0% of the time, Pallas kernels for 13%

profile of v6, /device:TPU:0, one launch (start us, length us, event | category | flops | bytes accessed | tf_op | source)
XLA Modules:
  0.0 82.3 jit_solution(763839601164357244)
XLA Ops:
  0.0 1.9 %shard_map.73 = (f32[2,256,128]{2,1,0:T(8,128)S(1)}, f32[4,128,128]{2,1,0:T(8,128)S(1)}, f32[2,256,128]{2,1,0:T(8,128)S(1)}, f32[392,128]{1,0:T(8,128)S(1)}, f32[392,128]{1,0:T(8,128)S(1)}) custom-call(f32[2,512,128]{2,1,0:T(8,128)} %bitcast.3, bf16[2,512,128]{2,1,0:T(8,128)(2,1)} %source_hbm.3, bf16[2,512,512]{2,1,0:T(8,128)(2,1)} %inverse_hbm.3, ...), custom_call_target="tpu_custom_call" | custom-call | flops 268435456 | bytes 3026944 | tf_op jit(solution)/shard_map/pallas_call | solution.py:34
  1.9 3.0 %collective-permute-start = (f32[392,128]{1,0:T(8,128)S(1)}, f32[392,128]{1,0:T(8,128)S(1)}, u32[]{:S(2)}, u32[]{:S(2)}) collective-permute-start(f32[392,128]{1,0:T(8,128)S(1)} %get-tuple-element.63), channel_id=1, source_target_pairs={{0,1},{1,0},{2,3},{3,2},{4,5},{5,4},{6,7},{7,6},{8,9},{9,8},{10,11... | collective-permute-start | bytes 602120 | tf_op jit(solution)/shard_map/ppermute | solution.py:466
  4.9 2.2 %shard_map.74 = (bf16[2,256,256]{2,1,0:T(8,128)(2,1)S(1)}, bf16[2,256,256]{2,1,0:T(8,128)(2,1)S(1)}, bf16[2,256,256]{2,1,0:T(8,128)(2,1)S(1)}, bf16[2,256,256]{2...) custom-call(f32[2,512,128]{2,1,0:T(8,128)} %bitcast.4, ...), custom_call_target="tpu_custom_call" | custom-call | flops 268435456 | bytes 4197376 | tf_op jit(solution)/shard_map/pallas_call | solution.py:34
  7.8 5.6 %collective-permute-done.refs_0_ = f32[392,128]{1,0:T(8,128)S(1)} collective-permute-done((f32[392,128]{1,0:T(8,128)S(1)}, f32[392,128]{1,0:T(8,128)S(1)}, u32[]{:S(2)}, u32[]{:S(2)}) %collective-permute-start) | collective-permute-done | bytes 200736 | tf_op jit(solution)/shard_map/ppermute | solution.py:466
  13.5 0.7 shard_map.77
  14.2 2.5 %collective-permute-start.2 = (f32[264,128]{1,0:T(8,128)S(1)}, f32[264,128]{1,0:T(8,128)S(1)}, u32[]{:S(2)}, u32[]{:S(2)}) collective-permute-start(f32[264,128]{1,0:T(8,128)S(1)} %get-tuple-element.76), channel_id=1, source_target_pairs={{0,1},{1,0},{2,3},{3,2},{4,5},{5,4},{6,7},{7,6},{8,9},{9,8},{10,11... | collective-permute-start | bytes 405512 | tf_op jit(solution)/shard_map/ppermute | solution.py:466
  16.7 4.9 %collective-permute-done.2.first_ref = f32[264,128]{1,0:T(8,128)S(1)} collective-permute-done((f32[264,128]{1,0:T(8,128)S(1)}, f32[264,128]{1,0:T(8,128)S(1)}, u32[]{:S(2)}, u32[]{:S(2)}) %collective-permute-start.2) | collective-permute-done | bytes 135200 | tf_op jit(solution)/shard_map/ppermute | solution.py:466
  21.6 0.8 shard_map.78
  22.4 2.5 %collective-permute-start.4 = (f32[256,128]{1,0:T(8,128)S(1)}, f32[256,128]{1,0:T(8,128)S(1)}, u32[]{:S(2)}, u32[]{:S(2)}) collective-permute-start(f32[256,128]{1,0:T(8,128)S(1)} %get-tuple-element.84), channel_id=1, source_target_pairs={{0,1},{1,0},{2,3},{3,2},{4,5},{5,4},{6,7},{7,6},{8,9},{9,8},{10,11... | collective-permute-start | bytes 393224 | tf_op jit(solution)/shard_map/ppermute | solution.py:466
  25.4 4.4 %collective-permute-done.4.refs_0_ = f32[256,128]{1,0:T(8,128)S(1)} collective-permute-done((f32[256,128]{1,0:T(8,128)S(1)}, f32[256,128]{1,0:T(8,128)S(1)}, u32[]{:S(2)}, u32[]{:S(2)}) %collective-permute-start.4) | collective-permute-done | bytes 131104 | tf_op jit(solution)/shard_map/ppermute | solution.py:466
  29.8 0.6 shard_map.80
  30.3 2.5 %collective-permute-start.6 = (f32[256,128]{1,0:T(8,128)S(1)}, f32[256,128]{1,0:T(8,128)S(1)}, u32[]{:S(2)}, u32[]{:S(2)}) collective-permute-start(f32[256,128]{1,0:T(8,128)S(1)} %get-tuple-element.90), channel_id=1, source_target_pairs={{0,1},{1,0},{2,3},{3,2},{4,5},{5,4},{6,7},{7,6},{8,9},{9,8},{10,11... | collective-permute-start | bytes 393224 | tf_op jit(solution)/shard_map/ppermute | solution.py:466
  32.9 4.8 %collective-permute-done.6.first_ref = f32[256,128]{1,0:T(8,128)S(1)} collective-permute-done((f32[256,128]{1,0:T(8,128)S(1)}, f32[256,128]{1,0:T(8,128)S(1)}, u32[]{:S(2)}, u32[]{:S(2)}) %collective-permute-start.6) | collective-permute-done | bytes 131104 | tf_op jit(solution)/shard_map/ppermute | solution.py:466
  37.7 0.8 shard_map.81
  38.5 2.5 %collective-permute-start.8 = (f32[256,128]{1,0:T(8,128)S(1)}, f32[256,128]{1,0:T(8,128)S(1)}, u32[]{:S(2)}, u32[]{:S(2)}) collective-permute-start(f32[256,128]{1,0:T(8,128)S(1)} %get-tuple-element.94), channel_id=1, source_target_pairs={{0,1},{1,0},{2,3},{3,2},{4,5},{5,4},{6,7},{7,6},{8,9},{9,8},{10,11... | collective-permute-start | bytes 393224 | tf_op jit(solution)/shard_map/ppermute | solution.py:466
  41.4 4.4 %collective-permute-done.8.refs_0_ = f32[256,128]{1,0:T(8,128)S(1)} collective-permute-done((f32[256,128]{1,0:T(8,128)S(1)}, f32[256,128]{1,0:T(8,128)S(1)}, u32[]{:S(2)}, u32[]{:S(2)}) %collective-permute-start.8) | collective-permute-done | bytes 131104 | tf_op jit(solution)/shard_map/ppermute | solution.py:466
  45.8 0.6 shard_map.83
  46.4 2.5 %collective-permute-start.10 = (f32[256,128]{1,0:T(8,128)S(1)}, f32[256,128]{1,0:T(8,128)S(1)}, u32[]{:S(2)}, u32[]{:S(2)}) collective-permute-start(f32[256,128]{1,0:T(8,128)S(1)} %get-tuple-element.100), channel_id=1, source_target_pairs={{0,1},{1,0},{2,3},{3,2},{4,5},{5,4},{6,7},{7,6},{8,9},{9,8},{10,11... | collective-permute-start | bytes 393224 | tf_op jit(solution)/shard_map/ppermute | solution.py:466
  48.9 4.8 %collective-permute-done.10.first_ref = f32[256,128]{1,0:T(8,128)S(1)} collective-permute-done((f32[256,128]{1,0:T(8,128)S(1)}, f32[256,128]{1,0:T(8,128)S(1)}, u32[]{:S(2)}, u32[]{:S(2)}) %collective-permute-start.10) | collective-permute-done | bytes 131104 | tf_op jit(solution)/shard_map/ppermute | solution.py:466
  53.7 0.8 shard_map.84
  54.5 2.5 %collective-permute-start.12 = (f32[256,128]{1,0:T(8,128)S(1)}, f32[256,128]{1,0:T(8,128)S(1)}, u32[]{:S(2)}, u32[]{:S(2)}) collective-permute-start(f32[256,128]{1,0:T(8,128)S(1)} %get-tuple-element.105), channel_id=1, source_target_pairs={{0,1},{1,0},{2,3},{3,2},{4,5},{5,4},{6,7},{7,6},{8,9},{9,8},{10,11... | collective-permute-start | bytes 393224 | tf_op jit(solution)/shard_map/ppermute | solution.py:466
  57.0 0.5 collective-permute-start.16
  57.5 1.1 %collective-permute-start.18 = (f32[2,256,128]{2,1,0:T(8,128)S(1)}, f32[2,256,128]{2,1,0:T(8,128)S(1)}, u32[]{:S(2)}, u32[]{:S(2)}) collective-permute-start(f32[2,256,128]{2,1,0:T(8,128)S(1)} %get-tuple-element.107.mid_ref), channel_id=1, source_target_pairs={{0,8},{8,16},{16,24},{24,0},{1,9},{9,17},{17,25},{25,1},{2,10},{10... | collective-permute-start | bytes 786440 | tf_op jit(solution)/shard_map/ppermute | solution.py:538
  58.9 2.9 %collective-permute-done.12.refs_0_ = f32[256,128]{1,0:T(8,128)S(1)} collective-permute-done((f32[256,128]{1,0:T(8,128)S(1)}, f32[256,128]{1,0:T(8,128)S(1)}, u32[]{:S(2)}, u32[]{:S(2)}) %collective-permute-start.12) | collective-permute-done | bytes 131104 | tf_op jit(solution)/shard_map/ppermute | solution.py:466
  61.8 0.6 shard_map.86
  62.5 3.7 %collective-permute-start.14 = (f32[256,128]{1,0:T(8,128)S(1)}, f32[256,128]{1,0:T(8,128)S(1)}, u32[]{:S(2)}, u32[]{:S(2)}) collective-permute-start(f32[256,128]{1,0:T(8,128)S(1)} %get-tuple-element.117), channel_id=1, source_target_pairs={{0,9},{1,8},{2,11},{3,10},{4,13},{5,12},{6,15},{7,14},{8,17},{9,16... | collective-permute-start | bytes 393224 | tf_op jit(solution)/shard_map/ppermute | solution.py:466
  66.1 3.0 %shard_map.87.op_ref = f32[8,64,128]{2,1,0:T(8,128)S(1)} custom-call(s32[16]{0:T(128)} %partner_hbm.1, f32[16]{0:T(128)} %cond_hbm.1), custom_call_target="tpu_custom_call" | custom-call | flops 268435456 | bytes 262272 | tf_op jit(solution)/shard_map/pallas_call | solution.py:34
  69.2 0.8 shard_map.88
  70.0 5.1 %all-to-all-start = ((f32[32,2,128]{2,1,0:T(2,128)}), f32[32,2,128]{2,1,0:T(2,128)S(1)}, u32[]{:S(2)}, u32[]{:S(2)}) async-start(f32[32,2,128]{2,1,0:T(2,128)} %bitcast.1), calls=%async_computation | async-start | bytes 65536 | tf_op jit(solution)/shard_map/all_to_all | solution.py:581
  75.2 0.7 copy-done
  75.9 2.6 %shard_map.89 = (f32[2,512,128]{2,1,0:T(8,128)S(1)}, f32[2,512,128]{2,1,0:T(8,128)}) custom-call(f32[256,128]{1,0:T(8,128)S(1)} %collective-permute-done.14.first_ref, f32[256,128]{1,0:T(8,128)S(1)} %collective-permute-done.15.second_ref, bf16[2,256,256]{2,1,0:T(8,128)(2,1)S(1)} %get-tuple-element.65.ff_ref.refs_2_, f32[2,256,128]{2,1,0:T(8,128)} %copy-done, ...), custom_call_target="tpu_custom_call" | custom-call | flops 268435456 | bytes 4128768 | tf_op jit(solution)/shard_map/pallas_call | solution.py:34
  78.6 3.7 %all-to-all-done.parts_ref = f32[32,2,128]{2,1,0:T(2,128)S(1)} async-done(((f32[32,2,128]{2,1,0:T(2,128)}), f32[32,2,128]{2,1,0:T(2,128)S(1)}, u32[]{:S(2)}, u32[]{:S(2)}) %all-to-all-start) | async-done | bytes 32800 | tf_op jit(solution)/shard_map/all_to_all | solution.py:581
  (30 shorter events, 1.9 us)
Async XLA Ops:
  1.9 11.6 %collective-permute-start = (f32[392,128]{1,0:T(8,128)S(1)}, f32[392,128]{1,0:T(8,128)S(1)}, u32[]{:S(2)}, u32[]{:S(2)}) collective-permute-start(f32[392,128]{1,0:T(8,128)S(1)} %get-tuple-element.63), channel_id=1, source_target_pairs={{0,1},{1,0},{2,3},{3,2},{4,5},{5,4},{6,7},{7,6},{8,9},{9,8},{10,11... | collective-permute-start | bytes 602120 | tf_op jit(solution)/shard_map/ppermute | solution.py:466
  4.9 8.6 %collective-permute-start.1 = (f32[392,128]{1,0:T(8,128)S(1)}, f32[392,128]{1,0:T(8,128)S(1)}, u32[]{:S(2)}, u32[]{:S(2)}) collective-permute-start(f32[392,128]{1,0:T(8,128)S(1)} %get-tuple-element.64), channel_id=1, source_target_pairs={{0,8},{1,2},{2,1},{3,4},{4,3},{5,6},{6,5},{7,15},{8,0},{9,10},{10,... | collective-permute-start | bytes 602120 | tf_op jit(solution)/shard_map/ppermute | solution.py:465
  14.2 7.5 %collective-permute-start.2 = (f32[264,128]{1,0:T(8,128)S(1)}, f32[264,128]{1,0:T(8,128)S(1)}, u32[]{:S(2)}, u32[]{:S(2)}) collective-permute-start(f32[264,128]{1,0:T(8,128)S(1)} %get-tuple-element.76), channel_id=1, source_target_pairs={{0,1},{1,0},{2,3},{3,2},{4,5},{5,4},{6,7},{7,6},{8,9},{9,8},{10,11... | collective-permute-start | bytes 405512 | tf_op jit(solution)/shard_map/ppermute | solution.py:466
  16.7 4.9 %collective-permute-start.3 = (f32[264,128]{1,0:T(8,128)S(1)}, f32[264,128]{1,0:T(8,128)S(1)}, u32[]{:S(2)}, u32[]{:S(2)}) collective-permute-start(f32[264,128]{1,0:T(8,128)S(1)} %get-tuple-element.77), channel_id=1, source_target_pairs={{0,8},{1,2},{2,1},{3,4},{4,3},{5,6},{6,5},{7,15},{8,0},{9,10},{10,... | collective-permute-start | bytes 405512 | tf_op jit(solution)/shard_map/ppermute | solution.py:465
  22.4 7.3 %collective-permute-start.4 = (f32[256,128]{1,0:T(8,128)S(1)}, f32[256,128]{1,0:T(8,128)S(1)}, u32[]{:S(2)}, u32[]{:S(2)}) collective-permute-start(f32[256,128]{1,0:T(8,128)S(1)} %get-tuple-element.84), channel_id=1, source_target_pairs={{0,1},{1,0},{2,3},{3,2},{4,5},{5,4},{6,7},{7,6},{8,9},{9,8},{10,11... | collective-permute-start | bytes 393224 | tf_op jit(solution)/shard_map/ppermute | solution.py:466
  25.0 4.8 %collective-permute-start.5 = (f32[256,128]{1,0:T(8,128)S(1)}, f32[256,128]{1,0:T(8,128)S(1)}, u32[]{:S(2)}, u32[]{:S(2)}) collective-permute-start(f32[256,128]{1,0:T(8,128)S(1)} %get-tuple-element.85), channel_id=1, source_target_pairs={{0,8},{1,2},{2,1},{3,4},{4,3},{5,6},{6,5},{7,15},{8,0},{9,10},{10,... | collective-permute-start | bytes 393224 | tf_op jit(solution)/shard_map/ppermute | solution.py:465
  30.3 7.3 %collective-permute-start.6 = (f32[256,128]{1,0:T(8,128)S(1)}, f32[256,128]{1,0:T(8,128)S(1)}, u32[]{:S(2)}, u32[]{:S(2)}) collective-permute-start(f32[256,128]{1,0:T(8,128)S(1)} %get-tuple-element.90), channel_id=1, source_target_pairs={{0,1},{1,0},{2,3},{3,2},{4,5},{5,4},{6,7},{7,6},{8,9},{9,8},{10,11... | collective-permute-start | bytes 393224 | tf_op jit(solution)/shard_map/ppermute | solution.py:466
  32.9 4.8 %collective-permute-start.7 = (f32[256,128]{1,0:T(8,128)S(1)}, f32[256,128]{1,0:T(8,128)S(1)}, u32[]{:S(2)}, u32[]{:S(2)}) collective-permute-start(f32[256,128]{1,0:T(8,128)S(1)} %get-tuple-element.91), channel_id=1, source_target_pairs={{0,8},{1,2},{2,1},{3,4},{4,3},{5,6},{6,5},{7,15},{8,0},{9,10},{10,... | collective-permute-start | bytes 393224 | tf_op jit(solution)/shard_map/ppermute | solution.py:465
  38.5 7.3 %collective-permute-start.8 = (f32[256,128]{1,0:T(8,128)S(1)}, f32[256,128]{1,0:T(8,128)S(1)}, u32[]{:S(2)}, u32[]{:S(2)}) collective-permute-start(f32[256,128]{1,0:T(8,128)S(1)} %get-tuple-element.94), channel_id=1, source_target_pairs={{0,1},{1,0},{2,3},{3,2},{4,5},{5,4},{6,7},{7,6},{8,9},{9,8},{10,11... | collective-permute-start | bytes 393224 | tf_op jit(solution)/shard_map/ppermute | solution.py:466
  41.0 4.8 %collective-permute-start.9 = (f32[256,128]{1,0:T(8,128)S(1)}, f32[256,128]{1,0:T(8,128)S(1)}, u32[]{:S(2)}, u32[]{:S(2)}) collective-permute-start(f32[256,128]{1,0:T(8,128)S(1)} %get-tuple-element.95), channel_id=1, source_target_pairs={{0,8},{1,2},{2,1},{3,4},{4,3},{5,6},{6,5},{7,15},{8,0},{9,10},{10,... | collective-permute-start | bytes 393224 | tf_op jit(solution)/shard_map/ppermute | solution.py:465
  46.4 7.3 %collective-permute-start.10 = (f32[256,128]{1,0:T(8,128)S(1)}, f32[256,128]{1,0:T(8,128)S(1)}, u32[]{:S(2)}, u32[]{:S(2)}) collective-permute-start(f32[256,128]{1,0:T(8,128)S(1)} %get-tuple-element.100), channel_id=1, source_target_pairs={{0,1},{1,0},{2,3},{3,2},{4,5},{5,4},{6,7},{7,6},{8,9},{9,8},{10,11... | collective-permute-start | bytes 393224 | tf_op jit(solution)/shard_map/ppermute | solution.py:466
  48.9 4.8 %collective-permute-start.11 = (f32[256,128]{1,0:T(8,128)S(1)}, f32[256,128]{1,0:T(8,128)S(1)}, u32[]{:S(2)}, u32[]{:S(2)}) collective-permute-start(f32[256,128]{1,0:T(8,128)S(1)} %get-tuple-element.101), channel_id=1, source_target_pairs={{0,8},{1,2},{2,1},{3,4},{4,3},{5,6},{6,5},{7,15},{8,0},{9,10},{10,... | collective-permute-start | bytes 393224 | tf_op jit(solution)/shard_map/ppermute | solution.py:465
  54.5 7.3 %collective-permute-start.12 = (f32[256,128]{1,0:T(8,128)S(1)}, f32[256,128]{1,0:T(8,128)S(1)}, u32[]{:S(2)}, u32[]{:S(2)}) collective-permute-start(f32[256,128]{1,0:T(8,128)S(1)} %get-tuple-element.105), channel_id=1, source_target_pairs={{0,1},{1,0},{2,3},{3,2},{4,5},{5,4},{6,7},{7,6},{8,9},{9,8},{10,11... | collective-permute-start | bytes 393224 | tf_op jit(solution)/shard_map/ppermute | solution.py:466
  57.0 4.8 %collective-permute-start.13 = (f32[256,128]{1,0:T(8,128)S(1)}, f32[256,128]{1,0:T(8,128)S(1)}, u32[]{:S(2)}, u32[]{:S(2)}) collective-permute-start(f32[256,128]{1,0:T(8,128)S(1)} %get-tuple-element.106), channel_id=1, source_target_pairs={{0,8},{1,2},{2,1},{3,4},{4,3},{5,6},{6,5},{7,15},{8,0},{9,10},{10,... | collective-permute-start | bytes 393224 | tf_op jit(solution)/shard_map/ppermute | solution.py:465
  57.0 18.1 %collective-permute-start.16 = (f32[2,256,128]{2,1,0:T(8,128)S(1)}, f32[2,256,128]{2,1,0:T(8,128)S(1)}, u32[]{:S(2)}, u32[]{:S(2)}) collective-permute-start(f32[2,256,128]{2,1,0:T(8,128)S(1)} %get-tuple-element.104.refs_4_.rhs_ref), channel_id=1, source_target_pairs={{0,8},{8,16},{16,24},{24,0},{1,9},{9,17},{17,25},{25,1},{2,10},{10... | collective-permute-start | bytes 786440 | tf_op jit(solution)/shard_map/ppermute | solution.py:539
  57.5 17.6 %collective-permute-start.18 = (f32[2,256,128]{2,1,0:T(8,128)S(1)}, f32[2,256,128]{2,1,0:T(8,128)S(1)}, u32[]{:S(2)}, u32[]{:S(2)}) collective-permute-start(f32[2,256,128]{2,1,0:T(8,128)S(1)} %get-tuple-element.107.mid_ref), channel_id=1, source_target_pairs={{0,8},{8,16},{16,24},{24,0},{1,9},{9,17},{17,25},{25,1},{2,10},{10... | collective-permute-start | bytes 786440 | tf_op jit(solution)/shard_map/ppermute | solution.py:538
  62.4 12.8 %collective-permute-start.17 = (f32[2,256,128]{2,1,0:T(8,128)S(1)}, f32[2,256,128]{2,1,0:T(8,128)}, u32[]{:S(2)}, u32[]{:S(2)}) collective-permute-start(f32[2,256,128]{2,1,0:T(8,128)S(1)} %get-tuple-element.111.faces_ref), channel_id=1, source_target_pairs={{0,8},{8,16},{16,24},{24,0},{1,9},{9,17},{17,25},{25,1},{2,10},{10... | collective-permute-start | bytes 786440 | tf_op jit(solution)/shard_map/ppermute | solution.py:574
  62.5 12.7 %collective-permute-start.14 = (f32[256,128]{1,0:T(8,128)S(1)}, f32[256,128]{1,0:T(8,128)S(1)}, u32[]{:S(2)}, u32[]{:S(2)}) collective-permute-start(f32[256,128]{1,0:T(8,128)S(1)} %get-tuple-element.117), channel_id=1, source_target_pairs={{0,9},{1,8},{2,11},{3,10},{4,13},{5,12},{6,15},{7,14},{8,17},{9,16... | collective-permute-start | bytes 393224 | tf_op jit(solution)/shard_map/ppermute | solution.py:466
  66.1 9.0 %collective-permute-start.15 = (f32[256,128]{1,0:T(8,128)S(1)}, f32[256,128]{1,0:T(8,128)S(1)}, u32[]{:S(2)}, u32[]{:S(2)}) collective-permute-start(f32[256,128]{1,0:T(8,128)S(1)} %get-tuple-element.118), channel_id=1, source_target_pairs={{0,8},{1,10},{2,9},{3,12},{4,11},{5,14},{6,13},{7,15},{8,16},{9,18... | collective-permute-start | bytes 393224 | tf_op jit(solution)/shard_map/ppermute | solution.py:465
  70.0 12.3 %all-to-all-start = ((f32[32,2,128]{2,1,0:T(2,128)}), f32[32,2,128]{2,1,0:T(2,128)S(1)}, u32[]{:S(2)}, u32[]{:S(2)}) async-start(f32[32,2,128]{2,1,0:T(2,128)} %bitcast.1), calls=%async_computation | async-start | bytes 65536 | tf_op jit(solution)/shard_map/all_to_all | solution.py:581
  75.1 0.7 copy-start
  75.2 0.8 copy-start.1

commit v7 on v6

--- a/solution.py
+++ b/solution.py
@@ -248,6 +248,8 @@
         for i in range(count):
             next_faces[0][i, :face] = next_low[i]
             next_faces[0][i, face:] = next_up[i]
+        next_faces[1][0] = dot(near_ref[0], (near_link_ref[0] * low[0]).astype(BF16))
+        next_faces[1][1] = dot(near_ref[1], (near_link_ref[1] * up[-1]).astype(BF16))
         upward, downward = (up[-1], next_up[-1]), (low[0], next_low[0])
     else:
         upward, downward = outgoing(count, ff_ref, y_ref[0, :face], y_ref[count - 1, face:], rhs_ref, link_ref, low, up)
@@ -326,13 +328,12 @@
         out_ref[i : i + 1] = total / (2 * face + rm_ref.shape[1])
 
 
-def means_payload(count, rhs_ref, link_ref, faces_ref, next_ref, near_ref, near_link_ref,
+def means_payload(count, rhs_ref, link_ref, faces_ref, next_ref, outer_ref,
                   column_ref, mass_ref, base_mean_ref, mean_ref, op_ref, parts_ref):
     low, up = load_faces(count, faces_ref)
     next_low, next_up = load_faces(count, next_ref)
     last = count - 1
-    next_below = dot(near_ref[0], (near_link_ref[0] * low[0]).astype(BF16))
-    next_above = dot(near_ref[1], (near_link_ref[1] * up[last]).astype(BF16))
+    next_below, next_above = outer_ref[0], outer_ref[1]
     rows = []
     for i in range(count):
         v_low, v_up = face_vector(i, count, rhs_ref, link_ref, next_low, next_up, next_below, next_above)
@@ -558,7 +559,8 @@
                 else:
                     faces, first, second, *ahead = call(
                         functools.partial(middle_window, count, False),
-                        [faces_shape, message, message] + [faces_shape] * final,
+                        [faces_shape, message, message]
+                        + [faces_shape, sds((2, face, scenarios), F32)] * final,
                         common + (near, near_link),
                     )
             elif not ending:
@@ -575,7 +577,7 @@
     (parts,) = call(
         functools.partial(means_payload, count),
         [sds((slices * blocks, scenarios), F32)],
-        (rhs, link, faces, ahead[0], near, near_link, near_column, mass, base_mean, mean, op),
+        (rhs, link, faces, *ahead, near_column, mass, base_mean, mean, op),
     )
     parts = parts.reshape(slices * sub, count, scenarios)
     parts = lax.all_to_all(parts, ("cuts", "sub"), 0, 0, tiled=True)

time: 82.6 us -> 82.5 us (level)
  no operation moved by 1% of the time
where the time goes in v7:
time: 82.5 us; the launch traced here: 82.3 us
  waiting for transfers between devices  35.5 us (43%)
  starting transfers between devices  28.8 us (35%)
  Pallas kernels  17 us (21%)
    ppermute x8, waiting for transfers between devices, exchange(): near = lax.ppermute(first, ('cuts', 'sub'), pairs)  31.8 us
    ppermute x8, starting transfers between devices, exchange(): near = lax.ppermute(first, ('cuts', 'sub'), pairs)  22 us
    pallas_call x18, Pallas kernels, call(): pl.pallas_call(body, out_shape=out_shape, in_specs=[hbm if k in stay else...  17 us
    all_to_all x1, starting transfers between devices, on_device(): parts = lax.all_to_all(parts, ('cuts', 'sub'), 0, 0, tiled=True)  5.14 us
    all_to_all x1, waiting for transfers between devices, on_device(): parts = lax.all_to_all(parts, ('cuts', 'sub'), 0, 0, tiled=True)  3.71 us
  transfers between devices with their start and end apart: 20, of which 8 were waited for; matrix products, arithmetic and copies ran while one was open for 0% of the time, Pallas kernels for 13%

profile of v7, /device:TPU:0, one launch (start us, length us, event | category | flops | bytes accessed | tf_op | source)
XLA Modules:
  0.0 82.3 jit_solution(9310698355050749755)
XLA Ops:
  0.0 1.9 %shard_map.73 = (f32[2,256,128]{2,1,0:T(8,128)S(1)}, f32[4,128,128]{2,1,0:T(8,128)S(1)}, f32[2,256,128]{2,1,0:T(8,128)S(1)}, f32[392,128]{1,0:T(8,128)S(1)}, f32[392,128]{1,0:T(8,128)S(1)}) custom-call(f32[2,512,128]{2,1,0:T(8,128)} %bitcast.3, bf16[2,512,128]{2,1,0:T(8,128)(2,1)} %source_hbm.3, bf16[2,512,512]{2,1,0:T(8,128)(2,1)} %inverse_hbm.3, ...), custom_call_target="tpu_custom_call" | custom-call | flops 268435456 | bytes 3026944 | tf_op jit(solution)/shard_map/pallas_call | solution.py:34
  1.9 3.0 %collective-permute-start = (f32[392,128]{1,0:T(8,128)S(1)}, f32[392,128]{1,0:T(8,128)S(1)}, u32[]{:S(2)}, u32[]{:S(2)}) collective-permute-start(f32[392,128]{1,0:T(8,128)S(1)} %get-tuple-element.64), channel_id=1, source_target_pairs={{0,1},{1,0},{2,3},{3,2},{4,5},{5,4},{6,7},{7,6},{8,9},{9,8},{10,11... | collective-permute-start | bytes 602120 | tf_op jit(solution)/shard_map/ppermute | solution.py:467
  4.9 2.2 %shard_map.74 = (bf16[2,256,256]{2,1,0:T(8,128)(2,1)S(1)}, bf16[2,256,256]{2,1,0:T(8,128)(2,1)S(1)}, bf16[2,256,256]{2,1,0:T(8,128)(2,1)S(1)}, bf16[2,256,256]{2...) custom-call(f32[2,512,128]{2,1,0:T(8,128)} %bitcast.4, ...), custom_call_target="tpu_custom_call" | custom-call | flops 268435456 | bytes 4197376 | tf_op jit(solution)/shard_map/pallas_call | solution.py:34
  7.8 5.6 %collective-permute-done.refs_0_ = f32[392,128]{1,0:T(8,128)S(1)} collective-permute-done((f32[392,128]{1,0:T(8,128)S(1)}, f32[392,128]{1,0:T(8,128)S(1)}, u32[]{:S(2)}, u32[]{:S(2)}) %collective-permute-start) | collective-permute-done | bytes 200736 | tf_op jit(solution)/shard_map/ppermute | solution.py:467
  13.5 0.7 shard_map.77
  14.2 2.5 %collective-permute-start.2 = (f32[264,128]{1,0:T(8,128)S(1)}, f32[264,128]{1,0:T(8,128)S(1)}, u32[]{:S(2)}, u32[]{:S(2)}) collective-permute-start(f32[264,128]{1,0:T(8,128)S(1)} %get-tuple-element.77), channel_id=1, source_target_pairs={{0,1},{1,0},{2,3},{3,2},{4,5},{5,4},{6,7},{7,6},{8,9},{9,8},{10,11... | collective-permute-start | bytes 405512 | tf_op jit(solution)/shard_map/ppermute | solution.py:467
  16.7 4.9 %collective-permute-done.2.first_ref = f32[264,128]{1,0:T(8,128)S(1)} collective-permute-done((f32[264,128]{1,0:T(8,128)S(1)}, f32[264,128]{1,0:T(8,128)S(1)}, u32[]{:S(2)}, u32[]{:S(2)}) %collective-permute-start.2) | collective-permute-done | bytes 135200 | tf_op jit(solution)/shard_map/ppermute | solution.py:467
  21.6 0.8 shard_map.78
  22.4 2.5 %collective-permute-start.4 = (f32[256,128]{1,0:T(8,128)S(1)}, f32[256,128]{1,0:T(8,128)S(1)}, u32[]{:S(2)}, u32[]{:S(2)}) collective-permute-start(f32[256,128]{1,0:T(8,128)S(1)} %get-tuple-element.85), channel_id=1, source_target_pairs={{0,1},{1,0},{2,3},{3,2},{4,5},{5,4},{6,7},{7,6},{8,9},{9,8},{10,11... | collective-permute-start | bytes 393224 | tf_op jit(solution)/shard_map/ppermute | solution.py:467
  25.4 4.4 %collective-permute-done.4.refs_0_ = f32[256,128]{1,0:T(8,128)S(1)} collective-permute-done((f32[256,128]{1,0:T(8,128)S(1)}, f32[256,128]{1,0:T(8,128)S(1)}, u32[]{:S(2)}, u32[]{:S(2)}) %collective-permute-start.4) | collective-permute-done | bytes 131104 | tf_op jit(solution)/shard_map/ppermute | solution.py:467
  29.8 0.6 shard_map.80
  30.3 2.5 %collective-permute-start.6 = (f32[256,128]{1,0:T(8,128)S(1)}, f32[256,128]{1,0:T(8,128)S(1)}, u32[]{:S(2)}, u32[]{:S(2)}) collective-permute-start(f32[256,128]{1,0:T(8,128)S(1)} %get-tuple-element.91), channel_id=1, source_target_pairs={{0,1},{1,0},{2,3},{3,2},{4,5},{5,4},{6,7},{7,6},{8,9},{9,8},{10,11... | collective-permute-start | bytes 393224 | tf_op jit(solution)/shard_map/ppermute | solution.py:467
  32.9 4.8 %collective-permute-done.6.first_ref = f32[256,128]{1,0:T(8,128)S(1)} collective-permute-done((f32[256,128]{1,0:T(8,128)S(1)}, f32[256,128]{1,0:T(8,128)S(1)}, u32[]{:S(2)}, u32[]{:S(2)}) %collective-permute-start.6) | collective-permute-done | bytes 131104 | tf_op jit(solution)/shard_map/ppermute | solution.py:467
  37.7 0.8 shard_map.81
  38.5 2.5 %collective-permute-start.8 = (f32[256,128]{1,0:T(8,128)S(1)}, f32[256,128]{1,0:T(8,128)S(1)}, u32[]{:S(2)}, u32[]{:S(2)}) collective-permute-start(f32[256,128]{1,0:T(8,128)S(1)} %get-tuple-element.95), channel_id=1, source_target_pairs={{0,1},{1,0},{2,3},{3,2},{4,5},{5,4},{6,7},{7,6},{8,9},{9,8},{10,11... | collective-permute-start | bytes 393224 | tf_op jit(solution)/shard_map/ppermute | solution.py:467
  41.4 4.4 %collective-permute-done.8.refs_0_ = f32[256,128]{1,0:T(8,128)S(1)} collective-permute-done((f32[256,128]{1,0:T(8,128)S(1)}, f32[256,128]{1,0:T(8,128)S(1)}, u32[]{:S(2)}, u32[]{:S(2)}) %collective-permute-start.8) | collective-permute-done | bytes 131104 | tf_op jit(solution)/shard_map/ppermute | solution.py:467
  45.8 0.6 shard_map.83
  46.4 2.5 %collective-permute-start.10 = (f32[256,128]{1,0:T(8,128)S(1)}, f32[256,128]{1,0:T(8,128)S(1)}, u32[]{:S(2)}, u32[]{:S(2)}) collective-permute-start(f32[256,128]{1,0:T(8,128)S(1)} %get-tuple-element.101), channel_id=1, source_target_pairs={{0,1},{1,0},{2,3},{3,2},{4,5},{5,4},{6,7},{7,6},{8,9},{9,8},{10,11... | collective-permute-start | bytes 393224 | tf_op jit(solution)/shard_map/ppermute | solution.py:467
  48.9 4.8 %collective-permute-done.10.first_ref = f32[256,128]{1,0:T(8,128)S(1)} collective-permute-done((f32[256,128]{1,0:T(8,128)S(1)}, f32[256,128]{1,0:T(8,128)S(1)}, u32[]{:S(2)}, u32[]{:S(2)}) %collective-permute-start.10) | collective-permute-done | bytes 131104 | tf_op jit(solution)/shard_map/ppermute | solution.py:467
  53.7 0.8 shard_map.84
  54.5 2.5 %collective-permute-start.12 = (f32[256,128]{1,0:T(8,128)S(1)}, f32[256,128]{1,0:T(8,128)S(1)}, u32[]{:S(2)}, u32[]{:S(2)}) collective-permute-start(f32[256,128]{1,0:T(8,128)S(1)} %get-tuple-element.106), channel_id=1, source_target_pairs={{0,1},{1,0},{2,3},{3,2},{4,5},{5,4},{6,7},{7,6},{8,9},{9,8},{10,11... | collective-permute-start | bytes 393224 | tf_op jit(solution)/shard_map/ppermute | solution.py:467
  57.0 0.5 collective-permute-start.16
  57.5 1.1 %collective-permute-start.18 = (f32[2,256,128]{2,1,0:T(8,128)S(1)}, f32[2,256,128]{2,1,0:T(8,128)S(1)}, u32[]{:S(2)}, u32[]{:S(2)}) collective-permute-start(f32[2,256,128]{2,1,0:T(8,128)S(1)} %get-tuple-element.108.mid_ref), channel_id=1, source_target_pairs={{0,8},{8,16},{16,24},{24,0},{1,9},{9,17},{17,25},{25,1},{2,10},{10... | collective-permute-start | bytes 786440 | tf_op jit(solution)/shard_map/ppermute | solution.py:539
  58.9 2.9 %collective-permute-done.12.refs_0_ = f32[256,128]{1,0:T(8,128)S(1)} collective-permute-done((f32[256,128]{1,0:T(8,128)S(1)}, f32[256,128]{1,0:T(8,128)S(1)}, u32[]{:S(2)}, u32[]{:S(2)}) %collective-permute-start.12) | collective-permute-done | bytes 131104 | tf_op jit(solution)/shard_map/ppermute | solution.py:467
  61.8 0.6 shard_map.86
  62.5 3.7 %collective-permute-start.14 = (f32[256,128]{1,0:T(8,128)S(1)}, f32[256,128]{1,0:T(8,128)S(1)}, u32[]{:S(2)}, u32[]{:S(2)}) collective-permute-start(f32[256,128]{1,0:T(8,128)S(1)} %get-tuple-element.119), channel_id=1, source_target_pairs={{0,9},{1,8},{2,11},{3,10},{4,13},{5,12},{6,15},{7,14},{8,17},{9,16... | collective-permute-start | bytes 393224 | tf_op jit(solution)/shard_map/ppermute | solution.py:467
  66.1 3.0 %shard_map.87.op_ref = f32[8,64,128]{2,1,0:T(8,128)S(1)} custom-call(s32[16]{0:T(128)} %partner_hbm.1, f32[16]{0:T(128)} %cond_hbm.1), custom_call_target="tpu_custom_call" | custom-call | flops 268435456 | bytes 262272 | tf_op jit(solution)/shard_map/pallas_call | solution.py:34
  69.2 0.7 shard_map.88
  69.9 5.1 %all-to-all-start = ((f32[32,2,128]{2,1,0:T(2,128)}), f32[32,2,128]{2,1,0:T(2,128)S(1)}, u32[]{:S(2)}, u32[]{:S(2)}) async-start(f32[32,2,128]{2,1,0:T(2,128)} %bitcast.1), calls=%async_computation | async-start | bytes 65536 | tf_op jit(solution)/shard_map/all_to_all | solution.py:583
  75.1 0.7 copy-done
  75.9 2.6 %shard_map.89 = (f32[2,512,128]{2,1,0:T(8,128)S(1)}, f32[2,512,128]{2,1,0:T(8,128)}) custom-call(f32[256,128]{1,0:T(8,128)S(1)} %collective-permute-done.14.first_ref, f32[256,128]{1,0:T(8,128)S(1)} %collective-permute-done.15.second_ref, bf16[2,256,256]{2,1,0:T(8,128)(2,1)S(1)} %get-tuple-element.66.ff_ref.refs_2_, f32[2,256,128]{2,1,0:T(8,128)} %copy-done, ...), custom_call_target="tpu_custom_call" | custom-call | flops 268435456 | bytes 4128768 | tf_op jit(solution)/shard_map/pallas_call | solution.py:34
  78.5 3.7 %all-to-all-done.parts_ref = f32[32,2,128]{2,1,0:T(2,128)S(1)} async-done(((f32[32,2,128]{2,1,0:T(2,128)}), f32[32,2,128]{2,1,0:T(2,128)S(1)}, u32[]{:S(2)}, u32[]{:S(2)}) %all-to-all-start) | async-done | bytes 32800 | tf_op jit(solution)/shard_map/all_to_all | solution.py:583
  (30 shorter events, 1.9 us)
Async XLA Ops:
  1.9 11.6 %collective-permute-start = (f32[392,128]{1,0:T(8,128)S(1)}, f32[392,128]{1,0:T(8,128)S(1)}, u32[]{:S(2)}, u32[]{:S(2)}) collective-permute-start(f32[392,128]{1,0:T(8,128)S(1)} %get-tuple-element.64), channel_id=1, source_target_pairs={{0,1},{1,0},{2,3},{3,2},{4,5},{5,4},{6,7},{7,6},{8,9},{9,8},{10,11... | collective-permute-start | bytes 602120 | tf_op jit(solution)/shard_map/ppermute | solution.py:467
  4.9 8.6 %collective-permute-start.1 = (f32[392,128]{1,0:T(8,128)S(1)}, f32[392,128]{1,0:T(8,128)S(1)}, u32[]{:S(2)}, u32[]{:S(2)}) collective-permute-start(f32[392,128]{1,0:T(8,128)S(1)} %get-tuple-element.65), channel_id=1, source_target_pairs={{0,8},{1,2},{2,1},{3,4},{4,3},{5,6},{6,5},{7,15},{8,0},{9,10},{10,... | collective-permute-start | bytes 602120 | tf_op jit(solution)/shard_map/ppermute | solution.py:466
  14.2 7.5 %collective-permute-start.2 = (f32[264,128]{1,0:T(8,128)S(1)}, f32[264,128]{1,0:T(8,128)S(1)}, u32[]{:S(2)}, u32[]{:S(2)}) collective-permute-start(f32[264,128]{1,0:T(8,128)S(1)} %get-tuple-element.77), channel_id=1, source_target_pairs={{0,1},{1,0},{2,3},{3,2},{4,5},{5,4},{6,7},{7,6},{8,9},{9,8},{10,11... | collective-permute-start | bytes 405512 | tf_op jit(solution)/shard_map/ppermute | solution.py:467
  16.7 4.9 %collective-permute-start.3 = (f32[264,128]{1,0:T(8,128)S(1)}, f32[264,128]{1,0:T(8,128)S(1)}, u32[]{:S(2)}, u32[]{:S(2)}) collective-permute-start(f32[264,128]{1,0:T(8,128)S(1)} %get-tuple-element.78), channel_id=1, source_target_pairs={{0,8},{1,2},{2,1},{3,4},{4,3},{5,6},{6,5},{7,15},{8,0},{9,10},{10,... | collective-permute-start | bytes 405512 | tf_op jit(solution)/shard_map/ppermute | solution.py:466
  22.4 7.3 %collective-permute-start.4 = (f32[256,128]{1,0:T(8,128)S(1)}, f32[256,128]{1,0:T(8,128)S(1)}, u32[]{:S(2)}, u32[]{:S(2)}) collective-permute-start(f32[256,128]{1,0:T(8,128)S(1)} %get-tuple-element.85), channel_id=1, source_target_pairs={{0,1},{1,0},{2,3},{3,2},{4,5},{5,4},{6,7},{7,6},{8,9},{9,8},{10,11... | collective-permute-start | bytes 393224 | tf_op jit(solution)/shard_map/ppermute | solution.py:467
  25.0 4.8 %collective-permute-start.5 = (f32[256,128]{1,0:T(8,128)S(1)}, f32[256,128]{1,0:T(8,128)S(1)}, u32[]{:S(2)}, u32[]{:S(2)}) collective-permute-start(f32[256,128]{1,0:T(8,128)S(1)} %get-tuple-element.86), channel_id=1, source_target_pairs={{0,8},{1,2},{2,1},{3,4},{4,3},{5,6},{6,5},{7,15},{8,0},{9,10},{10,... | collective-permute-start | bytes 393224 | tf_op jit(solution)/shard_map/ppermute | solution.py:466
  30.3 7.3 %collective-permute-start.6 = (f32[256,128]{1,0:T(8,128)S(1)}, f32[256,128]{1,0:T(8,128)S(1)}, u32[]{:S(2)}, u32[]{:S(2)}) collective-permute-start(f32[256,128]{1,0:T(8,128)S(1)} %get-tuple-element.91), channel_id=1, source_target_pairs={{0,1},{1,0},{2,3},{3,2},{4,5},{5,4},{6,7},{7,6},{8,9},{9,8},{10,11... | collective-permute-start | bytes 393224 | tf_op jit(solution)/shard_map/ppermute | solution.py:467
  32.9 4.8 %collective-permute-start.7 = (f32[256,128]{1,0:T(8,128)S(1)}, f32[256,128]{1,0:T(8,128)S(1)}, u32[]{:S(2)}, u32[]{:S(2)}) collective-permute-start(f32[256,128]{1,0:T(8,128)S(1)} %get-tuple-element.92), channel_id=1, source_target_pairs={{0,8},{1,2},{2,1},{3,4},{4,3},{5,6},{6,5},{7,15},{8,0},{9,10},{10,... | collective-permute-start | bytes 393224 | tf_op jit(solution)/shard_map/ppermute | solution.py:466
  38.5 7.3 %collective-permute-start.8 = (f32[256,128]{1,0:T(8,128)S(1)}, f32[256,128]{1,0:T(8,128)S(1)}, u32[]{:S(2)}, u32[]{:S(2)}) collective-permute-start(f32[256,128]{1,0:T(8,128)S(1)} %get-tuple-element.95), channel_id=1, source_target_pairs={{0,1},{1,0},{2,3},{3,2},{4,5},{5,4},{6,7},{7,6},{8,9},{9,8},{10,11... | collective-permute-start | bytes 393224 | tf_op jit(solution)/shard_map/ppermute | solution.py:467
  41.0 4.8 %collective-permute-start.9 = (f32[256,128]{1,0:T(8,128)S(1)}, f32[256,128]{1,0:T(8,128)S(1)}, u32[]{:S(2)}, u32[]{:S(2)}) collective-permute-start(f32[256,128]{1,0:T(8,128)S(1)} %get-tuple-element.96), channel_id=1, source_target_pairs={{0,8},{1,2},{2,1},{3,4},{4,3},{5,6},{6,5},{7,15},{8,0},{9,10},{10,... | collective-permute-start | bytes 393224 | tf_op jit(solution)/shard_map/ppermute | solution.py:466
  46.4 7.3 %collective-permute-start.10 = (f32[256,128]{1,0:T(8,128)S(1)}, f32[256,128]{1,0:T(8,128)S(1)}, u32[]{:S(2)}, u32[]{:S(2)}) collective-permute-start(f32[256,128]{1,0:T(8,128)S(1)} %get-tuple-element.101), channel_id=1, source_target_pairs={{0,1},{1,0},{2,3},{3,2},{4,5},{5,4},{6,7},{7,6},{8,9},{9,8},{10,11... | collective-permute-start | bytes 393224 | tf_op jit(solution)/shard_map/ppermute | solution.py:467
  48.9 4.8 %collective-permute-start.11 = (f32[256,128]{1,0:T(8,128)S(1)}, f32[256,128]{1,0:T(8,128)S(1)}, u32[]{:S(2)}, u32[]{:S(2)}) collective-permute-start(f32[256,128]{1,0:T(8,128)S(1)} %get-tuple-element.102), channel_id=1, source_target_pairs={{0,8},{1,2},{2,1},{3,4},{4,3},{5,6},{6,5},{7,15},{8,0},{9,10},{10,... | collective-permute-start | bytes 393224 | tf_op jit(solution)/shard_map/ppermute | solution.py:466
  54.5 7.3 %collective-permute-start.12 = (f32[256,128]{1,0:T(8,128)S(1)}, f32[256,128]{1,0:T(8,128)S(1)}, u32[]{:S(2)}, u32[]{:S(2)}) collective-permute-start(f32[256,128]{1,0:T(8,128)S(1)} %get-tuple-element.106), channel_id=1, source_target_pairs={{0,1},{1,0},{2,3},{3,2},{4,5},{5,4},{6,7},{7,6},{8,9},{9,8},{10,11... | collective-permute-start | bytes 393224 | tf_op jit(solution)/shard_map/ppermute | solution.py:467
  57.0 4.8 %collective-permute-start.13 = (f32[256,128]{1,0:T(8,128)S(1)}, f32[256,128]{1,0:T(8,128)S(1)}, u32[]{:S(2)}, u32[]{:S(2)}) collective-permute-start(f32[256,128]{1,0:T(8,128)S(1)} %get-tuple-element.107), channel_id=1, source_target_pairs={{0,8},{1,2},{2,1},{3,4},{4,3},{5,6},{6,5},{7,15},{8,0},{9,10},{10,... | collective-permute-start | bytes 393224 | tf_op jit(solution)/shard_map/ppermute | solution.py:466
  57.0 18.1 %collective-permute-start.16 = (f32[2,256,128]{2,1,0:T(8,128)S(1)}, f32[2,256,128]{2,1,0:T(8,128)S(1)}, u32[]{:S(2)}, u32[]{:S(2)}) collective-permute-start(f32[2,256,128]{2,1,0:T(8,128)S(1)} %get-tuple-element.105.refs_4_.rhs_ref), channel_id=1, source_target_pairs={{0,8},{8,16},{16,24},{24,0},{1,9},{9,17},{17,25},{25,1},{2,10},{10... | collective-permute-start | bytes 786440 | tf_op jit(solution)/shard_map/ppermute | solution.py:540
  57.5 17.6 %collective-permute-start.18 = (f32[2,256,128]{2,1,0:T(8,128)S(1)}, f32[2,256,128]{2,1,0:T(8,128)S(1)}, u32[]{:S(2)}, u32[]{:S(2)}) collective-permute-start(f32[2,256,128]{2,1,0:T(8,128)S(1)} %get-tuple-element.108.mid_ref), channel_id=1, source_target_pairs={{0,8},{8,16},{16,24},{24,0},{1,9},{9,17},{17,25},{25,1},{2,10},{10... | collective-permute-start | bytes 786440 | tf_op jit(solution)/shard_map/ppermute | solution.py:539
  62.4 12.7 %collective-permute-start.17 = (f32[2,256,128]{2,1,0:T(8,128)S(1)}, f32[2,256,128]{2,1,0:T(8,128)}, u32[]{:S(2)}, u32[]{:S(2)}) collective-permute-start(f32[2,256,128]{2,1,0:T(8,128)S(1)} %get-tuple-element.112.faces_ref), channel_id=1, source_target_pairs={{0,8},{8,16},{16,24},{24,0},{1,9},{9,17},{17,25},{25,1},{2,10},{10... | collective-permute-start | bytes 786440 | tf_op jit(solution)/shard_map/ppermute | solution.py:576
  62.5 12.6 %collective-permute-start.14 = (f32[256,128]{1,0:T(8,128)S(1)}, f32[256,128]{1,0:T(8,128)S(1)}, u32[]{:S(2)}, u32[]{:S(2)}) collective-permute-start(f32[256,128]{1,0:T(8,128)S(1)} %get-tuple-element.119), channel_id=1, source_target_pairs={{0,9},{1,8},{2,11},{3,10},{4,13},{5,12},{6,15},{7,14},{8,17},{9,16... | collective-permute-start | bytes 393224 | tf_op jit(solution)/shard_map/ppermute | solution.py:467
  66.1 8.9 %collective-permute-start.15 = (f32[256,128]{1,0:T(8,128)S(1)}, f32[256,128]{1,0:T(8,128)S(1)}, u32[]{:S(2)}, u32[]{:S(2)}) collective-permute-start(f32[256,128]{1,0:T(8,128)S(1)} %get-tuple-element.120), channel_id=1, source_target_pairs={{0,8},{1,10},{2,9},{3,12},{4,11},{5,14},{6,13},{7,15},{8,16},{9,18... | collective-permute-start | bytes 393224 | tf_op jit(solution)/shard_map/ppermute | solution.py:466
  69.9 12.3 %all-to-all-start = ((f32[32,2,128]{2,1,0:T(2,128)}), f32[32,2,128]{2,1,0:T(2,128)S(1)}, u32[]{:S(2)}, u32[]{:S(2)}) async-start(f32[32,2,128]{2,1,0:T(2,128)} %bitcast.1), calls=%async_computation | async-start | bytes 65536 | tf_op jit(solution)/shard_map/all_to_all | solution.py:583
  75.1 0.7 copy-start
  75.1 0.8 copy-start.1
